TPU v7x, 128 devices: a whole 4x4x4 slice. The times are simulated.
128 devices in a mesh: replica: 8 (over x, y_hi), fsdp: 16 (over y_lo, z, core).
Axes of the slice: x: 4, y: 4 (y_hi: 2, y_lo: 2; y = y_hi * 2 + y_lo), z: 4, core: 2. Of those that a mesh axis runs over, the one named last changes fastest.
Arguments:
- tokens: bfloat16 [147456, 1024], P(('replica', 'fsdp')), may hold values from -6 to 6
- cotangent: bfloat16 [147456, 1024], P(('replica', 'fsdp')), may hold values from -6 to 6
- lengths: int32 [128, 3], P(('replica', 'fsdp')), may hold values from 1 to 1024, 1152 in all within a row
- deal_order: int32 [147456], P(('replica', 'fsdp')), may hold values from 0 to 147455, as said below
- inverse: int32 [147456], P(('replica', 'fsdp')), may hold values from 0 to 147455, as said below
- ln1_gain: bfloat16 [1024], P('fsdp'), may hold values from 0.5 to 1.5
- ln1_bias: bfloat16 [1024], P('fsdp'), may hold values from -1 to 1
- w_qkv: bfloat16 [1024, 3072], P('fsdp'), may hold values from -0.1875 to 0.1875
- b_query: bfloat16 [1024], P('fsdp'), may hold values from -1 to 1
- b_value: bfloat16 [1024], P('fsdp'), may hold values from -1 to 1
- head_scale: bfloat16 [16], P('fsdp'), may hold values from 0.5 to 1.5
- w_out: bfloat16 [1024, 1024], P('fsdp'), may hold values from -0.1875 to 0.1875
- b_out: bfloat16 [1024], P('fsdp'), may hold values from -1 to 1
- post_gain: bfloat16 [1024], P('fsdp'), may hold values from 0.5 to 1.5
- post_bias: bfloat16 [1024], P('fsdp'), may hold values from -1 to 1
- ln2_gain: bfloat16 [1024], P('fsdp'), may hold values from 0.5 to 1.5
- ln2_bias: bfloat16 [1024], P('fsdp'), may hold values from -1 to 1
- w_fc1: bfloat16 [1024, 4096], P('fsdp'), may hold values from -0.1875 to 0.1875
- b_fc1: bfloat16 [4096], P('fsdp'), may hold values from -1 to 1
- ffn_gain: bfloat16 [4096], P('fsdp'), may hold values from 0.5 to 1.5
- ffn_bias: bfloat16 [4096], P('fsdp'), may hold values from -1 to 1
- w_fc2: bfloat16 [4096, 1024], P('fsdp'), may hold values from -0.09375 to 0.09375
- b_fc2: bfloat16 [1024], P('fsdp'), may hold values from -1 to 1
Outputs:
- output: bfloat16 [147456, 1024], P(('replica', 'fsdp'))
- grad_tokens: bfloat16 [147456, 1024], P(('replica', 'fsdp'))
- grad_ln1_gain: float32 [1024], P('fsdp')
- grad_ln1_bias: float32 [1024], P('fsdp')
- grad_w_qkv: float32 [1024, 3072], P('fsdp')
- grad_b_query: float32 [1024], P('fsdp')
- grad_b_value: float32 [1024], P('fsdp')
- grad_head_scale: float32 [16], P('fsdp')
- grad_w_out: float32 [1024, 1024], P('fsdp')
- grad_b_out: float32 [1024], P('fsdp')
- grad_post_gain: float32 [1024], P('fsdp')
- grad_post_bias: float32 [1024], P('fsdp')
- grad_ln2_gain: float32 [1024], P('fsdp')
- grad_ln2_bias: float32 [1024], P('fsdp')
- grad_w_fc1: float32 [1024, 4096], P('fsdp')
- grad_b_fc1: float32 [4096], P('fsdp')
- grad_ffn_gain: float32 [4096], P('fsdp')
- grad_ffn_bias: float32 [4096], P('fsdp')
- grad_w_fc2: float32 [4096, 1024], P('fsdp')
- grad_b_fc2: float32 [1024], P('fsdp')
Inputs may be any that keep to these rules, and one draw needn't show every extreme that they name: deal_order is a permutation of all rows; of the 1152 rows that one device holds in the device order exactly 9 come from each device's rows of the given order. inverse[deal_order[i]] = i for every i. `lengths`: each row sums to 1152; each row's longest sequence has 1024 rows.
All inputs are finite; a program needn't handle non-finite values.
Results may differ from a plain program's by a relative error of at most 0.03.
Values may be sent and summed in bfloat16 or wider, within the bound.
No kernel may reach another device: no remote copies, remote signals or barrier semaphores. Data moves between devices by JAX's collectives and lax.ppermute only.
A program may use at most 320 MiB of HBM per device.

v0:
```python
import jax
import jax.numpy as jnp
from jax import lax
from jax.sharding import PartitionSpec as P

H = 16
HD = 64
QB = 576


EPS = 1e-05
NEG = -1000000000.0


def side_by_side(arrays, axis, dim, along):
    columns = [a.reshape(*a.shape[:along], -1) for a in arrays]
    both = jnp.concatenate(columns, axis=along)
    whole, at, gathered = (lax.psum_scatter(both, axis, scatter_dimension=dim, tiled=True), 0, [])
    for a, column in zip(arrays, columns):
        share = whole[..., at : at + column.shape[along]]
        gathered.append(share.reshape(*share.shape[:along], *a.shape[along:]))
        at += column.shape[along]
    return tuple(gathered)


def layer_norm(values, gain_vec, bias_vec):
    mean_row = jnp.mean(values, axis=-1, keepdims=True)
    centred = values - mean_row
    spread = jnp.mean(centred * centred, axis=-1, keepdims=True)
    return centred * lax.rsqrt(spread + EPS) * gain_vec + bias_vec


def gelu_norm(values, gain_vec, bias_vec):
    return layer_norm(jax.nn.gelu(values, approximate=False), gain_vec, bias_vec)


def segment_ids(lengths_row, count):
    seq_ends = jnp.cumsum(lengths_row)
    places = jnp.arange(count, dtype=jnp.int32)
    return jnp.sum((places[:, None] >= seq_ends[None, :]).astype(jnp.int32), axis=1)


def block_parts(proj_b, segments, turn_index):
    count = proj_b.shape[0]
    width = H * HD
    group_cols = 4 * HD
    groups = H // 4
    window = min(count, 3 * QB)
    q_start = turn_index // groups * QB
    k_start = jnp.clip(q_start + QB - window, 0, count - window)
    col_start = turn_index % groups * group_cols
    query_rows = lax.dynamic_slice(proj_b, (q_start, col_start), (QB, group_cols)).reshape(
        QB, 4, HD
    )
    key_rows = lax.dynamic_slice(
        proj_b, (k_start, width + col_start), (window, group_cols)
    ).reshape(window, 4, HD)
    value_rows = lax.dynamic_slice(
        proj_b, (k_start, 2 * width + col_start), (window, group_cols)
    ).reshape(window, 4, HD)
    q_seg = lax.dynamic_slice(segments, (q_start,), (QB,))
    q_pos = q_start + jnp.arange(QB, dtype=jnp.int32)
    k_pos = k_start + jnp.arange(window, dtype=jnp.int32)
    allowed = (q_seg[:, None] == segments[None, :]) & (k_pos[None, :] <= q_pos[:, None])
    raw_scores = jnp.einsum(
        "qhd,khd->hqk", query_rows, key_rows, preferred_element_type=jnp.float32
    ) * HD ** (-0.5)
    scores = jnp.where(allowed[None], raw_scores, NEG)
    return (query_rows, key_rows, value_rows, scores, q_start, k_start, col_start)


def attend_forward(proj_b, segments):
    count = proj_b.shape[0]
    turns = count // QB * (H // 4)

    def attend_turn(turn_index, carry):
        attn_acc, lse_acc = carry
        query_rows, key_rows, value_rows, scores, q_start, k_start, col_start = block_parts(
            proj_b, segments, turn_index
        )
        row_max = jnp.max(scores, axis=-1, keepdims=True)
        exponent = jnp.exp(scores - row_max)
        row_total = jnp.sum(exponent, axis=-1, keepdims=True)
        prob_rows = exponent / row_total
        mixed_rows = jnp.einsum(
            "hqk,khd->qhd",
            prob_rows.astype(jnp.bfloat16),
            value_rows,
            preferred_element_type=jnp.float32,
        )
        attn_acc = lax.dynamic_update_slice(
            attn_acc, mixed_rows.reshape(QB, 4 * HD), (q_start, col_start)
        )
        lse_rows = (row_max + jnp.log(row_total))[..., 0]
        head_start = turn_index % (H // 4) * 4
        lse_acc = lax.dynamic_update_slice(lse_acc, lse_rows, (head_start, q_start))
        return (attn_acc, lse_acc)

    initial = (jnp.zeros((count, H * HD), jnp.float32), jnp.zeros((H, count), jnp.float32))
    return lax.fori_loop(0, turns, attend_turn, initial)


def attend_backward(proj_b, segments, lse_all, d_attn_b):
    count = proj_b.shape[0]
    width = H * HD
    window = min(count, 3 * QB)
    turns = count // QB * (H // 4)
    scale_val = HD ** (-0.5)

    def back_turn(turn_index, grad_acc):
        query_rows, key_rows, value_rows, scores, q_start, k_start, col_start = block_parts(
            proj_b, segments, turn_index
        )
        head_start = turn_index % (H // 4) * 4
        lse_rows = lax.dynamic_slice(lse_all, (head_start, q_start), (4, QB))
        prob_rows = jnp.exp(scores - lse_rows[..., None])
        d_out = lax.dynamic_slice(d_attn_b, (q_start, col_start), (QB, 4 * HD)).reshape(QB, 4, HD)
        d_prob = jnp.einsum("qhd,khd->hqk", d_out, value_rows, preferred_element_type=jnp.float32)
        centre = jnp.sum(prob_rows * d_prob, axis=-1, keepdims=True)
        d_score = (prob_rows * (d_prob - centre)).astype(jnp.bfloat16)
        d_query = (
            jnp.einsum("hqk,khd->qhd", d_score, key_rows, preferred_element_type=jnp.float32)
            * scale_val
        )
        d_key = (
            jnp.einsum("hqk,qhd->khd", d_score, query_rows, preferred_element_type=jnp.float32)
            * scale_val
        )
        d_value = jnp.einsum(
            "hqk,qhd->khd",
            prob_rows.astype(jnp.bfloat16),
            d_out,
            preferred_element_type=jnp.float32,
        )
        grad_acc = lax.dynamic_update_slice(
            grad_acc, d_query.reshape(QB, 4 * HD), (q_start, col_start)
        )
        old_key = lax.dynamic_slice(grad_acc, (k_start, width + col_start), (window, 4 * HD))
        grad_acc = lax.dynamic_update_slice(
            grad_acc, old_key + d_key.reshape(window, 4 * HD), (k_start, width + col_start)
        )
        old_value = lax.dynamic_slice(grad_acc, (k_start, 2 * width + col_start), (window, 4 * HD))
        grad_acc = lax.dynamic_update_slice(
            grad_acc, old_value + d_value.reshape(window, 4 * HD), (k_start, 2 * width + col_start)
        )
        return grad_acc

    return lax.fori_loop(0, turns, back_turn, jnp.zeros((count, 3 * width), jnp.float32))


def on_device(
    tokens,
    cotangent,
    lengths,
    deal_order,
    inverse,
    ln1_gain,
    ln1_bias,
    w_qkv,
    b_query,
    b_value,
    head_scale,
    w_out,
    b_out,
    post_gain,
    post_bias,
    ln2_gain,
    ln2_bias,
    w_fc1,
    b_fc1,
    ffn_gain,
    ffn_bias,
    w_fc2,
    b_fc2,
):
    devices = lax.axis_size(("replica", "fsdp"))
    count = tokens.shape[0]
    width = tokens.shape[1]
    per_pair = count // devices
    send_order = jnp.argsort(inverse)
    src_device = deal_order // count
    recv_order = jnp.argsort(src_device * count + jnp.arange(count, dtype=jnp.int32))
    placing = jnp.argsort(recv_order)
    got_x, got_dy = (
        lax.all_to_all(
            jnp.take(tokens, send_order, axis=0).reshape(devices, per_pair, width),
            ("replica", "fsdp"),
            split_axis=0,
            concat_axis=0,
            tiled=True,
        ),
        lax.all_to_all(
            jnp.take(cotangent, send_order, axis=0).reshape(devices, per_pair, width),
            ("replica", "fsdp"),
            split_axis=0,
            concat_axis=0,
            tiled=True,
        ),
    )
    x_rows = jnp.take(got_x.reshape(count, width), placing, axis=0)
    dy_rows = jnp.take(got_dy.reshape(count, width), placing, axis=0)
    segments = segment_ids(lengths[0], count)
    g_one, b_one, qkv_full, bq_full, bv_full, hs_full, out_full, bo_full, pg_full, pb_full = (
        lax.all_gather(ln1_gain, "fsdp", axis=0, tiled=True),
        lax.all_gather(ln1_bias, "fsdp", axis=0, tiled=True),
        lax.all_gather(w_qkv, "fsdp", axis=0, tiled=True),
        lax.all_gather(b_query, "fsdp", axis=0, tiled=True),
        lax.all_gather(b_value, "fsdp", axis=0, tiled=True),
        lax.all_gather(head_scale, "fsdp", axis=0, tiled=True),
        lax.all_gather(w_out, "fsdp", axis=0, tiled=True),
        lax.all_gather(b_out, "fsdp", axis=0, tiled=True),
        lax.all_gather(post_gain, "fsdp", axis=0, tiled=True),
        lax.all_gather(post_bias, "fsdp", axis=0, tiled=True),
    )
    x_vals = x_rows.astype(jnp.float32)
    normed, ln1_pull = jax.vjp(
        layer_norm, x_vals, g_one.astype(jnp.float32), b_one.astype(jnp.float32)
    )
    normed_b = normed.astype(jnp.bfloat16)
    bias_full = jnp.concatenate(
        [bq_full.astype(jnp.float32), jnp.zeros((width,), jnp.float32), bv_full.astype(jnp.float32)]
    )
    proj_b = (jnp.dot(normed_b, qkv_full, preferred_element_type=jnp.float32) + bias_full).astype(
        jnp.bfloat16
    )
    attn, lse_all = attend_forward(proj_b, segments)
    mixed_b = (attn * jnp.repeat(hs_full.astype(jnp.float32), HD)).astype(jnp.bfloat16)
    z_vals = jnp.dot(mixed_b, out_full, preferred_element_type=jnp.float32) + bo_full.astype(
        jnp.float32
    )
    post_vals, post_pull = jax.vjp(
        layer_norm, z_vals, pg_full.astype(jnp.float32), pb_full.astype(jnp.float32)
    )
    resid = x_vals + post_vals
    g_two, b_two, fc1_full, bf1_full, fg_full, fb_full, fc2_full, bf2_full = (
        lax.all_gather(ln2_gain, "fsdp", axis=0, tiled=True),
        lax.all_gather(ln2_bias, "fsdp", axis=0, tiled=True),
        lax.all_gather(w_fc1, "fsdp", axis=0, tiled=True),
        lax.all_gather(b_fc1, "fsdp", axis=0, tiled=True),
        lax.all_gather(ffn_gain, "fsdp", axis=0, tiled=True),
        lax.all_gather(ffn_bias, "fsdp", axis=0, tiled=True),
        lax.all_gather(w_fc2, "fsdp", axis=0, tiled=True),
        lax.all_gather(b_fc2, "fsdp", axis=0, tiled=True),
    )
    normed_two, ln2_pull = jax.vjp(
        layer_norm, resid, g_two.astype(jnp.float32), b_two.astype(jnp.float32)
    )
    normed_two_b = normed_two.astype(jnp.bfloat16)
    up_vals = jnp.dot(normed_two_b, fc1_full, preferred_element_type=jnp.float32) + bf1_full.astype(
        jnp.float32
    )
    inner, inner_pull = jax.vjp(
        gelu_norm, up_vals, fg_full.astype(jnp.float32), fb_full.astype(jnp.float32)
    )
    inner_b = inner.astype(jnp.bfloat16)
    out_rows = (
        resid
        + jnp.dot(inner_b, fc2_full, preferred_element_type=jnp.float32)
        + bf2_full.astype(jnp.float32)
    ).astype(jnp.bfloat16)
    fc1_back, fc2_back = (
        lax.all_gather(w_fc1, "fsdp", axis=0, tiled=True),
        lax.all_gather(w_fc2, "fsdp", axis=0, tiled=True),
    )
    dy_vals = dy_rows.astype(jnp.float32)
    grad_fc2 = jnp.einsum("tf,td->fd", inner_b, dy_rows, preferred_element_type=jnp.float32)
    grad_bf2 = jnp.sum(dy_vals, axis=0)
    d_inner = jnp.einsum("td,fd->tf", dy_rows, fc2_back, preferred_element_type=jnp.float32)
    d_up, grad_fg, grad_fb = inner_pull(d_inner)
    d_up_b = d_up.astype(jnp.bfloat16)
    grad_fc1 = jnp.einsum("td,tf->df", normed_two_b, d_up_b, preferred_element_type=jnp.float32)
    grad_bf1 = jnp.sum(d_up_b.astype(jnp.float32), axis=0)
    d_normed_two = jnp.einsum("tf,df->td", d_up_b, fc1_back, preferred_element_type=jnp.float32)
    d_resid_two, grad_g_two, grad_b_two = ln2_pull(d_normed_two)
    d_resid = dy_vals + d_resid_two
    ffn_grads = (
        lax.psum_scatter(
            grad_g_two.astype(jnp.bfloat16), "fsdp", scatter_dimension=0, tiled=True
        ).astype(jnp.float32),
        *tuple(
            (
                part.astype(jnp.float32)
                for part in side_by_side(
                    (grad_b_two.astype(jnp.bfloat16), grad_fc1.astype(jnp.bfloat16)), "fsdp", 0, 1
                )
            )
        ),
        lax.psum_scatter(
            grad_bf1.astype(jnp.bfloat16), "fsdp", scatter_dimension=0, tiled=True
        ).astype(jnp.float32),
        lax.psum_scatter(
            grad_fg.astype(jnp.bfloat16), "fsdp", scatter_dimension=0, tiled=True
        ).astype(jnp.float32),
        *tuple(
            (
                part.astype(jnp.float32)
                for part in side_by_side(
                    (grad_fb.astype(jnp.bfloat16), grad_fc2.astype(jnp.bfloat16)), "fsdp", 0, 1
                )
            )
        ),
        lax.psum_scatter(
            grad_bf2.astype(jnp.bfloat16), "fsdp", scatter_dimension=0, tiled=True
        ).astype(jnp.float32),
    )
    ffn_grads = (
        lax.psum(ffn_grads[0].astype(jnp.bfloat16), "replica").astype(jnp.float32),
        lax.psum(ffn_grads[1].astype(jnp.bfloat16), "replica").astype(jnp.float32),
        lax.psum(ffn_grads[2].astype(jnp.bfloat16), "replica").astype(jnp.float32),
        lax.psum(ffn_grads[3].astype(jnp.bfloat16), "replica").astype(jnp.float32),
        lax.psum(ffn_grads[4].astype(jnp.bfloat16), "replica").astype(jnp.float32),
        lax.psum(ffn_grads[5].astype(jnp.bfloat16), "replica").astype(jnp.float32),
        lax.psum(ffn_grads[6].astype(jnp.bfloat16), "replica").astype(jnp.float32),
        lax.psum(ffn_grads[7].astype(jnp.bfloat16), "replica").astype(jnp.float32),
    )
    qkv_back, out_back, hs_back = (
        lax.all_gather(w_qkv, "fsdp", axis=0, tiled=True),
        lax.all_gather(w_out, "fsdp", axis=0, tiled=True),
        lax.all_gather(head_scale, "fsdp", axis=0, tiled=True),
    )
    d_z, grad_pg, grad_pb = post_pull(d_resid)
    d_z_b = d_z.astype(jnp.bfloat16)
    grad_out = jnp.einsum("te,td->ed", mixed_b, d_z_b, preferred_element_type=jnp.float32)
    grad_bo = jnp.sum(d_z_b.astype(jnp.float32), axis=0)
    d_mixed = jnp.einsum("td,ed->te", d_z_b, out_back, preferred_element_type=jnp.float32)
    grad_hs = jnp.sum(jnp.sum(d_mixed * attn, axis=0).reshape(H, HD), axis=1)
    d_attn_b = (d_mixed * jnp.repeat(hs_back.astype(jnp.float32), HD)).astype(jnp.bfloat16)
    d_proj_b = attend_backward(proj_b, segments, lse_all, d_attn_b).astype(jnp.bfloat16)
    grad_qkv = jnp.einsum("td,te->de", normed_b, d_proj_b, preferred_element_type=jnp.float32)
    col_sums = jnp.sum(d_proj_b.astype(jnp.float32), axis=0)
    grad_bq = col_sums[:width]
    grad_bv = col_sums[2 * width :]
    d_normed = jnp.einsum("te,de->td", d_proj_b, qkv_back, preferred_element_type=jnp.float32)
    d_x_one, grad_g_one, grad_b_one = ln1_pull(d_normed)
    dx_rows = (d_resid + d_x_one).astype(jnp.bfloat16)
    attn_grads = (
        lax.psum_scatter(
            grad_g_one.astype(jnp.bfloat16), "fsdp", scatter_dimension=0, tiled=True
        ).astype(jnp.float32),
        lax.psum_scatter(
            grad_b_one.astype(jnp.bfloat16), "fsdp", scatter_dimension=0, tiled=True
        ).astype(jnp.float32),
        lax.psum_scatter(
            grad_qkv.astype(jnp.bfloat16), "fsdp", scatter_dimension=0, tiled=True
        ).astype(jnp.float32),
        lax.psum_scatter(
            grad_bq.astype(jnp.bfloat16), "fsdp", scatter_dimension=0, tiled=True
        ).astype(jnp.float32),
        lax.psum_scatter(
            grad_bv.astype(jnp.bfloat16), "fsdp", scatter_dimension=0, tiled=True
        ).astype(jnp.float32),
        lax.psum_scatter(
            grad_hs.astype(jnp.bfloat16), "fsdp", scatter_dimension=0, tiled=True
        ).astype(jnp.float32),
        lax.psum_scatter(
            grad_out.astype(jnp.bfloat16), "fsdp", scatter_dimension=0, tiled=True
        ).astype(jnp.float32),
        lax.psum_scatter(
            grad_bo.astype(jnp.bfloat16), "fsdp", scatter_dimension=0, tiled=True
        ).astype(jnp.float32),
        lax.psum_scatter(
            grad_pg.astype(jnp.bfloat16), "fsdp", scatter_dimension=0, tiled=True
        ).astype(jnp.float32),
        lax.psum_scatter(
            grad_pb.astype(jnp.bfloat16), "fsdp", scatter_dimension=0, tiled=True
        ).astype(jnp.float32),
    )
    attn_grads = (
        lax.psum(attn_grads[0].astype(jnp.bfloat16), "replica").astype(jnp.float32),
        lax.psum(attn_grads[1].astype(jnp.bfloat16), "replica").astype(jnp.float32),
        lax.psum(attn_grads[2].astype(jnp.bfloat16), "replica").astype(jnp.float32),
        lax.psum(attn_grads[3].astype(jnp.bfloat16), "replica").astype(jnp.float32),
        lax.psum(attn_grads[4].astype(jnp.bfloat16), "replica").astype(jnp.float32),
        lax.psum(attn_grads[5].astype(jnp.bfloat16), "replica").astype(jnp.float32),
        lax.psum(attn_grads[6].astype(jnp.bfloat16), "replica").astype(jnp.float32),
        lax.psum(attn_grads[7].astype(jnp.bfloat16), "replica").astype(jnp.float32),
        lax.psum(attn_grads[8].astype(jnp.bfloat16), "replica").astype(jnp.float32),
        lax.psum(attn_grads[9].astype(jnp.bfloat16), "replica").astype(jnp.float32),
    )
    got_out, got_dx = (
        lax.all_to_all(
            jnp.take(out_rows, recv_order, axis=0).reshape(devices, per_pair, width),
            ("replica", "fsdp"),
            split_axis=0,
            concat_axis=0,
            tiled=True,
        ),
        lax.all_to_all(
            jnp.take(dx_rows, recv_order, axis=0).reshape(devices, per_pair, width),
            ("replica", "fsdp"),
            split_axis=0,
            concat_axis=0,
            tiled=True,
        ),
    )
    restore = jnp.argsort(send_order)
    output = jnp.take(got_out.reshape(count, width), restore, axis=0)
    grad_tokens = jnp.take(got_dx.reshape(count, width), restore, axis=0)
    return (
        output,
        grad_tokens,
        attn_grads[0],
        attn_grads[1],
        attn_grads[2],
        attn_grads[3],
        attn_grads[4],
        attn_grads[5],
        attn_grads[6],
        attn_grads[7],
        attn_grads[8],
        attn_grads[9],
        ffn_grads[0],
        ffn_grads[1],
        ffn_grads[2],
        ffn_grads[3],
        ffn_grads[4],
        ffn_grads[5],
        ffn_grads[6],
        ffn_grads[7],
    )


def solution(mesh):
    in_specs = (
        P(("replica", "fsdp"), None),
        P(("replica", "fsdp"), None),
        P(("replica", "fsdp"), None),
        P(("replica", "fsdp")),
        P(("replica", "fsdp")),
        P("fsdp"),
        P("fsdp"),
        P("fsdp", None),
        P("fsdp"),
        P("fsdp"),
        P("fsdp"),
        P("fsdp", None),
        P("fsdp"),
        P("fsdp"),
        P("fsdp"),
        P("fsdp"),
        P("fsdp"),
        P("fsdp", None),
        P("fsdp"),
        P("fsdp"),
        P("fsdp"),
        P("fsdp", None),
        P("fsdp"),
    )
    out_specs = (
        P(("replica", "fsdp"), None),
        P(("replica", "fsdp"), None),
        P("fsdp"),
        P("fsdp"),
        P("fsdp", None),
        P("fsdp"),
        P("fsdp"),
        P("fsdp"),
        P("fsdp", None),
        P("fsdp"),
        P("fsdp"),
        P("fsdp"),
        P("fsdp"),
        P("fsdp"),
        P("fsdp", None),
        P("fsdp"),
        P("fsdp"),
        P("fsdp"),
        P("fsdp", None),
        P("fsdp"),
    )
    return jax.shard_map(
        on_device, mesh=mesh, in_specs=in_specs, out_specs=out_specs, check_vma=False
    )
```

profile of v0, /device:TPU:0, one launch (start us, length us, event | category | flops | bytes accessed | tf_op | source)
XLA Modules:
  0.0 1442.6 jit_solution(6756166801208897077)
XLA Ops:
  9.4 5.7 sort.59
  20.2 9.0 gather_fusion
  33.1 5.3 reshape.542
  38.4 11.5 all-to-all-start
  52.9 49.8 %all-to-all-done = bf16[128,9,1024]{2,1,0:T(8,128)(2,1)} async-done(((bf16[128,9,1024]{2,1,0:T(8,128)(2,1)}), bf16[128,9,1024]{2,1,0:T(8,128)(2,1)}, u32[]{:S(2)}, u32[]{:S(2)}) %all-to-all-start) | async-done | bytes 2359328 | tf_op jit(solution)/shard_map/all_to_all | solution.py:185
  102.7 7.4 all-to-all-start.2
  115.0 93.5 %all-reduce.24 = (bf16[16]{0:T(256)(128)(2,1)S(1)}, bf16[1024]{0:T(1024)(128)(2,1)S(1)}, bf16[1024]{0:T(1024)(128)(2,1)S(1)}, bf16[1024]{0:T(1024)(128)(2,1)S(1)...) all-reduce(bf16[16]{0:T(256)(128)(2,1)S(1)} %dynamic-update-slice.4, ...), channel_id=1, replica_groups=mesh['replica'=8,'fsdp'=16] {'fsdp'}, use_global_device_ids=true, to_apply=%add.4 | all-reduce | flops 9232 | bytes 36928
  209.5 16.0 %all-gather = bf16[16,1,256]{2,1,0:T(2,128)(2,1)S(1)} all-gather(bf16[1,1,256]{2,1,0:T(2,128)(2,1)S(1)} %reshape.660), channel_id=1, replica_groups=mesh['replica'=8,'fsdp'=16] {'fsdp'}, dimensions={0}, use_global_device_ids=true | all-gather | bytes 8704 | tf_op jit(solution)/shard_map/all_gather | solution.py:239
  227.9 18.5 %all-gather.1 = bf16[16,1,256]{2,1,0:T(2,128)(2,1)S(1)} all-gather(bf16[1,1,256]{2,1,0:T(2,128)(2,1)S(1)} %reshape.662), channel_id=1, replica_groups=mesh['replica'=8,'fsdp'=16] {'fsdp'}, dimensions={0}, use_global_device_ids=true | all-gather | bytes 8704 | tf_op jit(solution)/shard_map/all_gather | solution.py:240
  247.1 16.4 %all-gather.2 = bf16[16,1,256]{2,1,0:T(2,128)(2,1)S(1)} all-gather(bf16[1,1,256]{2,1,0:T(2,128)(2,1)S(1)} %reshape.664), channel_id=1, replica_groups=mesh['replica'=8,'fsdp'=16] {'fsdp'}, dimensions={0}, use_global_device_ids=true | all-gather | bytes 8704 | tf_op jit(solution)/shard_map/all_gather | solution.py:241
  302.4 13.0 add_convert_fusion.2
  315.4 10.0 copy.91
  328.0 141.4 %while.36 = (s32[]{:T(128)}, f32[1152,1024]{1,0:T(8,128)}, f32[16,1152]{1,0:T(8,128)S(1)}, bf16[1152,3072]{0,1:T(8,128)(2,1)}, s32[1152]{0:T(1024)S(1)}, /*index...) while((s32[]{:T(128)}, f32[1152,1024]{1,0:T(8,128)}, ...), condition=%wide.region_10.12_spmd, body=%wide.region_7.11_spmd.sunk | while | flops 713317888 | bytes 41995628 | solution.py:100
  470.1 6.2 fusion.54
  485.7 56.0 %fusion.49 = (f32[1152]{0:T(1024)S(1)}, f32[1152,4096]{1,0:T(8,128)}, f32[1152,4096]{1,0:T(8,128)}, f32[1152,4096]{1,0:T(8,128)}) fusion(f32[4096]{0:T(1024)S(1)} %bitcast.127, bf16[1024,4096]{1,0:T(8,128)(2,1)} %all-gather.12.cloned.1.call-done, bf16[1152,1024]{0,1:T(8,128)(2,1)} %add_convert_fusion.8.clone.4), kind=kOutput, calls=%fused_computation.168 | convolution fusion | flops 9975102464 | bytes 67392000 | tf_op jit(solution)/shard_map/dot_general | solution.py:249
  541.7 22.2 %multiply_reduce_fusion.2 = (f32[1152]{0:T(1024)S(1)}, f32[1152]{0:T(1024)S(1)}, bf16[4096]{0:T(1024)(128)(2,1)S(1)}, f32[1152,4096]{1,0:T(8,128)}) fusion(f32[1152,4096]{1,0:T(8,128)} %get-tuple-element.620, f32[4096]{0:T(1024)S(1)} %bitcast.123, f32[1152]{0:T(1024)S(1)} %broadcast_multiply_fusion, bf16[4096,1024]{1,0:T(8,128)(2,1)} %all-gather.14.cloned.1.call-done, ...), kind=kOutput, calls=%fused_computation.43 | convolution fusion | flops 9697880064 | bytes 48536192 | tf_op jit(solution)/shard_map/td,fd->tf/dot_general | solution.py:268
  563.9 19.8 %multiply_reduce_fusion.1 = (bf16[4096]{0:T(1024)(128)(2,1)}, f32[1152]{0:T(1024)S(1)}, bf16[1152,4096]{1,0:T(8,128)(2,1)}) fusion(f32[1152,4096]{1,0:T(8,128)} %get-tuple-element.650, f32[1152,4096]{1,0:T(8,128)} %get-tuple-element.620, f32[1152]{0:T(1024)S(1)} %get-tuple-element.636, f32[1152]{0:T(1024)S(1)} %broadcast_multiply_fusion, ...), kind=kLoop, calls=%fused_computation.41 | loop fusion | flops 61336448 | bytes 47245312 | tf_op jit(solution)/shard_map/transpose(jvp())/reduce_sum | solution.py:30
  583.7 26.5 %fusion.47 = (bf16[4096]{0:T(1024)(128)(2,1)}, bf16[1152,4096]{1,0:T(8,128)(2,1)S(1)}) fusion(f32[1152,4096]{1,0:T(8,128)} %get-tuple-element.621, f32[1152,4096]{1,0:T(8,128)} %get-tuple-element.649, f32[1152]{0:T(1024)S(1)} %negate_multiply_fusion.4, f32[1152]{0:T(1024)S(1)} %get-tuple-element.635, f32[1152,4096]{1,0:T(8,128)} %get-tuple-element.620, ...), kind=kLoop, calls=%fused_computation.166 | loop fusion | flops 103804928 | bytes 84977664 | tf_op jit(solution)/shard_map/reduce_sum | solution.py:272
  610.3 13.9 convolution_convert_fusion.1
  624.1 14.2 fusion.56
  638.5 11.1 pad_maximum_fusion
  649.6 16.6 %convolution_convert_fusion = bf16[4096,1024]{0,1:T(8,128)(2,1)} fusion(bf16[1152,4096]{1,0:T(8,128)(2,1)} %get-tuple-element.632, bf16[1152,1024]{0,1:T(8,128)(2,1)S(1)} %copy-done.13, pred[1152]{0:T(1024)(128)(4,1)S(1)} %copy-done.28), kind=kOutput, calls=%fused_computation.65 | convolution fusion | flops 9669050368 | bytes 20186240 | tf_op jit(solution)/shard_map/tf,td->fd/dot_general | solution.py:266
  666.3 9.7 pad_maximum_fusion.1
  680.5 6.3 copy.96
  710.0 7.8 multiply_reduce_fusion.6
  717.8 5.9 broadcast_in_dim.195
  723.8 344.0 %while.37 = (s32[]{:T(128)}, f32[1152,3072]{0,1:T(8,128)}, bf16[1152,3072]{0,1:T(8,128)(2,1)}, s32[1152]{0:T(1024)S(1)}, f32[16,1152]{1,0:T(8,128)}, /*index=5*/...) while((s32[]{:T(128)}, f32[1152,3072]{0,1:T(8,128)}, ...), condition=%wide.region_26.28_spmd, body=%wide.region_24.27_spmd.sunk | while | flops 1725603328 | bytes 194861568 | solution.py:148
  726.8 5.5 fusion.120
  735.0 7.8 multiply_reduce_fusion.12
  759.8 5.2 fusion.121
  770.0 5.5 fusion.120
  778.3 7.8 multiply_reduce_fusion.12
  803.1 5.1 fusion.121
  813.1 5.5 fusion.120
  821.3 7.7 multiply_reduce_fusion.12
  846.0 5.1 fusion.121
  856.1 5.5 fusion.120
  864.3 7.8 multiply_reduce_fusion.12
  889.1 5.1 fusion.121
  899.1 5.5 fusion.120
  907.3 7.8 multiply_reduce_fusion.12
  931.9 5.1 fusion.121
  941.9 5.5 fusion.120
  950.1 7.7 multiply_reduce_fusion.12
  984.7 5.5 fusion.120
  992.9 7.7 multiply_reduce_fusion.12
  1017.4 5.1 fusion.121
  1027.5 5.5 fusion.120
  1035.7 7.8 multiply_reduce_fusion.12
  1060.3 5.1 fusion.121
  1067.8 16.1 %convolution_convert_fusion.2 = bf16[1024,3072]{1,0:T(8,128)(2,1)} fusion(f32[1152,3072]{0,1:T(8,128)} %get-tuple-element.413, f32[1024]{0:T(1024)S(1)} %copy-done.72, f32[1024]{0:T(1024)S(1)} %copy-done.54, f32[1152]{0:T(1024)S(1)} %copy-done.51, f32[1152]{0:T(1024)S(1)} %copy-done.26, bf16[1152,1024]{0,1:T(8,128)(2,1)} %copy-done.6, ...), kind=kOutput, calls=%fused_computation.77 | convolution fusion | flops 7262699520 | bytes 22825088 | tf_op jit(solution)/shard_map/td,te->de/dot_general | solution.py:329
  1084.0 15.4 %fusion.55 = (bf16[1024]{0:T(1024)(128)(2,1)S(1)}, f32[1152,1024]{1,0:T(8,128)}) fusion(bf16[1024,3072]{1,0:T(8,128)(2,1)} %all-gather.8.cloned.1.call-done, f32[1152,3072]{0,1:T(8,128)} %get-tuple-element.413), kind=kOutput, calls=%fused_computation.173 | convolution fusion | flops 7252474880 | bytes 25167872 | tf_op jit(solution)/shard_map/te,de->td/dot_general | solution.py:333
  1099.4 6.3 copy.99
  1118.7 5.8 convert_reduce_fusion.2
  1124.6 54.7 %all-reduce.23 = (bf16[1024]{0:T(1024)(128)(2,1)S(1)}, bf16[1024]{0:T(1024)(128)(2,1)S(1)}, bf16[1024]{0:T(1024)(128)(2,1)S(1)}, bf16[1024]{0:T(1024)(128)(2,1)S...) all-reduce(bf16[1024]{0:T(1024)(128)(2,1)} %dynamic-update-slice.10, ...), channel_id=1, replica_groups=mesh['replica'=8,'fsdp'=16] {'fsdp'}, use_global_device_ids=true, to_apply=%add.10 | all-reduce | flops 18448 | bytes 73792
  1179.3 18.0 %add_convert_fusion.5 = bf16[1152,1024]{0,1:T(8,128)(2,1)} fusion(f32[1152,1024]{0,1:T(8,128)} %copy-done.4, bf16[1152,4096]{1,0:T(8,128)(2,1)} %get-tuple-element.632, bf16[4096,1024]{1,0:T(8,128)(2,1)} %all-gather.14.cloned.1.call-done, f32[1024]{0:T(1024)S(1)} %convert_element_type.303), kind=kOutput, calls=%fused_computation.94 | convolution fusion | flops 9667215360 | bytes 24907776 | tf_op jit(solution)/shard_map/dot_general | solution.py:258
  1206.5 8.7 gather_fusion.2
  1219.1 5.4 reshape.550
  1224.5 8.3 all-to-all-start.3
  1235.6 49.9 %all-to-all-done.3 = bf16[128,9,1024]{2,1,0:T(8,128)(2,1)} async-done(((bf16[128,9,1024]{2,1,0:T(8,128)(2,1)}), bf16[128,9,1024]{2,1,0:T(8,128)(2,1)}, u32[]{:S(2)}, u32[]{:S(2)}) %all-to-all-start.3) | async-done | bytes 2359328 | tf_op jit(solution)/shard_map/all_to_all | solution.py:388
  1285.5 5.8 all-to-all-start.1
  1313.3 36.3 %all-to-all-done.1 = bf16[128,9,1024]{2,1,0:T(8,128)(2,1)} async-done(((bf16[128,9,1024]{2,1,0:T(8,128)(2,1)}), bf16[128,9,1024]{2,1,0:T(8,128)(2,1)}, u32[]{:S(2)}, u32[]{:S(2)}) %all-to-all-start.1) | async-done | bytes 2359328 | tf_op jit(solution)/shard_map/all_to_all | solution.py:381
  1364.8 29.2 %all-reduce.25 = (bf16[64]{0:T(256)(128)(2,1)S(1)}, bf16[64]{0:T(256)(128)(2,1)S(1)}, bf16[64]{0:T(256)(128)(2,1)S(1)}, bf16[64]{0:T(256)(128)(2,1)S(1)}, bf16[1...) all-reduce(bf16[64]{0:T(256)(128)(2,1)S(1)} %dynamic-slice.12, ...), channel_id=1, replica_groups=mesh['replica'=8,'fsdp'=16] {'replica'}, use_global_device_ids=true, to_apply=%region_31.33 | all-reduce | flops 1409 | bytes 5636 | tf_op jit(solution)/shard_map/psum | solution.py:369
  1401.5 25.4 %all-reduce.29.cloned.1.call-done = (bf16[256,1024]{0,1:T(8,128)(2,1)}, bf16[64,3072]{1,0:T(8,128)(2,1)}, bf16[64,1024]{1,0:T(8,128)(2,1)}, bf16[64,4096]{1,0:T(8,128)(2,1)}) async-done(((bf16[256,1024]{0,1:T(8,128)(2,1)}, bf16[64,3072]{1,0:T(8,128)(2,1)}, bf16[64,1024]{1,0:T(8,128)(2,1)}, bf16[64,4096]{1,0:T(8,128)(2,1)}), (bf16[256,1024]{0,1:T(8,128)(2,1)}, bf16[64,3072]{1,0:T(8,128)(2,1)}, ...) | async-done | bytes 1572880 | tf_op jit(solution)/shard_map/psum | solution.py:313
  (692 shorter events, 520.7 us)
Async XLA Ops:
  7.2 295.1 %all-gather.8.cloned.1.call-start = ((), (), s32[]{:S(2)}) async-start(), calls=%async_computation.8 | async-start | bytes 6684672 | tf_op jit(solution)/shard_map/all_gather | solution.py:206
  7.9 461.6 %all-gather.10.cloned.1.call-start = ((), (), s32[]{:S(2)}) async-start(), calls=%async_computation.9 | async-start | bytes 2228224 | tf_op jit(solution)/shard_map/all_gather | solution.py:210
  8.7 476.9 %all-gather.12.cloned.1.call-start = ((), (), s32[]{:S(2)}) async-start(), calls=%async_computation.10 | async-start | bytes 8912896 | tf_op jit(solution)/shard_map/all_gather | solution.py:238
  15.2 14.0 copy-start.46
  20.2 9.0 copy-start.15
  38.4 11.5 copy-start.16
  38.4 64.2 %all-to-all-start = ((bf16[128,9,1024]{2,1,0:T(8,128)(2,1)}), bf16[128,9,1024]{2,1,0:T(8,128)(2,1)}, u32[]{:S(2)}, u32[]{:S(2)}) async-start(bf16[128,9,1024]{2,1,0:T(8,128)(2,1)} %reshape.542), calls=%async_computation | async-start | bytes 8388608 | tf_op jit(solution)/shard_map/all_to_all | solution.py:185
  52.7 58.1 %copy-start.73 = (u32[128]{0:T(128)S(1)}, u32[128]{0:T(128)}, u32[]{:S(2)}) copy-start(u32[128]{0:T(128)} %constant.634) | copy-start | bytes 1540
  52.7 59.3 %copy-start.74 = (bf16[64]{0:T(256)(128)(2,1)S(1)}, bf16[64]{0:T(256)(128)(2,1)}, u32[]{:S(2)}) copy-start(bf16[64]{0:T(256)(128)(2,1)} %param.41) | copy-start | bytes 388
  52.7 59.6 %copy-start.75 = (bf16[64]{0:T(256)(128)(2,1)S(1)}, bf16[64]{0:T(256)(128)(2,1)}, u32[]{:S(2)}) copy-start(bf16[64]{0:T(256)(128)(2,1)} %param.38) | copy-start | bytes 388
  52.8 59.8 %copy-start.76 = (bf16[64]{0:T(256)(128)(2,1)S(1)}, bf16[64]{0:T(256)(128)(2,1)}, u32[]{:S(2)}) copy-start(bf16[64]{0:T(256)(128)(2,1)} %param.37) | copy-start | bytes 388
  52.8 60.0 %copy-start.77 = (bf16[64]{0:T(256)(128)(2,1)S(1)}, bf16[64]{0:T(256)(128)(2,1)}, u32[]{:S(2)}) copy-start(bf16[64]{0:T(256)(128)(2,1)} %param.35) | copy-start | bytes 388
  52.8 60.3 %copy-start.78 = (bf16[64]{0:T(256)(128)(2,1)S(1)}, bf16[64]{0:T(256)(128)(2,1)}, u32[]{:S(2)}) copy-start(bf16[64]{0:T(256)(128)(2,1)} %param.34) | copy-start | bytes 388
  52.8 60.5 %copy-start.79 = (bf16[64]{0:T(256)(128)(2,1)S(1)}, bf16[64]{0:T(256)(128)(2,1)}, u32[]{:S(2)}) copy-start(bf16[64]{0:T(256)(128)(2,1)} %param.43) | copy-start | bytes 388
  52.8 60.7 %copy-start.80 = (bf16[64]{0:T(256)(128)(2,1)S(1)}, bf16[64]{0:T(256)(128)(2,1)}, u32[]{:S(2)}) copy-start(bf16[64]{0:T(256)(128)(2,1)} %param.42) | copy-start | bytes 388
  52.8 60.9 %copy-start.81 = (bf16[64]{0:T(256)(128)(2,1)S(1)}, bf16[64]{0:T(256)(128)(2,1)}, u32[]{:S(2)}) copy-start(bf16[64]{0:T(256)(128)(2,1)} %param.45) | copy-start | bytes 388
  52.8 61.1 %copy-start.82 = (bf16[64]{0:T(256)(128)(2,1)S(1)}, bf16[64]{0:T(256)(128)(2,1)}, u32[]{:S(2)}) copy-start(bf16[64]{0:T(256)(128)(2,1)} %param.44) | copy-start | bytes 388
  52.8 156.3 %copy-start.83 = (s32[1,3]{1,0:T(1,128)S(1)}, s32[1,3]{1,0:T(1,128)}, u32[]{:S(2)}) copy-start(s32[1,3]{1,0:T(1,128)} %param.31) | copy-start | bytes 40
  52.8 156.7 %copy-start.84 = (bf16[256]{0:T(256)(128)(2,1)S(1)}, bf16[256]{0:T(256)(128)(2,1)}, u32[]{:S(2)}) copy-start(bf16[256]{0:T(256)(128)(2,1)} %param.47) | copy-start | bytes 1540
  52.9 175.0 %copy-start.85 = (bf16[256]{0:T(256)(128)(2,1)S(1)}, bf16[256]{0:T(256)(128)(2,1)}, u32[]{:S(2)}) copy-start(bf16[256]{0:T(256)(128)(2,1)} %param.48) | copy-start | bytes 1540
  52.9 194.2 %copy-start.86 = (bf16[256]{0:T(256)(128)(2,1)S(1)}, bf16[256]{0:T(256)(128)(2,1)}, u32[]{:S(2)}) copy-start(bf16[256]{0:T(256)(128)(2,1)} %param.49) | copy-start | bytes 1540
  52.9 211.2 %copy-start.67 = (s32[1152]{0:T(1024)S(1)}, s32[1152]{0:T(1024)}, u32[]{:S(2)}) copy-start(s32[1152]{0:T(1024)} %param.32) | copy-start | bytes 13828
  102.7 186.0 %all-to-all-start.2 = ((bf16[128,9,1024]{2,1,0:T(8,128)(2,1)}), bf16[128,9,1024]{2,1,0:T(8,128)(2,1)}, u32[]{:S(2)}, u32[]{:S(2)}) async-start(bf16[128,9,1024]{2,1,0:T(8,128)(2,1)} %reshape.548), calls=%async_computation.2 | async-start | bytes 8388608 | tf_op jit(solution)/shard_map/all_to_all | solution.py:192
  110.1 431.6 %all-gather.14.cloned.1.call-start = ((), (), s32[]{:S(2)}) async-start(), calls=%async_computation.11 | async-start | bytes 8912896 | tf_op jit(solution)/shard_map/all_gather | solution.py:242
  115.0 1183.1 %reduce-scatter.9.cloned.1.call-start = ((), (), s32[]{:S(2)}) async-start(), calls=%async_computation.14 | async-start | bytes 9191424 | tf_op jit(solution)/shard_map/reduce_scatter | solution.py:18
  209.1 93.2 %copy-start.71 = (f32[1024]{0:T(1024)}, f32[1024]{0:T(1024)S(1)}, u32[]{:S(2)}) copy-start(f32[1024]{0:T(1024)S(1)} %convert_element_type.285) | copy-start | bytes 12292
  209.2 93.2 %copy-start.53 = (f32[1024]{0:T(1024)}, f32[1024]{0:T(1024)S(1)}, u32[]{:S(2)}) copy-start(f32[1024]{0:T(1024)S(1)} %convert_element_type.284) | copy-start | bytes 12292
  209.5 260.0 %copy-start.68 = (f32[1024]{0:T(1024)}, f32[1024]{0:T(1024)S(1)}, u32[]{:S(2)}) copy-start(f32[1024]{0:T(1024)S(1)} %mul.433) | copy-start | bytes 12292
  274.4 202.5 %copy-start.27 = (pred[1152]{0:T(1024)(128)(4,1)}, pred[1152]{0:T(1024)(128)(4,1)S(1)}, u32[]{:S(2)}) copy-start(pred[1152]{0:T(1024)(128)(4,1)S(1)} %compare_and_fusion.4) | copy-start | bytes 3460
  287.3 15.1 %copy-start.25 = (f32[1152]{0:T(1024)}, f32[1152]{0:T(1024)S(1)}, u32[]{:S(2)}) copy-start(f32[1152]{0:T(1024)S(1)} %broadcast_multiply_fusion.3) | copy-start | bytes 13828
  288.7 13.7 copy-start.50
  485.6 56.0 %copy-start.13 = (bf16[1152,1024]{0,1:T(8,128)(2,1)S(1)}, bf16[1152,1024]{0,1:T(8,128)(2,1)}, u32[]{:S(2)}) copy-start(bf16[1152,1024]{0,1:T(8,128)(2,1)} %copy.95) | copy-start | bytes 7077892
  485.6 56.0 %copy-start.28 = (pred[1152]{0:T(1024)(128)(4,1)S(1)}, pred[1152]{0:T(1024)(128)(4,1)}, u32[]{:S(2)}) copy-start(pred[1152]{0:T(1024)(128)(4,1)} %copy-done.27) | copy-start | bytes 3460
  485.7 56.0 %copy-start.30 = (f32[16,1,256]{2,1,0:T(1,128)S(1)}, f32[16,1,256]{2,1,0:T(1,128)}, u32[]{:S(2)}) copy-start(f32[16,1,256]{2,1,0:T(1,128)} %convert_element_type.346) | copy-start | bytes 49156
  541.7 22.2 %copy-start.52 = (f32[16,1,256]{2,1,0:T(1,128)S(1)}, f32[16,1,256]{2,1,0:T(1,128)}, u32[]{:S(2)}) copy-start(f32[16,1,256]{2,1,0:T(1,128)} %convert_element_type.347) | copy-start | bytes 49156
  563.9 46.3 %slice-start.3 = ((s8[4718592]{0:T(1024)(128)(4,1)}), s8[4194304]{0:T(1024)(128)(4,1)S(1)}, s32[]{:S(2)}) async-start(s8[4718592]{0:T(1024)(128)(4,1)} %bitcast.101), calls=%async_computation.20 | async-start | bytes 8388608
  583.7 26.5 %slice-start.4 = ((s8[4718592]{0:T(1024)(128)(4,1)}), s8[524288]{0:T(1024)(128)(4,1)S(1)}, s32[]{:S(2)}) async-start(s8[4718592]{0:T(1024)(128)(4,1)} %bitcast.101), calls=%async_computation.21 | async-start | bytes 1048576
  583.7 26.5 %copy-start.23 = (f32[1152]{0:T(1024)S(1)}, f32[1152]{0:T(1024)}, u32[]{:S(2)}) copy-start(f32[1152]{0:T(1024)} %copy-done.22) | copy-start | bytes 13828
  583.7 26.5 %copy-start.34 = (f32[1152]{0:T(1024)S(1)}, f32[1152]{0:T(1024)}, u32[]{:S(2)}) copy-start(f32[1152]{0:T(1024)} %copy-done.33) | copy-start | bytes 13828
  583.7 26.5 %copy-start.38 = (f32[1024]{0:T(1024)S(1)}, f32[1024]{0:T(1024)}, u32[]{:S(2)}) copy-start(f32[1024]{0:T(1024)} %convert_element_type.296) | copy-start | bytes 12292
  583.7 26.5 %copy-start.59 = (f32[1024]{0:T(1024)S(1)}, f32[1024]{0:T(1024)}, u32[]{:S(2)}) copy-start(f32[1024]{0:T(1024)} %convert_element_type.297) | copy-start | bytes 12292
  649.6 650.5 %reduce-scatter.11.cloned.1.call-start = ((), (), s32[]{:S(2)}) async-start(), calls=%async_computation.15 | async-start | bytes 8982528 | tf_op jit(solution)/shard_map/reduce_scatter | solution.py:18
  676.0 626.1 %reduce-scatter.7.cloned.1.call-start = ((), (), s32[]{:S(2)}) async-start(), calls=%async_computation.13 | async-start | bytes 2228224 | tf_op jit(solution)/shard_map/reduce_scatter | solution.py:355
  680.5 11.0 slice-start.5
  686.8 9.5 slice-start.7
  709.9 592.1 %reduce-scatter.5.cloned.1.call-start = ((), (), s32[]{:S(2)}) async-start(), calls=%async_computation.12 | async-start | bytes 6684672 | tf_op jit(solution)/shard_map/reduce_scatter | solution.py:343
  723.7 344.1 %copy-start.26 = (f32[1152]{0:T(1024)S(1)}, f32[1152]{0:T(1024)}, u32[]{:S(2)}) copy-start(f32[1152]{0:T(1024)} %copy-done.25) | copy-start | bytes 13828
  723.7 344.1 %copy-start.29 = (pred[1152]{0:T(1024)(128)(4,1)S(1)}, pred[1152]{0:T(1024)(128)(4,1)}, u32[]{:S(2)}) copy-start(pred[1152]{0:T(1024)(128)(4,1)} %copy-done.27) | copy-start | bytes 3460
  723.7 344.1 %copy-start.51 = (f32[1152]{0:T(1024)S(1)}, f32[1152]{0:T(1024)}, u32[]{:S(2)}) copy-start(f32[1152]{0:T(1024)} %copy-done.50) | copy-start | bytes 13828
  723.7 344.1 %copy-start.54 = (f32[1024]{0:T(1024)S(1)}, f32[1024]{0:T(1024)}, u32[]{:S(2)}) copy-start(f32[1024]{0:T(1024)} %copy-done.53) | copy-start | bytes 12292
  723.8 344.1 %copy-start.72 = (f32[1024]{0:T(1024)S(1)}, f32[1024]{0:T(1024)}, u32[]{:S(2)}) copy-start(f32[1024]{0:T(1024)} %copy-done.71) | copy-start | bytes 12292
  734.4 8.4 slice-start
  777.7 8.4 slice-start
  863.7 8.4 slice-start
  906.7 8.4 slice-start
  1099.4 9.8 copy-start.41
  1099.4 12.8 slice-start.9
  1206.5 8.7 copy-start.14
  1206.5 8.7 copy-start.61
  1224.5 61.0 %all-to-all-start.3 = ((bf16[128,9,1024]{2,1,0:T(8,128)(2,1)}), bf16[128,9,1024]{2,1,0:T(8,128)(2,1)}, u32[]{:S(2)}, u32[]{:S(2)}) async-start(bf16[128,9,1024]{2,1,0:T(8,128)(2,1)} %reshape.550), calls=%async_computation.3 | async-start | bytes 8388608 | tf_op jit(solution)/shard_map/all_to_all | solution.py:388
  1235.6 56.1 %copy-start.47 = (s32[1152]{0:T(1024)S(1)}, s32[1152]{0:T(1024)}, u32[]{:S(2)}) copy-start(s32[1152]{0:T(1024)} %copy-done.46) | copy-start | bytes 13828
  1285.5 64.2 %all-to-all-start.1 = ((bf16[128,9,1024]{2,1,0:T(8,128)(2,1)}), bf16[128,9,1024]{2,1,0:T(8,128)(2,1)}, u32[]{:S(2)}, u32[]{:S(2)}) async-start(bf16[128,9,1024]{2,1,0:T(8,128)(2,1)} %reshape.546), calls=%async_computation.1 | async-start | bytes 8388608 | tf_op jit(solution)/shard_map/all_to_all | solution.py:381
  1291.4 135.5 %all-reduce.29.cloned.1.call-start = ((), (), s32[]{:S(2)}) async-start(), calls=%async_computation.16 | async-start | bytes 3145728 | tf_op jit(solution)/shard_map/psum | solution.py:313
  1358.8 75.9 %copy-start.1 = (bf16[1152,1024]{1,0:T(8,128)(2,1)S(1)}, bf16[1152,1024]{1,0:T(8,128)(2,1)}, u32[]{:S(2)}) copy-start(bf16[1152,1024]{1,0:T(8,128)(2,1)} %param.30) | copy-start | bytes 7077892
  (85 other events, 411.6 us)
Sparse Core Ops, SparseCore 0:
  9.7 90.5 all-gather.7
  102.0 77.2 all-gather.9
  181.0 53.5 all-gather.11
  236.2 53.1 all-gather.13
  649.7 75.3 reduce-scatter.8
  727.5 73.4 reduce-scatter.10
  803.6 61.9 reduce-scatter.6
  1084.1 70.9 reduce-scatter.4
  1302.2 124.5 all-reduce.28
where the time goes:
time: 1460 us; the launch traced here: 1440 us
  matrix products  438 us (30%)
  local copies, waits for them, and re-layouts  315 us (22%)
  other arithmetic  241 us (17%)
  blocking collectives  228 us (16%)
  waiting for transfers between devices  164 us (11%)
  starting transfers between devices  33.6 us (2%)
  between operations  19.7 us (1%)
    unnamed x2, blocking collectives  148 us
    dot_general x16, matrix products, block_parts(): jnp.einsum('qhd,khd->hqk', query_rows, key_rows, preferred_element_type=j...  81.1 us
    dot_general x1, matrix products, on_device(): jnp.dot(normed_two_b, fc1_full, preferred_element_type=jnp.float32)  56 us
    all_to_all x1, waiting for transfers between devices, on_device(): lax.all_to_all(jnp.take(dx_rows, recv_order, axis=0).reshape(devices, per...  49.9 us
    all_to_all x1, waiting for transfers between devices, on_device(): lax.all_to_all(jnp.take(tokens, send_order, axis=0).reshape(devices, per_...  49.8 us
    dot_general x8, matrix products, back_turn(): jnp.einsum('qhd,khd->hqk', d_out, value_rows, preferred_element_type=jnp....  44 us
    dot_general x8, matrix products, back_turn(): jnp.einsum('hqk,qhd->khd', prob_rows.astype(jnp.bfloat16), d_out, preferr...  40.6 us
    reduce_sum x7, other arithmetic, layer_norm(): return centred * lax.rsqrt(spread + EPS) * gain_vec + bias_vec  40.1 us
  transfers between devices with their start and end apart: 13, of which 4 were waited for; matrix products, arithmetic and copies ran while one was open for 58% of the time, Pallas kernels for 0%

commit v1 on v0

--- a/solution.py
+++ b/solution.py
@@ -35,9 +35,13 @@
 
 
 def segment_ids(lengths_row, count):
-    seq_ends = jnp.cumsum(lengths_row)
     places = jnp.arange(count, dtype=jnp.int32)
-    return jnp.sum((places[:, None] >= seq_ends[None, :]).astype(jnp.int32), axis=1)
+    segments = jnp.zeros((count,), jnp.int32)
+    seq_end = jnp.zeros((), jnp.int32)
+    for i in range(lengths_row.shape[0]):
+        seq_end = seq_end + lengths_row[i]
+        segments = segments + (places >= seq_end).astype(jnp.int32)
+    return segments
 
 
 def block_parts(proj_b, segments, turn_index):

time: 1460 us -> 1460 us (level)
  no operation moved by 1% of the time
where the time goes in v1:
time: 1460 us; the launch traced here: 1450 us
  matrix products  438 us (30%)
  local copies, waits for them, and re-layouts  316 us (22%)
  other arithmetic  242 us (17%)
  blocking collectives  228 us (16%)
  waiting for transfers between devices  163 us (11%)
  starting transfers between devices  33.6 us (2%)
  between operations  21.7 us (1%)
    unnamed x2, blocking collectives  148 us
    dot_general x16, matrix products, block_parts(): jnp.einsum('qhd,khd->hqk', query_rows, key_rows, preferred_element_type=j...  81.1 us
    dot_general x1, matrix products, on_device(): jnp.dot(normed_two_b, fc1_full, preferred_element_type=jnp.float32)  56 us
    all_to_all x1, waiting for transfers between devices, on_device(): lax.all_to_all(jnp.take(dx_rows, recv_order, axis=0).reshape(devices, per...  49.9 us
    all_to_all x1, waiting for transfers between devices, on_device(): lax.all_to_all(jnp.take(tokens, send_order, axis=0).reshape(devices, per_...  49.8 us
    dot_general x8, matrix products, back_turn(): jnp.einsum('qhd,khd->hqk', d_out, value_rows, preferred_element_type=jnp....  44 us
    dot_general x8, matrix products, back_turn(): jnp.einsum('hqk,qhd->khd', prob_rows.astype(jnp.bfloat16), d_out, preferr...  40.6 us
    reduce_sum x7, other arithmetic, layer_norm(): return centred * lax.rsqrt(spread + EPS) * gain_vec + bias_vec  40.2 us
  transfers between devices with their start and end apart: 13, of which 4 were waited for; matrix products, arithmetic and copies ran while one was open for 58% of the time, Pallas kernels for 0%

profile of v1, /device:TPU:0, one launch (start us, length us, event | category | flops | bytes accessed | tf_op | source)
XLA Modules:
  0.0 1445.6 jit_solution(2935785435335697814)
XLA Ops:
  9.4 5.7 sort.59
  20.2 9.0 gather_fusion
  33.1 5.3 reshape.524
  38.4 11.5 all-to-all-start
  52.9 49.8 %all-to-all-done = bf16[128,9,1024]{2,1,0:T(8,128)(2,1)} async-done(((bf16[128,9,1024]{2,1,0:T(8,128)(2,1)}), bf16[128,9,1024]{2,1,0:T(8,128)(2,1)}, u32[]{:S(2)}, u32[]{:S(2)}) %all-to-all-start) | async-done | bytes 2359328 | tf_op jit(solution)/shard_map/all_to_all | solution.py:189
  102.7 7.4 all-to-all-start.2
  115.0 93.5 %all-reduce.24 = (bf16[16]{0:T(256)(128)(2,1)S(1)}, bf16[1024]{0:T(1024)(128)(2,1)S(1)}, bf16[1024]{0:T(1024)(128)(2,1)S(1)}, bf16[1024]{0:T(1024)(128)(2,1)S(1)...) all-reduce(bf16[16]{0:T(256)(128)(2,1)S(1)} %dynamic-update-slice.4, ...), channel_id=1, replica_groups=mesh['replica'=8,'fsdp'=16] {'fsdp'}, use_global_device_ids=true, to_apply=%add.4 | all-reduce | flops 9232 | bytes 36928
  209.3 16.0 %all-gather = bf16[16,1,256]{2,1,0:T(2,128)(2,1)S(1)} all-gather(bf16[1,1,256]{2,1,0:T(2,128)(2,1)S(1)} %reshape.640), channel_id=1, replica_groups=mesh['replica'=8,'fsdp'=16] {'fsdp'}, dimensions={0}, use_global_device_ids=true | all-gather | bytes 8704 | tf_op jit(solution)/shard_map/all_gather | solution.py:243
  227.7 18.5 %all-gather.1 = bf16[16,1,256]{2,1,0:T(2,128)(2,1)S(1)} all-gather(bf16[1,1,256]{2,1,0:T(2,128)(2,1)S(1)} %reshape.642), channel_id=1, replica_groups=mesh['replica'=8,'fsdp'=16] {'fsdp'}, dimensions={0}, use_global_device_ids=true | all-gather | bytes 8704 | tf_op jit(solution)/shard_map/all_gather | solution.py:244
  246.9 16.4 %all-gather.2 = bf16[16,1,256]{2,1,0:T(2,128)(2,1)S(1)} all-gather(bf16[1,1,256]{2,1,0:T(2,128)(2,1)S(1)} %reshape.644), channel_id=1, replica_groups=mesh['replica'=8,'fsdp'=16] {'fsdp'}, dimensions={0}, use_global_device_ids=true | all-gather | bytes 8704 | tf_op jit(solution)/shard_map/all_gather | solution.py:245
  305.2 13.0 add_convert_fusion.2
  318.3 10.1 copy.91
  331.1 141.4 %while.36 = (s32[]{:T(128)}, f32[1152,1024]{1,0:T(8,128)}, f32[16,1152]{1,0:T(8,128)S(1)}, bf16[1152,3072]{0,1:T(8,128)(2,1)}, s32[1152]{0:T(1024)S(1)}, /*index...) while((s32[]{:T(128)}, f32[1152,1024]{1,0:T(8,128)}, ...), condition=%wide.region_8.10_spmd, body=%wide.region_5.9_spmd.sunk | while | flops 713317888 | bytes 41995628 | solution.py:104
  473.1 6.2 fusion.55
  488.6 56.0 %fusion.49 = (f32[1152]{0:T(1024)S(1)}, f32[1152,4096]{1,0:T(8,128)}, f32[1152,4096]{1,0:T(8,128)}, f32[1152,4096]{1,0:T(8,128)}) fusion(f32[4096]{0:T(1024)S(1)} %bitcast.128, bf16[1024,4096]{1,0:T(8,128)(2,1)} %all-gather.12.cloned.1.call-done, bf16[1152,1024]{0,1:T(8,128)(2,1)} %add_convert_fusion.8.clone.4), kind=kOutput, calls=%fused_computation.170 | convolution fusion | flops 9975102464 | bytes 67392000 | tf_op jit(solution)/shard_map/dot_general | solution.py:253
  544.7 22.2 %multiply_reduce_fusion.2 = (f32[1152]{0:T(1024)S(1)}, f32[1152]{0:T(1024)S(1)}, bf16[4096]{0:T(1024)(128)(2,1)S(1)}, f32[1152,4096]{1,0:T(8,128)}) fusion(f32[1152,4096]{1,0:T(8,128)} %get-tuple-element.620, f32[4096]{0:T(1024)S(1)} %bitcast.124, f32[1152]{0:T(1024)S(1)} %broadcast_multiply_fusion, bf16[4096,1024]{1,0:T(8,128)(2,1)} %all-gather.14.cloned.1.call-done, ...), kind=kOutput, calls=%fused_computation.43 | convolution fusion | flops 9697880064 | bytes 48536192 | tf_op jit(solution)/shard_map/td,fd->tf/dot_general | solution.py:272
  566.9 19.9 %multiply_reduce_fusion.1 = (bf16[4096]{0:T(1024)(128)(2,1)}, f32[1152]{0:T(1024)S(1)}, bf16[1152,4096]{1,0:T(8,128)(2,1)}) fusion(f32[1152,4096]{1,0:T(8,128)} %get-tuple-element.653, f32[1152,4096]{1,0:T(8,128)} %get-tuple-element.620, f32[1152]{0:T(1024)S(1)} %get-tuple-element.636, f32[1152]{0:T(1024)S(1)} %broadcast_multiply_fusion, ...), kind=kLoop, calls=%fused_computation.41 | loop fusion | flops 61336448 | bytes 47245312 | tf_op jit(solution)/shard_map/transpose(jvp())/reduce_sum | solution.py:30
  586.8 26.5 %fusion.47 = (bf16[4096]{0:T(1024)(128)(2,1)}, bf16[1152,4096]{1,0:T(8,128)(2,1)S(1)}) fusion(f32[1152,4096]{1,0:T(8,128)} %get-tuple-element.621, f32[1152,4096]{1,0:T(8,128)} %get-tuple-element.652, f32[1152]{0:T(1024)S(1)} %negate_multiply_fusion.4, f32[1152]{0:T(1024)S(1)} %get-tuple-element.635, f32[1152,4096]{1,0:T(8,128)} %get-tuple-element.620, ...), kind=kLoop, calls=%fused_computation.168 | loop fusion | flops 103804928 | bytes 84977664 | tf_op jit(solution)/shard_map/reduce_sum | solution.py:276
  613.3 14.0 convolution_convert_fusion.1
  627.3 14.2 fusion.57
  641.7 11.1 pad_maximum_fusion
  652.9 16.6 %convolution_convert_fusion = bf16[4096,1024]{0,1:T(8,128)(2,1)} fusion(bf16[1152,4096]{1,0:T(8,128)(2,1)} %get-tuple-element.632, bf16[1152,1024]{0,1:T(8,128)(2,1)S(1)} %copy-done.13, pred[1152]{0:T(1024)(128)(4,1)S(1)} %copy-done.28), kind=kOutput, calls=%fused_computation.65 | convolution fusion | flops 9669050368 | bytes 20186240 | tf_op jit(solution)/shard_map/tf,td->fd/dot_general | solution.py:270
  669.5 9.7 pad_maximum_fusion.1
  683.8 6.2 copy.96
  713.3 7.8 multiply_reduce_fusion.6
  721.1 6.0 broadcast_in_dim.193
  727.1 344.2 %while.37 = (s32[]{:T(128)}, f32[1152,3072]{0,1:T(8,128)}, bf16[1152,3072]{0,1:T(8,128)(2,1)}, s32[1152]{0:T(1024)S(1)}, f32[16,1152]{1,0:T(8,128)}, /*index=5*/...) while((s32[]{:T(128)}, f32[1152,3072]{0,1:T(8,128)}, ...), condition=%wide.region_24.26_spmd, body=%wide.region_22.25_spmd.sunk | while | flops 1725603328 | bytes 194861568 | solution.py:152
  730.1 5.5 fusion.121
  738.3 7.8 multiply_reduce_fusion.12
  763.1 5.2 fusion.122
  773.4 5.5 fusion.121
  781.6 7.7 multiply_reduce_fusion.12
  806.4 5.1 fusion.122
  816.4 5.5 fusion.121
  824.7 7.7 multiply_reduce_fusion.12
  849.4 5.1 fusion.122
  859.5 5.5 fusion.121
  867.7 7.7 multiply_reduce_fusion.12
  892.5 5.1 fusion.122
  902.5 5.5 fusion.121
  910.7 7.8 multiply_reduce_fusion.12
  935.3 5.1 fusion.122
  945.3 5.5 fusion.121
  953.5 7.7 multiply_reduce_fusion.12
  988.1 5.5 fusion.121
  996.3 7.8 multiply_reduce_fusion.12
  1020.9 5.1 fusion.122
  1031.0 5.5 fusion.121
  1039.2 7.8 multiply_reduce_fusion.12
  1063.8 5.0 fusion.122
  1071.3 16.1 %convolution_convert_fusion.2 = bf16[1024,3072]{1,0:T(8,128)(2,1)} fusion(f32[1152,3072]{0,1:T(8,128)} %get-tuple-element.413, f32[1024]{0:T(1024)S(1)} %copy-done.73, f32[1024]{0:T(1024)S(1)} %copy-done.54, f32[1152]{0:T(1024)S(1)} %copy-done.51, f32[1152]{0:T(1024)S(1)} %copy-done.26, bf16[1152,1024]{0,1:T(8,128)(2,1)} %copy-done.6, ...), kind=kOutput, calls=%fused_computation.77 | convolution fusion | flops 7262699520 | bytes 22825088 | tf_op jit(solution)/shard_map/td,te->de/dot_general | solution.py:333
  1087.4 15.4 %fusion.56 = (bf16[1024]{0:T(1024)(128)(2,1)S(1)}, f32[1152,1024]{1,0:T(8,128)}) fusion(bf16[1024,3072]{1,0:T(8,128)(2,1)} %all-gather.8.cloned.1.call-done, f32[1152,3072]{0,1:T(8,128)} %get-tuple-element.413), kind=kOutput, calls=%fused_computation.176 | convolution fusion | flops 7252474880 | bytes 25167872 | tf_op jit(solution)/shard_map/te,de->td/dot_general | solution.py:337
  1102.9 6.3 copy.99
  1122.2 5.8 convert_reduce_fusion.1
  1128.1 54.7 %all-reduce.23 = (bf16[1024]{0:T(1024)(128)(2,1)S(1)}, bf16[1024]{0:T(1024)(128)(2,1)S(1)}, bf16[1024]{0:T(1024)(128)(2,1)S(1)}, bf16[1024]{0:T(1024)(128)(2,1)S...) all-reduce(bf16[1024]{0:T(1024)(128)(2,1)} %dynamic-update-slice.10, ...), channel_id=1, replica_groups=mesh['replica'=8,'fsdp'=16] {'fsdp'}, use_global_device_ids=true, to_apply=%add.10 | all-reduce | flops 18448 | bytes 73792
  1182.8 18.0 %add_convert_fusion.5 = bf16[1152,1024]{0,1:T(8,128)(2,1)} fusion(f32[1152,1024]{0,1:T(8,128)} %copy-done.4, bf16[1152,4096]{1,0:T(8,128)(2,1)} %get-tuple-element.632, bf16[4096,1024]{1,0:T(8,128)(2,1)} %all-gather.14.cloned.1.call-done, f32[1024]{0:T(1024)S(1)} %convert_element_type.311), kind=kOutput, calls=%fused_computation.94 | convolution fusion | flops 9667215360 | bytes 24907776 | tf_op jit(solution)/shard_map/dot_general | solution.py:262
  1210.0 8.7 gather_fusion.2
  1222.6 5.4 reshape.530
  1228.0 8.2 all-to-all-start.3
  1239.2 49.9 %all-to-all-done.3 = bf16[128,9,1024]{2,1,0:T(8,128)(2,1)} async-done(((bf16[128,9,1024]{2,1,0:T(8,128)(2,1)}), bf16[128,9,1024]{2,1,0:T(8,128)(2,1)}, u32[]{:S(2)}, u32[]{:S(2)}) %all-to-all-start.3) | async-done | bytes 2359328 | tf_op jit(solution)/shard_map/all_to_all | solution.py:392
  1289.0 5.8 all-to-all-start.1
  1316.8 36.3 %all-to-all-done.1 = bf16[128,9,1024]{2,1,0:T(8,128)(2,1)} async-done(((bf16[128,9,1024]{2,1,0:T(8,128)(2,1)}), bf16[128,9,1024]{2,1,0:T(8,128)(2,1)}, u32[]{:S(2)}, u32[]{:S(2)}) %all-to-all-start.1) | async-done | bytes 2359328 | tf_op jit(solution)/shard_map/all_to_all | solution.py:385
  1368.3 29.2 %all-reduce.25 = (bf16[64]{0:T(256)(128)(2,1)S(1)}, bf16[64]{0:T(256)(128)(2,1)S(1)}, bf16[64]{0:T(256)(128)(2,1)S(1)}, bf16[64]{0:T(256)(128)(2,1)S(1)}, bf16[1...) all-reduce(bf16[64]{0:T(256)(128)(2,1)S(1)} %dynamic-slice.12, ...), channel_id=1, replica_groups=mesh['replica'=8,'fsdp'=16] {'replica'}, use_global_device_ids=true, to_apply=%region_29.31 | all-reduce | flops 1409 | bytes 5636 | tf_op jit(solution)/shard_map/psum | solution.py:373
  1404.9 24.9 %all-reduce.29.cloned.1.call-done = (bf16[256,1024]{0,1:T(8,128)(2,1)}, bf16[64,3072]{1,0:T(8,128)(2,1)}, bf16[64,1024]{1,0:T(8,128)(2,1)}, bf16[64,4096]{1,0:T(8,128)(2,1)}) async-done(((bf16[256,1024]{0,1:T(8,128)(2,1)}, bf16[64,3072]{1,0:T(8,128)(2,1)}, bf16[64,1024]{1,0:T(8,128)(2,1)}, bf16[64,4096]{1,0:T(8,128)(2,1)}), (bf16[256,1024]{0,1:T(8,128)(2,1)}, bf16[64,3072]{1,0:T(8,128)(2,1)}, ...) | async-done | bytes 1572880 | tf_op jit(solution)/shard_map/psum | solution.py:317
  (692 shorter events, 521.8 us)
Async XLA Ops:
  7.2 298.0 %all-gather.8.cloned.1.call-start = ((), (), s32[]{:S(2)}) async-start(), calls=%async_computation.8 | async-start | bytes 6684672 | tf_op jit(solution)/shard_map/all_gather | solution.py:210
  7.9 464.6 %all-gather.10.cloned.1.call-start = ((), (), s32[]{:S(2)}) async-start(), calls=%async_computation.9 | async-start | bytes 2228224 | tf_op jit(solution)/shard_map/all_gather | solution.py:214
  8.7 479.9 %all-gather.12.cloned.1.call-start = ((), (), s32[]{:S(2)}) async-start(), calls=%async_computation.10 | async-start | bytes 8912896 | tf_op jit(solution)/shard_map/all_gather | solution.py:242
  15.2 14.0 copy-start.46
  20.2 9.0 copy-start.15
  38.4 11.5 copy-start.16
  38.4 64.2 %all-to-all-start = ((bf16[128,9,1024]{2,1,0:T(8,128)(2,1)}), bf16[128,9,1024]{2,1,0:T(8,128)(2,1)}, u32[]{:S(2)}, u32[]{:S(2)}) async-start(bf16[128,9,1024]{2,1,0:T(8,128)(2,1)} %reshape.524), calls=%async_computation | async-start | bytes 8388608 | tf_op jit(solution)/shard_map/all_to_all | solution.py:189
  52.7 58.1 %copy-start.74 = (u32[128]{0:T(128)S(1)}, u32[128]{0:T(128)}, u32[]{:S(2)}) copy-start(u32[128]{0:T(128)} %constant.631) | copy-start | bytes 1540
  52.7 59.3 %copy-start.75 = (bf16[64]{0:T(256)(128)(2,1)S(1)}, bf16[64]{0:T(256)(128)(2,1)}, u32[]{:S(2)}) copy-start(bf16[64]{0:T(256)(128)(2,1)} %param.41) | copy-start | bytes 388
  52.7 59.6 %copy-start.76 = (bf16[64]{0:T(256)(128)(2,1)S(1)}, bf16[64]{0:T(256)(128)(2,1)}, u32[]{:S(2)}) copy-start(bf16[64]{0:T(256)(128)(2,1)} %param.38) | copy-start | bytes 388
  52.7 59.8 %copy-start.77 = (bf16[64]{0:T(256)(128)(2,1)S(1)}, bf16[64]{0:T(256)(128)(2,1)}, u32[]{:S(2)}) copy-start(bf16[64]{0:T(256)(128)(2,1)} %param.37) | copy-start | bytes 388
  52.8 60.0 %copy-start.78 = (bf16[64]{0:T(256)(128)(2,1)S(1)}, bf16[64]{0:T(256)(128)(2,1)}, u32[]{:S(2)}) copy-start(bf16[64]{0:T(256)(128)(2,1)} %param.35) | copy-start | bytes 388
  52.8 60.3 %copy-start.79 = (bf16[64]{0:T(256)(128)(2,1)S(1)}, bf16[64]{0:T(256)(128)(2,1)}, u32[]{:S(2)}) copy-start(bf16[64]{0:T(256)(128)(2,1)} %param.34) | copy-start | bytes 388
  52.8 60.5 %copy-start.80 = (bf16[64]{0:T(256)(128)(2,1)S(1)}, bf16[64]{0:T(256)(128)(2,1)}, u32[]{:S(2)}) copy-start(bf16[64]{0:T(256)(128)(2,1)} %param.43) | copy-start | bytes 388
  52.8 60.7 %copy-start.81 = (bf16[64]{0:T(256)(128)(2,1)S(1)}, bf16[64]{0:T(256)(128)(2,1)}, u32[]{:S(2)}) copy-start(bf16[64]{0:T(256)(128)(2,1)} %param.42) | copy-start | bytes 388
  52.8 60.9 %copy-start.82 = (bf16[64]{0:T(256)(128)(2,1)S(1)}, bf16[64]{0:T(256)(128)(2,1)}, u32[]{:S(2)}) copy-start(bf16[64]{0:T(256)(128)(2,1)} %param.45) | copy-start | bytes 388
  52.8 61.2 %copy-start.83 = (bf16[64]{0:T(256)(128)(2,1)S(1)}, bf16[64]{0:T(256)(128)(2,1)}, u32[]{:S(2)}) copy-start(bf16[64]{0:T(256)(128)(2,1)} %param.44) | copy-start | bytes 388
  52.8 156.5 %copy-start.84 = (bf16[256]{0:T(256)(128)(2,1)S(1)}, bf16[256]{0:T(256)(128)(2,1)}, u32[]{:S(2)}) copy-start(bf16[256]{0:T(256)(128)(2,1)} %param.47) | copy-start | bytes 1540
  52.8 174.9 %copy-start.85 = (bf16[256]{0:T(256)(128)(2,1)S(1)}, bf16[256]{0:T(256)(128)(2,1)}, u32[]{:S(2)}) copy-start(bf16[256]{0:T(256)(128)(2,1)} %param.48) | copy-start | bytes 1540
  52.8 194.0 %copy-start.86 = (bf16[256]{0:T(256)(128)(2,1)S(1)}, bf16[256]{0:T(256)(128)(2,1)}, u32[]{:S(2)}) copy-start(bf16[256]{0:T(256)(128)(2,1)} %param.49) | copy-start | bytes 1540
  52.9 211.1 %copy-start.67 = (s32[1152]{0:T(1024)S(1)}, s32[1152]{0:T(1024)}, u32[]{:S(2)}) copy-start(s32[1152]{0:T(1024)} %param.32) | copy-start | bytes 13828
  52.9 221.2 %copy-start.68 = (s32[1,3]{1,0:T(1,128)S(1)}, s32[1,3]{1,0:T(1,128)}, u32[]{:S(2)}) copy-start(s32[1,3]{1,0:T(1,128)} %param.31) | copy-start | bytes 40
  102.7 188.9 %all-to-all-start.2 = ((bf16[128,9,1024]{2,1,0:T(8,128)(2,1)}), bf16[128,9,1024]{2,1,0:T(8,128)(2,1)}, u32[]{:S(2)}, u32[]{:S(2)}) async-start(bf16[128,9,1024]{2,1,0:T(8,128)(2,1)} %reshape.528), calls=%async_computation.2 | async-start | bytes 8388608 | tf_op jit(solution)/shard_map/all_to_all | solution.py:196
  110.1 434.5 %all-gather.14.cloned.1.call-start = ((), (), s32[]{:S(2)}) async-start(), calls=%async_computation.11 | async-start | bytes 8912896 | tf_op jit(solution)/shard_map/all_gather | solution.py:246
  115.0 1186.6 %reduce-scatter.9.cloned.1.call-start = ((), (), s32[]{:S(2)}) async-start(), calls=%async_computation.14 | async-start | bytes 9191424 | tf_op jit(solution)/shard_map/reduce_scatter | solution.py:18
  209.1 96.1 %copy-start.72 = (f32[1024]{0:T(1024)}, f32[1024]{0:T(1024)S(1)}, u32[]{:S(2)}) copy-start(f32[1024]{0:T(1024)S(1)} %convert_element_type.291) | copy-start | bytes 12292
  209.2 96.0 %copy-start.53 = (f32[1024]{0:T(1024)}, f32[1024]{0:T(1024)S(1)}, u32[]{:S(2)}) copy-start(f32[1024]{0:T(1024)S(1)} %convert_element_type.290) | copy-start | bytes 12292
  209.3 263.2 %copy-start.69 = (f32[1024]{0:T(1024)}, f32[1024]{0:T(1024)S(1)}, u32[]{:S(2)}) copy-start(f32[1024]{0:T(1024)S(1)} %mul.433) | copy-start | bytes 12292
  277.3 202.6 %copy-start.27 = (pred[1152]{0:T(1024)(128)(4,1)}, pred[1152]{0:T(1024)(128)(4,1)S(1)}, u32[]{:S(2)}) copy-start(pred[1152]{0:T(1024)(128)(4,1)S(1)} %compare_and_fusion.4) | copy-start | bytes 3460
  290.1 15.1 %copy-start.25 = (f32[1152]{0:T(1024)}, f32[1152]{0:T(1024)S(1)}, u32[]{:S(2)}) copy-start(f32[1152]{0:T(1024)S(1)} %broadcast_multiply_fusion.3) | copy-start | bytes 13828
  291.6 13.6 copy-start.50
  488.6 56.1 %copy-start.13 = (bf16[1152,1024]{0,1:T(8,128)(2,1)S(1)}, bf16[1152,1024]{0,1:T(8,128)(2,1)}, u32[]{:S(2)}) copy-start(bf16[1152,1024]{0,1:T(8,128)(2,1)} %copy.95) | copy-start | bytes 7077892
  488.6 56.1 %copy-start.28 = (pred[1152]{0:T(1024)(128)(4,1)S(1)}, pred[1152]{0:T(1024)(128)(4,1)}, u32[]{:S(2)}) copy-start(pred[1152]{0:T(1024)(128)(4,1)} %copy-done.27) | copy-start | bytes 3460
  488.6 56.1 %copy-start.30 = (f32[16,1,256]{2,1,0:T(1,128)S(1)}, f32[16,1,256]{2,1,0:T(1,128)}, u32[]{:S(2)}) copy-start(f32[16,1,256]{2,1,0:T(1,128)} %convert_element_type.354) | copy-start | bytes 49156
  544.7 22.2 %copy-start.52 = (f32[16,1,256]{2,1,0:T(1,128)S(1)}, f32[16,1,256]{2,1,0:T(1,128)}, u32[]{:S(2)}) copy-start(f32[16,1,256]{2,1,0:T(1,128)} %convert_element_type.355) | copy-start | bytes 49156
  566.9 46.4 %slice-start.3 = ((s8[4718592]{0:T(1024)(128)(4,1)}), s8[4194304]{0:T(1024)(128)(4,1)S(1)}, s32[]{:S(2)}) async-start(s8[4718592]{0:T(1024)(128)(4,1)} %bitcast.102), calls=%async_computation.20 | async-start | bytes 8388608
  586.8 26.5 %slice-start.4 = ((s8[4718592]{0:T(1024)(128)(4,1)}), s8[524288]{0:T(1024)(128)(4,1)S(1)}, s32[]{:S(2)}) async-start(s8[4718592]{0:T(1024)(128)(4,1)} %bitcast.102), calls=%async_computation.21 | async-start | bytes 1048576
  586.8 26.5 %copy-start.23 = (f32[1152]{0:T(1024)S(1)}, f32[1152]{0:T(1024)}, u32[]{:S(2)}) copy-start(f32[1152]{0:T(1024)} %copy-done.22) | copy-start | bytes 13828
  586.8 26.5 %copy-start.34 = (f32[1152]{0:T(1024)S(1)}, f32[1152]{0:T(1024)}, u32[]{:S(2)}) copy-start(f32[1152]{0:T(1024)} %copy-done.33) | copy-start | bytes 13828
  586.8 26.5 %copy-start.38 = (f32[1024]{0:T(1024)S(1)}, f32[1024]{0:T(1024)}, u32[]{:S(2)}) copy-start(f32[1024]{0:T(1024)} %convert_element_type.304) | copy-start | bytes 12292
  586.8 26.5 %copy-start.59 = (f32[1024]{0:T(1024)S(1)}, f32[1024]{0:T(1024)}, u32[]{:S(2)}) copy-start(f32[1024]{0:T(1024)} %convert_element_type.305) | copy-start | bytes 12292
  652.8 650.8 %reduce-scatter.11.cloned.1.call-start = ((), (), s32[]{:S(2)}) async-start(), calls=%async_computation.15 | async-start | bytes 8982528 | tf_op jit(solution)/shard_map/reduce_scatter | solution.py:18
  679.2 626.3 %reduce-scatter.7.cloned.1.call-start = ((), (), s32[]{:S(2)}) async-start(), calls=%async_computation.13 | async-start | bytes 2228224 | tf_op jit(solution)/shard_map/reduce_scatter | solution.py:359
  683.8 11.0 slice-start.5
  690.0 9.5 slice-start.7
  713.2 592.4 %reduce-scatter.5.cloned.1.call-start = ((), (), s32[]{:S(2)}) async-start(), calls=%async_computation.12 | async-start | bytes 6684672 | tf_op jit(solution)/shard_map/reduce_scatter | solution.py:347
  727.0 344.2 %copy-start.26 = (f32[1152]{0:T(1024)S(1)}, f32[1152]{0:T(1024)}, u32[]{:S(2)}) copy-start(f32[1152]{0:T(1024)} %copy-done.25) | copy-start | bytes 13828
  727.0 344.2 %copy-start.29 = (pred[1152]{0:T(1024)(128)(4,1)S(1)}, pred[1152]{0:T(1024)(128)(4,1)}, u32[]{:S(2)}) copy-start(pred[1152]{0:T(1024)(128)(4,1)} %copy-done.27) | copy-start | bytes 3460
  727.0 344.2 %copy-start.51 = (f32[1152]{0:T(1024)S(1)}, f32[1152]{0:T(1024)}, u32[]{:S(2)}) copy-start(f32[1152]{0:T(1024)} %copy-done.50) | copy-start | bytes 13828
  727.0 344.2 %copy-start.54 = (f32[1024]{0:T(1024)S(1)}, f32[1024]{0:T(1024)}, u32[]{:S(2)}) copy-start(f32[1024]{0:T(1024)} %copy-done.53) | copy-start | bytes 12292
  727.0 344.2 %copy-start.73 = (f32[1024]{0:T(1024)S(1)}, f32[1024]{0:T(1024)}, u32[]{:S(2)}) copy-start(f32[1024]{0:T(1024)} %copy-done.72) | copy-start | bytes 12292
  737.7 8.4 slice-start
  910.1 8.4 slice-start
  995.7 8.4 slice-start
  1038.5 8.4 slice-start
  1102.8 9.9 copy-start.41
  1102.8 12.8 slice-start.9
  1210.0 8.7 copy-start.14
  1210.0 8.7 copy-start.61
  1228.0 61.0 %all-to-all-start.3 = ((bf16[128,9,1024]{2,1,0:T(8,128)(2,1)}), bf16[128,9,1024]{2,1,0:T(8,128)(2,1)}, u32[]{:S(2)}, u32[]{:S(2)}) async-start(bf16[128,9,1024]{2,1,0:T(8,128)(2,1)} %reshape.530), calls=%async_computation.3 | async-start | bytes 8388608 | tf_op jit(solution)/shard_map/all_to_all | solution.py:392
  1239.2 56.0 %copy-start.47 = (s32[1152]{0:T(1024)S(1)}, s32[1152]{0:T(1024)}, u32[]{:S(2)}) copy-start(s32[1152]{0:T(1024)} %copy-done.46) | copy-start | bytes 13828
  1289.0 64.2 %all-to-all-start.1 = ((bf16[128,9,1024]{2,1,0:T(8,128)(2,1)}), bf16[128,9,1024]{2,1,0:T(8,128)(2,1)}, u32[]{:S(2)}, u32[]{:S(2)}) async-start(bf16[128,9,1024]{2,1,0:T(8,128)(2,1)} %reshape.526), calls=%async_computation.1 | async-start | bytes 8388608 | tf_op jit(solution)/shard_map/all_to_all | solution.py:385
  1294.9 134.9 %all-reduce.29.cloned.1.call-start = ((), (), s32[]{:S(2)}) async-start(), calls=%async_computation.16 | async-start | bytes 3145728 | tf_op jit(solution)/shard_map/psum | solution.py:317
  1362.3 75.3 %copy-start.1 = (bf16[1152,1024]{1,0:T(8,128)(2,1)S(1)}, bf16[1152,1024]{1,0:T(8,128)(2,1)}, u32[]{:S(2)}) copy-start(bf16[1152,1024]{1,0:T(8,128)(2,1)} %param.30) | copy-start | bytes 7077892
  (85 other events, 414.9 us)
Sparse Core Ops, SparseCore 0:
  9.7 90.5 all-gather.7
  102.0 77.2 all-gather.9
  181.0 53.5 all-gather.11
  236.2 53.1 all-gather.13
  652.9 75.3 reduce-scatter.8
  730.8 73.5 reduce-scatter.10
  806.9 61.9 reduce-scatter.6
  1087.6 70.9 reduce-scatter.4
  1305.7 124.0 all-reduce.28

commit v2 on v0

v2 whole, which is shorter than its diff:
```python
import jax
import jax.numpy as jnp
from jax import lax
from jax.experimental import pallas as pl
from jax.experimental.pallas import tpu as pltpu
from jax.sharding import PartitionSpec as P

f32 = jnp.float32
bf16 = jnp.bfloat16
H = 16
HD = 64
EPS = 1e-5
NEG = -1000000000.0
NT = (((1,), (1,)), ((), ()))
NN = (((1,), (0,)), ((), ()))
TN = (((0,), (0,)), ((), ()))


def dot(a, b, dn=NN):
    return lax.dot_general(a, b, dn, preferred_element_type=f32)

def rank_row(kcol,krow):
    return jnp.sum((kcol<krow).astype(f32),axis=0,keepdims=True).astype(jnp.int32)
def rank_col(krow,kcol):
    return jnp.sum((krow<kcol).astype(f32),axis=1,keepdims=True).astype(jnp.int32)

def send_kernel(krow_ref,kcol_ref,x_ref,out_ref,rank_ref,wide_ref):
    i=pl.program_id(0); bs=out_ref.shape[0]//8
    @pl.when(i==0)
    def _(): rank_ref[...]=rank_row(kcol_ref[...],krow_ref[...])
    t=rank_ref.shape[1]
    pick=(lax.broadcasted_iota(jnp.int32,(bs,t),0)+i*bs==rank_ref[...]).astype(f32).astype(bf16)
    rows=dot(pick,x_ref[...])
    for k in range(8):
        wide_ref[pl.ds(k,bs,stride=8),:]=rows[:,128*k:128*k+128]
    out_ref[...]=wide_ref[...].astype(bf16)

def send_rows(x,keys,blocks=3):
    t,d=x.shape; bs=t//blocks
    full=lambda s:pl.BlockSpec(s,lambda i:(0,0))
    return pl.pallas_call(send_kernel,grid=(blocks,),
        in_specs=[full((1,t)),full((t,1)),full((t,d))],
        out_specs=pl.BlockSpec((bs*8,128),lambda i:(i,0)),
        out_shape=jax.ShapeDtypeStruct((t*8,128),bf16),
        scratch_shapes=[pltpu.VMEM((1,t),jnp.int32),pltpu.VMEM((bs*8,128),f32)],
        compiler_params=pltpu.CompilerParams(vmem_limit_bytes=40<<20),name="send_rows")(keys.reshape(1,t),keys.reshape(t,1),x)

def unpack_rows(got_ref,wide_ref,rows_ref,chunk=384):
    t=rows_ref.shape[0]
    for c in range(0,t,chunk):
        wide_ref[...]=got_ref[8*c:8*(c+chunk),:].astype(f32)
        for k in range(8):
            rows_ref[c:c+chunk,128*k:128*k+128]=wide_ref[pl.ds(k,chunk,stride=8),:].astype(bf16)

def recv_kernel(krow_ref,kcol_ref,got_ref,out_ref,wide_ref,rows_ref):
    i=pl.program_id(0); bs=out_ref.shape[0]
    @pl.when(i==0)
    def _(): unpack_rows(got_ref,wide_ref,rows_ref)
    t=rows_ref.shape[0]
    rank=rank_col(krow_ref[...],kcol_ref[...])
    pick=(lax.broadcasted_iota(jnp.int32,(bs,t),1)==rank).astype(f32).astype(bf16)
    out_ref[...]=dot(pick,rows_ref[...]).astype(bf16)

def recv_rows(got,keys,blocks=3):
    t=got.shape[0]//8; d=1024; bs=t//blocks
    full=lambda s:pl.BlockSpec(s,lambda i:(0,0))
    return pl.pallas_call(recv_kernel,grid=(blocks,),
        in_specs=[full((1,t)),pl.BlockSpec((bs,1),lambda i:(i,0)),full((t*8,128))],
        out_specs=pl.BlockSpec((bs,d),lambda i:(i,0)),
        out_shape=jax.ShapeDtypeStruct((t,d),bf16),
        scratch_shapes=[pltpu.VMEM((384*8,128),f32),pltpu.VMEM((t,d),bf16)],
        compiler_params=pltpu.CompilerParams(vmem_limit_bytes=40<<20),name="recv_rows")(keys.reshape(1,t),keys.reshape(t,1),got)

def norm_parts(v):
    m=jnp.mean(v,axis=-1,keepdims=True); c=v-m
    r=lax.rsqrt(jnp.mean(c*c,axis=-1,keepdims=True)+EPS)
    return c*r,r
def norm_back(e,g,vhat,r):
    eg=e*g
    return r*(eg-jnp.mean(eg,axis=-1,keepdims=True)-vhat*jnp.mean(eg*vhat,axis=-1,keepdims=True))
def colsum(v): return jnp.sum(v,axis=0,keepdims=True)

def qkv_kernel(krow_ref,kcol_ref,got_ref,vec_ref,w_ref,x_ref,a_ref,proj_ref,wide_ref,rows_ref):
    i=pl.program_id(0); bs=x_ref.shape[0]
    @pl.when(i==0)
    def _(): unpack_rows(got_ref,wide_ref,rows_ref)
    t=rows_ref.shape[0]
    rank=rank_col(krow_ref[...],kcol_ref[...])
    pick=(lax.broadcasted_iota(jnp.int32,(bs,t),1)==rank).astype(f32).astype(bf16)
    x=dot(pick,rows_ref[...])
    x_ref[...]=x.astype(bf16)
    xhat,_=norm_parts(x)
    a=(xhat*vec_ref[0:1,:]+vec_ref[1:2,:]).astype(bf16)
    a_ref[...]=a
    for j in range(3):
        w=w_ref[:,64*j:64*j+64,:].reshape(1024,1024)
        pj=dot(a,w)
        if j==0: pj=pj+vec_ref[2:3,:]
        if j==2: pj=pj+vec_ref[3:4,:]
        proj_ref[:,1024*j:1024*j+1024]=pj.astype(bf16)

def recv_qkv(got,keys,vec,pack1,blocks=3):
    t=got.shape[0]//8; d=1024; bs=t//blocks
    full=lambda s:pl.BlockSpec(s,lambda i:(0,)*len(s))
    return pl.pallas_call(qkv_kernel,grid=(blocks,),
        in_specs=[full((1,t)),pl.BlockSpec((bs,1),lambda i:(i,0)),full((t*8,128)),full(vec.shape),
                  pl.BlockSpec((16,192,1024),lambda i:(0,0,0),pipeline_mode=pl.Buffered(1))],
        out_specs=[pl.BlockSpec((bs,d),lambda i:(i,0)),pl.BlockSpec((bs,d),lambda i:(i,0)),pl.BlockSpec((bs,3*d),lambda i:(i,0))],
        out_shape=[jax.ShapeDtypeStruct((t,d),bf16),jax.ShapeDtypeStruct((t,d),bf16),jax.ShapeDtypeStruct((t,3*d),bf16)],
        scratch_shapes=[pltpu.VMEM((384*8,128),f32),pltpu.VMEM((t,d),bf16)],
        compiler_params=pltpu.CompilerParams(vmem_limit_bytes=48<<20),name="recv_qkv")(keys.reshape(1,t),keys.reshape(t,1),got,vec,pack1)

RT2=0.7071067811865476; RPI=0.3989422804014327
def mid_kernel(c_ref,o_ref,x_ref,dy_ref,vec_ref,vff_ref,w_ref,
               y_ref,a2_ref,n_ref,du_ref,dz_ref,do_ref,dres_ref,gd_ref,gf_ref,g_s,gp_s,e_s,nc=1024):
    i=pl.program_id(0)
    ff=4096
    @pl.when(i==0)
    def _():
        gd_ref[...]=jnp.zeros_like(gd_ref); gf_ref[...]=jnp.zeros_like(gf_ref)
    vec=lambda k:vec_ref[k:k+1,:]
    w_out=w_ref[:,0:64,:].reshape(1024,1024)
    w1=lambda j:w_ref[:,64+64*j:128+64*j,:].reshape(1024,1024)
    w2=lambda j:w_ref[4*j:4*j+4,320:576,:].reshape(1024,1024)
    z=dot(c_ref[...],w_out)+vec(4)
    zhat,rz=norm_parts(z)
    hres=x_ref[...].astype(f32)+zhat*vec(5)+vec(6)
    hhat,rh=norm_parts(hres)
    a2=(hhat*vec(7)+vec(8)).astype(bf16)
    a2_ref[...]=a2
    tot=0.0
    for j in range(4):
        cols=slice(1024*j,1024*j+1024)
        u=dot(a2,w1(j))+vff_ref[0:1,cols]
        phi=0.5*(1.0+lax.erf(u*RT2))
        g=u*phi
        gp_s[:,cols]=(phi+u*(RPI*jnp.exp(-0.5*u*u))).astype(gp_s.dtype)
        g_s[:,cols]=g
        tot=tot+jnp.sum(g,axis=-1,keepdims=True)
    mean=tot*(1.0/ff)
    var=0.0
    for j in range(4):
        cols=slice(1024*j,1024*j+1024)
        cen=g_s[:,cols]-mean
        var=var+jnp.sum(cen*cen,axis=-1,keepdims=True)
    rf=lax.rsqrt(var*(1.0/ff)+EPS)
    y=hres+vec(9)
    dy=dy_ref[...]
    s1=0.0; s2=0.0
    for j in range(4):
        cols=slice(1024*j,1024*j+1024)
        vhat=(g_s[:,cols]-mean)*rf
        g_s[:,cols]=vhat
        n=(vhat*vff_ref[1:2,cols]+vff_ref[2:3,cols]).astype(bf16)
        n_ref[:,cols]=n
        y=y+dot(n,w2(j))
        dn=dot(dy,w2(j),NT)
        gf_ref[0:1,cols]+=colsum(dn*vhat)
        gf_ref[1:2,cols]+=colsum(dn)
        e=dn*vff_ref[1:2,cols]
        e_s[:,cols]=e
        s1=s1+jnp.sum(e,axis=-1,keepdims=True)
        s2=s2+jnp.sum(e*vhat,axis=-1,keepdims=True)
    y_ref[...]=y.astype(bf16)
    s1=s1*(1.0/ff); s2=s2*(1.0/ff)
    da2=0.0
    for j in range(4):
        cols=slice(1024*j,1024*j+1024)
        du=(gp_s[:,cols].astype(f32)*(rf*(e_s[:,cols]-s1-g_s[:,cols]*s2))).astype(bf16)
        du_ref[:,cols]=du
        gf_ref[2:3,cols]+=colsum(du.astype(f32))
        da2=da2+dot(du,w1(j),NT)
    dyf=dy.astype(f32)
    gd_ref[0:1,:]+=colsum(dyf)
    gd_ref[1:2,:]+=colsum(da2*hhat)
    gd_ref[2:3,:]+=colsum(da2)
    dres=dyf+norm_back(da2,vec(7),hhat,rh)
    dres_ref[...]=dres
    gd_ref[3:4,:]+=colsum(dres*zhat)
    gd_ref[4:5,:]+=colsum(dres)
    dz=norm_back(dres,vec(5),zhat,rz).astype(bf16)
    dz_ref[...]=dz
    gd_ref[5:6,:]+=colsum(dz.astype(f32))
    dc=dot(dz,w_out,NT)
    gd_ref[6:7,:]+=colsum(dc*o_ref[...])
    do_ref[...]=(dc*vec(10)).astype(bf16)

def mid(c,o,x,dy,vec,vff,pack2,bm=192):
    t,d=c.shape; ff=4096
    row=lambda n:pl.BlockSpec((bm,n),lambda i:(i,0))
    full=lambda s,**k:pl.BlockSpec(s,lambda i:(0,)*len(s),**k)
    sd=jax.ShapeDtypeStruct
    return pl.pallas_call(mid_kernel,grid=(t//bm,),
        in_specs=[row(d),row(d),row(d),row(d),full(vec.shape),full(vff.shape),full(pack2.shape,pipeline_mode=pl.Buffered(1))],
        out_specs=[row(d),row(d),row(ff),row(ff),row(d),row(d),row(d),full((8,d)),full((8,ff))],
        out_shape=[sd((t,d),bf16),sd((t,d),bf16),sd((t,ff),bf16),sd((t,ff),bf16),sd((t,d),bf16),sd((t,d),bf16),sd((t,d),f32),sd((8,d),f32),sd((8,ff),f32)],
        scratch_shapes=[pltpu.VMEM((bm,ff),f32),pltpu.VMEM((bm,ff),bf16),pltpu.VMEM((bm,ff),f32)],
        compiler_params=pltpu.CompilerParams(vmem_limit_bytes=60<<20),name="mid_rows")(c,o,x,dy,vec,vff,pack2)

def dx_kernel(dq_ref,dk_ref,dv_ref,x_ref,dres_ref,vec_ref,w_ref,dx_ref,g_ref):
    i=pl.program_id(0)
    @pl.when(i==0)
    def _(): g_ref[...]=jnp.zeros_like(g_ref)
    da=0.0
    for j,r in enumerate((dq_ref,dk_ref,dv_ref)):
        da=da+dot(r[...],w_ref[:,64*j:64*j+64,:].reshape(1024,1024),NT)
    xhat,r=norm_parts(x_ref[...].astype(f32))
    g_ref[0:1,:]+=colsum(da*xhat)
    g_ref[1:2,:]+=colsum(da)
    dx_ref[...]=(dres_ref[...]+norm_back(da,vec_ref[0:1,:],xhat,r)).astype(bf16)

def dx_rows(dq,dk,dv,x,dres,vec,pack1,blocks=3):
    t,d=x.shape; bs=t//blocks
    row=pl.BlockSpec((bs,d),lambda i:(i,0))
    full=lambda s,**k:pl.BlockSpec(s,lambda i:(0,)*len(s),**k)
    return pl.pallas_call(dx_kernel,grid=(blocks,),
        in_specs=[row,row,row,row,row,full(vec.shape),full((16,192,1024),pipeline_mode=pl.Buffered(1))],
        out_specs=[row,full((8,d))],
        out_shape=[jax.ShapeDtypeStruct((t,d),bf16),jax.ShapeDtypeStruct((8,d),f32)],
        compiler_params=pltpu.CompilerParams(vmem_limit_bytes=48<<20),name="dx_rows")(dq,dk,dv,x,dres,vec,pack1)

def grad2_kernel(c_ref,dz_ref,a2_ref,du_ref,n_ref,dy_ref,out_ref):
    def put(res,at):
        for f in range(4):
            out_ref[f,at:at+64,:]=res[64*f:64*f+64,:].astype(bf16)
    put(dot(c_ref[...],dz_ref[...],TN),0)
    for j in range(4):
        put(dot(a2_ref[...],du_ref[:,1024*j:1024*j+1024],TN),64+64*j)
    res=dot(n_ref[...],dy_ref[...],TN)
    for f in range(4):
        out_ref[f,320:576,:]=res[256*f:256*f+256,:].astype(bf16)

def grad2(c,dz,a2,du,n,dy):
    t,d=c.shape
    col=lambda n:pl.BlockSpec((t,n),lambda i:(0,i))
    full=lambda s:pl.BlockSpec(s,lambda i:(0,0),pipeline_mode=pl.Buffered(1))
    return pl.pallas_call(grad2_kernel,grid=(4,),
        in_specs=[col(256),full((t,d)),col(256),full((t,4096)),col(1024),full((t,d))],
        out_specs=pl.BlockSpec((4,576,1024),lambda i:(i,0,0)),
        out_shape=jax.ShapeDtypeStruct((16,576,1024),bf16),
        compiler_params=pltpu.CompilerParams(vmem_limit_bytes=56<<20),name="grad_ffn_out")(c,dz,a2,du,n,dy)

def grad1_kernel(a_ref,dq_ref,dk_ref,dv_ref,small_ref,out_ref):
    for j,r in enumerate((dq_ref,dk_ref,dv_ref)):
        res=dot(a_ref[...],r[...],TN)
        for f in range(4):
            out_ref[f,64*j:64*j+64,:]=res[64*f:64*f+64,:].astype(bf16)
    out_ref[:,192:200,:]=small_ref[...].astype(bf16)

def grad1(a,dq,dk,dv,small):
    t,d=a.shape
    full=pl.BlockSpec((t,d),lambda i:(0,0),pipeline_mode=pl.Buffered(1))
    return pl.pallas_call(grad1_kernel,grid=(4,),
        in_specs=[pl.BlockSpec((t,256),lambda i:(0,i)),full,full,full,pl.BlockSpec((4,8,1024),lambda i:(i,0,0))],
        out_specs=pl.BlockSpec((4,200,1024),lambda i:(i,0,0)),
        out_shape=jax.ShapeDtypeStruct((16,200,1024),bf16),
        compiler_params=pltpu.CompilerParams(vmem_limit_bytes=48<<20),name="grad_qkv")(a,dq,dk,dv,small)

T=1152; D=1024
BLOCKS=[(0,256),(256,256),(512,256),(768,256),(1024,128)]


def masked_scores(sT, start_row, q0, bq):
    keys=q0+bq
    kio=lax.broadcasted_iota(jnp.int32,(128,bq),0)
    qio=lax.broadcasted_iota(jnp.int32,(1,bq),1)+q0
    parts=[]
    for k0 in range(0,keys,128):
        t=sT[k0:k0+128]
        ok=None
        if k0==0 or q0>=1024:
            ok=kio>=start_row-k0
        if k0+127>q0:
            low=kio<=qio-k0
            ok=low if ok is None else ok&low
        parts.append(t if ok is None else jnp.where(ok,t,NEG))
    return jnp.concatenate(parts,axis=0) if len(parts)>1 else parts[0]

def fwd_kernel(start_ref,hs_ref,q_ref,k_ref,v_ref,o_ref,c_ref,lse_ref):
    lane=lax.broadcasted_iota(jnp.int32,(1,128),1)
    vT=v_ref[...].T
    oT=[]
    for q0,bq in BLOCKS:
        keys=q0+bq
        k=k_ref[0:keys,:]
        qb=q_ref[q0:q0+bq,:]*jnp.asarray(HD**-0.5,bf16)
        start=start_ref[0:1,q0:q0+bq]
        halves=[]
        for h in range(2):
            qh=jnp.where((lane>=64*h)&(lane<64*h+64),qb,jnp.zeros_like(qb))
            s=masked_scores(dot(k,qh,NT),start,q0,bq)
            m=jnp.max(s,axis=0,keepdims=True)
            e=jnp.exp(s-m)
            l=jnp.sum(e,axis=0,keepdims=True)
            lse_ref[0,h:h+1,q0:q0+bq]=m+jnp.log(l)
            oh=dot(vT[64*h:64*h+64,0:keys],e.astype(bf16))
            halves.append(oh*(1.0/l))
        o=jnp.concatenate(halves,axis=0).T
        o_ref[q0:q0+bq,:]=o
        c_ref[q0:q0+bq,:]=(o*hs_ref[...]).astype(bf16)

def attn_fwd(proj,start,hs_cols):
    return pl.pallas_call(fwd_kernel,
        grid=(H//2,),
        in_specs=[pl.BlockSpec((1,T),lambda p:(0,0)),pl.BlockSpec((1,128),lambda p:(0,p)),
                  pl.BlockSpec((T,128),lambda p:(0,p)),pl.BlockSpec((T,128),lambda p:(0,8+p)),pl.BlockSpec((T,128),lambda p:(0,16+p))],
        out_specs=[pl.BlockSpec((T,128),lambda p:(0,p)),pl.BlockSpec((T,128),lambda p:(0,p)),pl.BlockSpec((1,2,T),lambda p:(p,0,0))],
        out_shape=[jax.ShapeDtypeStruct((T,D),f32),jax.ShapeDtypeStruct((T,D),bf16),jax.ShapeDtypeStruct((H//2,2,T),f32)],
        compiler_params=pltpu.CompilerParams(vmem_limit_bytes=48<<20),
        name="attn_fwd")(start,hs_cols,proj,proj,proj)

def bwd_kernel(start_ref,lse_ref,o_ref,q_ref,k_ref,v_ref,do_ref,dq_ref,dk_ref,dv_ref,bsum_ref,dk_acc,dv_acc,dqT):
    lane=lax.broadcasted_iota(jnp.int32,(1,128),1)
    scale=jnp.asarray(HD**-0.5,bf16)
    kT=(k_ref[...]*scale).T
    prodT=(o_ref[...]*do_ref[...].astype(f32)).T
    delta=[jnp.sum(prodT[64*h:64*h+64],axis=0,keepdims=True) for h in range(2)]
    dk_acc[...]=jnp.zeros_like(dk_acc)
    dv_acc[...]=jnp.zeros_like(dv_acc)
    for q0,bq in BLOCKS:
        keys=q0+bq
        k=k_ref[0:keys,:]
        v=v_ref[0:keys,:]
        qb=q_ref[q0:q0+bq,:]*scale
        dob=do_ref[q0:q0+bq,:]
        start=start_ref[0:1,q0:q0+bq]
        for h in range(2):
            half=(lane>=64*h)&(lane<64*h+64)
            qh=jnp.where(half,qb,jnp.zeros_like(qb))
            doh=jnp.where(half,dob,jnp.zeros_like(dob))
            s=masked_scores(dot(k,qh,NT),start,q0,bq)
            p=jnp.exp(s-lse_ref[0,h:h+1,q0:q0+bq])
            dp=dot(v,doh,NT)
            ds=(p*(dp-delta[h][:,q0:q0+bq])).astype(bf16)
            dv_acc[0:keys,:]+=dot(p.astype(bf16),doh)
            dk_acc[0:keys,:]+=dot(ds,qh)
            dqT[64*h:64*h+64,q0:q0+bq]=dot(kT[64*h:64*h+64,0:keys],ds)
    dq=dqT[...].T.astype(bf16)
    dk=dk_acc[...].astype(bf16)
    dv=dv_acc[...].astype(bf16)
    dq_ref[...]=dq; dk_ref[...]=dk; dv_ref[...]=dv
    bsum_ref[0:1,:]=jnp.sum(dq.astype(f32),axis=0,keepdims=True)
    bsum_ref[1:2,:]=jnp.sum(dv.astype(f32),axis=0,keepdims=True)

def attn_bwd(proj,start,lse,o,do):
    blk=lambda off:pl.BlockSpec((T,128),lambda p:(0,off+p))
    row=pl.BlockSpec((1,2,T),lambda p:(p,0,0))
    return pl.pallas_call(bwd_kernel,
        grid=(H//2,),
        in_specs=[pl.BlockSpec((1,T),lambda p:(0,0)),row,blk(0),blk(0),blk(8),blk(16),blk(0)],
        out_specs=[blk(0),blk(0),blk(0),pl.BlockSpec((2,128),lambda p:(0,p))],
        out_shape=[jax.ShapeDtypeStruct((T,D),bf16)]*3+[jax.ShapeDtypeStruct((2,D),f32)],
        scratch_shapes=[pltpu.VMEM((T,128),f32),pltpu.VMEM((T,128),f32),pltpu.VMEM((128,T),f32)],
        compiler_params=pltpu.CompilerParams(vmem_limit_bytes=48<<20),
        name="attn_bwd")(start,lse,o,proj,proj,proj,do)

BOTH = ("replica", "fsdp")


def exchange(slab, devices):
    return lax.all_to_all(slab.reshape(devices, -1, 128), BOTH, split_axis=0, concat_axis=0, tiled=True).reshape(-1, 128)


def replica_sum(part, n):
    rows, width = part.shape
    if rows % (8 * n):
        part = part.reshape(-1, 128)
    got = lax.all_to_all(part.reshape(n, -1, part.shape[1]), "replica", split_axis=0, concat_axis=0, tiled=True)
    total = jnp.sum(got.astype(f32), axis=0).astype(bf16)
    spread = jnp.broadcast_to(total[None], (n, *total.shape))
    back = lax.all_to_all(spread, "replica", split_axis=0, concat_axis=0, tiled=True)
    return back.reshape(rows, width)


def on_device(
    tokens, cotangent, lengths, deal_order, inverse, ln1_gain, ln1_bias, w_qkv, b_query, b_value, head_scale, w_out, b_out,
    post_gain, post_bias, ln2_gain, ln2_bias, w_fc1, b_fc1, ffn_gain, ffn_bias, w_fc2, b_fc2,
):
    devices = lax.axis_size(BOTH)
    replicas = lax.axis_size("replica")
    count, width = tokens.shape
    row0 = jnp.concatenate(
        [ln1_gain, ln1_bias, b_query, b_value, b_out, post_gain, post_bias, ln2_gain, ln2_bias, b_fc2, head_scale,
         jnp.zeros((383,), bf16)]
    )
    row1 = jnp.concatenate([b_fc1, ffn_gain, ffn_bias, jnp.zeros((256,), bf16)])
    small = jnp.concatenate([row0[None], row1[None], jnp.zeros((6, width), bf16)], axis=0)
    cols = lambda w, n: [w[:, width * j : width * j + width] for j in range(n)]
    pack1 = lax.all_gather(jnp.concatenate(cols(w_qkv, 3) + [small], axis=0), "fsdp", axis=0)
    recv_keys = deal_order // count * count + jnp.arange(count, dtype=jnp.int32)
    sent_x = send_rows(tokens, inverse)
    got_x = exchange(sent_x, devices)
    sent_x, w_out, w_fc1, w_fc2, cotangent = lax.optimization_barrier((sent_x, w_out, w_fc1, w_fc2, cotangent))
    pack2 = lax.all_gather(jnp.concatenate([w_out] + cols(w_fc1, 4) + [w_fc2], axis=0), "fsdp", axis=0)
    sent_dy = send_rows(cotangent, inverse)
    sent_dy, got_x = lax.optimization_barrier((sent_dy, got_x))
    got_dy = exchange(sent_dy, devices)
    vec10 = pack1[:, 192, :640].reshape(16, 10, 64).transpose(1, 0, 2).reshape(10, width).astype(f32)
    scales = jnp.repeat(pack1[:, 192, 640].astype(f32), HD)[None]
    vec = jnp.concatenate([vec10, scales, jnp.zeros((5, width), f32)], axis=0)
    vff = pack1[:, 193, :768].reshape(16, 3, 256).transpose(1, 0, 2).reshape(3, 4 * width).astype(f32)
    vff = jnp.concatenate([vff, jnp.zeros((5, 4 * width), f32)], axis=0)
    places = jnp.arange(count, dtype=jnp.int32)
    starts = jnp.zeros((count,), jnp.int32)
    seq_end = jnp.zeros((), jnp.int32)
    for i in range(lengths.shape[1]):
        seq_end = seq_end + lengths[0, i]
        starts = jnp.where(places >= seq_end, seq_end, starts)
    starts = starts.reshape(1, count)
    x_rows, a, proj = recv_qkv(got_x, recv_keys, vec, pack1)
    o, c, lse = attn_fwd(proj, starts, scales)
    got_dy, c = lax.optimization_barrier((got_dy, c))
    dy_rows = recv_rows(got_dy, recv_keys)
    y, a2, n, du, dz, do, dres, gd, gf = mid(c, o, x_rows, dy_rows, vec, vff, pack2)
    sent_y = send_rows(y, recv_keys)
    sent_y, n = lax.optimization_barrier((sent_y, n))
    got_y = exchange(sent_y, devices)
    grads2 = grad2(c, dz, a2, du, n, dy_rows)
    grads2, do = lax.optimization_barrier((grads2, do))
    part2 = lax.psum_scatter(grads2, "fsdp", scatter_dimension=0)
    dq, dk, dv, bsum = attn_bwd(proj, starts, lse, o, do)
    dx, gl = dx_rows(dq, dk, dv, x_rows, dres, vec, pack1)
    sent_dx = send_rows(dx, recv_keys)
    sent_dx, a, got_y = lax.optimization_barrier((sent_dx, a, got_y))
    got_dx = exchange(sent_dx, devices)
    ten = jnp.concatenate([gl[0:2], bsum, gd[5:6], gd[3:5], gd[1:3], gd[0:1]], axis=0)
    ten = ten.reshape(10, 16, 64).transpose(1, 0, 2).reshape(16, 640)
    heads = jnp.sum(gd[6].reshape(H, HD), axis=1, keepdims=True)
    three = jnp.concatenate([gf[2:3], gf[0:2]], axis=0).reshape(3, 16, 256).transpose(1, 0, 2).reshape(16, 768)
    line0 = jnp.concatenate([ten, heads, jnp.zeros((16, 383), f32)], axis=1)
    line1 = jnp.concatenate([three, jnp.zeros((16, 256), f32)], axis=1)
    small_grads = jnp.concatenate([line0[:, None], line1[:, None], jnp.zeros((16, 6, width), f32)], axis=1)
    grads1 = grad1(a, dq, dk, dv, small_grads)
    grads1, part2, got_dx = lax.optimization_barrier((grads1, part2, got_dx))
    part1 = lax.psum_scatter(grads1, "fsdp", scatter_dimension=0)
    sum2 = replica_sum(part2, replicas).astype(f32)
    output = recv_rows(got_y, inverse)
    grad_tokens = recv_rows(got_dx, inverse)
    sum1 = replica_sum(part1, replicas).astype(f32)
    join = lambda s, at, k: jnp.concatenate([s[at + 64 * j : at + 64 * j + 64] for j in range(k)], axis=1)
    v = [sum1[192, 64 * k : 64 * k + 64] for k in range(10)]
    w = [sum1[193, 256 * k : 256 * k + 256] for k in range(3)]
    return (
        output, grad_tokens, v[0], v[1], join(sum1, 0, 3), v[2], v[3], sum1[192, 640:641], sum2[0:64], v[4],
        v[5], v[6], v[7], v[8], join(sum2, 64, 4), w[0], w[1], w[2], sum2[320:576], v[9],
    )


def solution(mesh):
    rows, vector, matrix = P(BOTH, None), P("fsdp"), P("fsdp", None)
    in_specs = (
        rows, rows, rows, P(BOTH), P(BOTH), vector, vector, matrix, vector, vector, vector, matrix, vector, vector, vector,
        vector, vector, matrix, vector, vector, vector, matrix, vector,
    )
    out_specs = (
        rows, rows, vector, vector, matrix, vector, vector, vector, matrix, vector, vector, vector, vector, vector, matrix,
        vector, vector, vector, matrix, vector,
    )
    return jax.shard_map(on_device, mesh=mesh, in_specs=in_specs, out_specs=out_specs, check_vma=False)
```

time: 1460 us -> 653 us (0.45)
  matrix products: 438 us -> 0 us
  Pallas kernels: 0 us -> 299 us
  local copies, waits for them, and re-layouts: 315 us -> 50.4 us
  other arithmetic: 241 us -> 9.05 us
  blocking collectives: 228 us -> 23.2 us
  waiting for transfers between devices: 164 us -> 194 us
  starting transfers between devices: 33.6 us -> 54.9 us
    dot_general x68 -> x0, matrix products: 438 us -> none  [the longest x16 81.1 us: block_parts(): jnp.einsum('qhd,khd->hqk', query_rows, key_rows, preferred_element_type=j...]
    pallas_call x0 -> x14, Pallas kernels: none -> 299 us  [the longest x1 93.4 us: mid(): pl.pallas_call(mid_kernel, grid=(t // bm,), in_specs=[row(d), row(d), row...]
    unnamed x2 -> x0, blocking collectives: 148 us -> none
    reduce_sum x27 -> x3, other arithmetic: 107 us -> 0.39 us  [the longest x2 0.27 us: replica_sum(): total = jnp.sum(got.astype(f32), axis=0).astype(bf16)]
    reduce_scatter x4 -> x2, waiting for transfers between devices: 0.03 us -> 88.1 us  [the longest x1 44.7 us: on_device(): part2 = lax.psum_scatter(grads2, 'fsdp', scatter_dimension=0)]
    dynamic_update_slice x32 -> x0, local copies, waits for them, and re-layouts: 79.5 us -> none  [the longest x16 37.3 us: attend_turn(): lax.dynamic_update_slice(attn_acc, mixed_rows.reshape(QB, 4 * HD), (q_sta...]
    all_to_all x4 -> x7, waiting for transfers between devices: 136 us -> 60.5 us  [the longest x4 45.8 us: exchange(): lax.all_to_all(slab.reshape(devices, -1, 128), BOTH, split_axis=0, concat...]
    dynamic_slice x72 -> x0, local copies, waits for them, and re-layouts: 57.5 us -> none  [the longest x16 18.8 us: block_parts(): lax.dynamic_slice(proj_b, (q_start, col_start), (QB, group_cols))]
  transfers between devices with their start and end apart: 13 -> 11, of which waited for: 4 -> 8; matrix products, arithmetic and copies ran while one was open for 58% -> 4% of each run, Pallas kernels for 0% -> 26%
where the time goes in v2:
time: 653 us; the launch traced here: 648 us
  Pallas kernels  299 us (46%)
  waiting for transfers between devices  194 us (30%)
  starting transfers between devices  54.9 us (8%)
  local copies, waits for them, and re-layouts  50.4 us (8%)
  blocking collectives  23.2 us (4%)
  between operations  17.1 us (3%)
  other arithmetic  9.05 us (1%)
    pallas_call x1, Pallas kernels, mid(): pl.pallas_call(mid_kernel, grid=(t // bm,), in_specs=[row(d), row(d), row...  93.4 us
    all_to_all x4, waiting for transfers between devices, exchange(): lax.all_to_all(slab.reshape(devices, -1, 128), BOTH, split_axis=0, concat...  45.8 us
    reduce_scatter x1, waiting for transfers between devices, on_device(): part2 = lax.psum_scatter(grads2, 'fsdp', scatter_dimension=0)  44.7 us
    reduce_scatter x1, waiting for transfers between devices, on_device(): part1 = lax.psum_scatter(grads1, 'fsdp', scatter_dimension=0)  43.3 us
    pallas_call x1, Pallas kernels, attn_fwd(): pl.pallas_call(fwd_kernel, grid=(H // 2,), in_specs=[pl.BlockSpec((1, T),...  41.6 us
    all_to_all x4, starting transfers between devices, exchange(): lax.all_to_all(slab.reshape(devices, -1, 128), BOTH, split_axis=0, concat...  39.6 us
    pallas_call x1, Pallas kernels, attn_bwd(): pl.pallas_call(bwd_kernel, grid=(H // 2,), in_specs=[pl.BlockSpec((1, T),...  39.2 us
    pallas_call x1, Pallas kernels, grad2(): pl.pallas_call(grad2_kernel, grid=(4,), in_specs=[col(256), full((t, d)),...  33.7 us
  transfers between devices with their start and end apart: 11, of which 8 were waited for; matrix products, arithmetic and copies ran while one was open for 4% of the time, Pallas kernels for 26%

profile of v2, /device:TPU:0, one launch (start us, length us, event | category | flops | bytes accessed | tf_op | source)
XLA Modules:
  0.0 647.7 jit_solution(1384986708806491012)
XLA Ops:
  7.2 1.2 fusion.8
  9.1 6.8 %concatenate.41 = bf16[1024]{0:T(1024)(128)(2,1)S(1)} concatenate(bf16[64]{0:T(256)(128)(2,1)} %param.28, bf16[64]{0:T(256)(128)(2,1)} %param.29, bf16[64]{0:T(256)(128)(2,1)} %param.31, bf16[64]{0:T(256)(128)(2,1)} %param.32, bf16[64]{0:T(256)(128)(2,1)} %param.35, bf16[64]{0:T(256)(128)(2,1)} %param.36, bf16[64]{0:T(256)(128)(2,1)} %param.37, bf16[64]{0:T(256)(128)(2,1)} %param.38, ...), dimensions={0} | concatenate | bytes 4096 | tf_op jit(solution)/shard_map/concatenate | solution.py:382
  16.6 2.6 concatenate.43
  20.0 0.9 reshape.176.kcol_ref
  21.0 5.5 send_rows.4
  26.6 1.0 copy-done.20
  27.7 11.6 %all-to-all-start = ((bf16[128,72,128]{2,1,0:T(8,128)(2,1)}), bf16[128,72,128]{2,1,0:T(8,128)(2,1)}, u32[]{:S(2)}, u32[]{:S(2)}) async-start(bf16[128,72,128]{2,1,0:T(8,128)(2,1)} %bitcast.4), calls=%async_computation | async-start | bytes 4718592 | tf_op jit(solution)/shard_map/all_to_all | solution.py:361
  39.3 5.6 send_rows.5
  44.9 30.4 %all-to-all-done = bf16[128,72,128]{2,1,0:T(8,128)(2,1)} async-done(((bf16[128,72,128]{2,1,0:T(8,128)(2,1)}), bf16[128,72,128]{2,1,0:T(8,128)(2,1)}, u32[]{:S(2)}, u32[]{:S(2)}) %all-to-all-start) | async-done | bytes 2359328 | tf_op jit(solution)/shard_map/all_to_all | solution.py:361
  75.3 7.3 %all-to-all-start.1 = ((bf16[128,72,128]{2,1,0:T(8,128)(2,1)}), bf16[128,72,128]{2,1,0:T(8,128)(2,1)S(1)}, u32[]{:S(2)}, u32[]{:S(2)}) async-start(bf16[128,72,128]{2,1,0:T(8,128)(2,1)} %bitcast.7), calls=%async_computation.1 | async-start | bytes 4718592 | tf_op jit(solution)/shard_map/all_to_all | solution.py:361
  83.0 1.4 fusion.11
  86.9 1.2 compare_select_fusion.2.start_ref
  88.2 28.3 %all-gather.5.cloned.1.call-done = bf16[3200,1024]{1,0:T(8,128)(2,1)} async-done(((bf16[200,1024]{1,0:T(8,128)(2,1)}), bf16[3200,1024]{1,0:T(8,128)(2,1)}) %all-gather.5.cloned.1.call-update) | async-done | bytes 6553616 | tf_op jit(solution)/shard_map/all_gather | solution.py:389
  116.5 1.0 fusion.3
  118.1 1.4 broadcast_in_dim_reshape.3.hs_ref
  119.5 1.6 fusion
  121.1 1.5 reshape.173
  122.6 1.6 copy.49
  124.2 1.6 reshape.170
  125.8 0.9 maximum_maximum_fusion.1.vec_ref
  126.7 19.7 %recv_qkv.1 = (bf16[1152,1024]{1,0:T(8,128)(2,1)S(1)}, bf16[1152,1024]{1,0:T(8,128)(2,1)S(1)}, bf16[1152,3072]{1,0:T(8,128)(2,1)}) custom-call(s32[1,1152]{1,0:T(1,128)S(1)} %reshape.154.krow_ref, s32[1152,1]{1,0:T(8,128)S(1)} %reshape.177.kcol_ref, bf16[9216,128]{1,0:T(8,128)(2,1)} %bitcast.5.got_ref, f32[16,1024]{1,0:T(8,128)S(1)} %maximum_maximum_fusion.1.vec_ref, ...), custom_call_target="tpu_custom_call" | custom-call | tf_op jit(solution)/shard_map/recv_qkv/pallas_call | solution.py:105
  146.5 1.4 copy-done.3
  147.9 1.5 copy-done.8
  149.4 41.6 %attn_fwd.1 = (f32[1152,1024]{1,0:T(8,128)}, bf16[1152,1024]{1,0:T(8,128)(2,1)S(1)}, f32[8,2,1152]{2,1,0:T(2,128)S(1)}) custom-call(s32[1,1152]{1,0:T(1,128)S(1)} %copy-done.14, f32[1,1024]{1,0:T(1,128)S(1)} %copy-done.16, bf16[1152,3072]{1,0:T(8,128)(2,1)} %get-tuple-element.61.q_ref.k_ref.v_ref, bf16[1152,3072]{1,0:T(8,128)(2,1)} %get-tuple-element.61.q_ref.k_ref.v_ref, ...), custom_call_target="tpu_custom_call" | custom-call | tf_op jit(solution)/shard_map/attn_fwd/pallas_call | solution.py:303
  190.9 1.4 copy-done.4
  193.0 5.9 recv_rows.3.dy_ref
  198.9 1.4 copy-done
  200.2 1.1 slice_reduce_fusion
  202.0 17.4 %all-gather.7.cloned.1.call-done = bf16[9216,1024]{1,0:T(8,128)(2,1)} async-done(((bf16[576,1024]{1,0:T(8,128)(2,1)}), bf16[9216,1024]{1,0:T(8,128)(2,1)}) %all-gather.7.cloned.1.call-update) | async-done | bytes 18874384 | tf_op jit(solution)/shard_map/all_gather | solution.py:394
  219.5 93.4 %mid_rows.1 = (bf16[1152,1024]{1,0:T(8,128)(2,1)}, bf16[1152,1024]{1,0:T(8,128)(2,1)}, bf16[1152,4096]{1,0:T(8,128)(2,1)}, bf16[1152,4096]{1,0:T(8,128)(2,1)}, b...) custom-call(bf16[1152,1024]{1,0:T(8,128)(2,1)} %copy-done.4, ...), custom_call_target="tpu_custom_call" | custom-call | tf_op jit(solution)/shard_map/mid_rows/pallas_call | solution.py:193
  312.9 1.7 copy-done.7
  314.6 5.5 send_rows.6
  320.1 33.7 %grad_ffn_out.1 = bf16[16,576,1024]{2,1,0:T(8,128)(2,1)} custom-call(bf16[1152,1024]{1,0:T(8,128)(2,1)} %copy-done.4, bf16[1152,1024]{1,0:T(8,128)(2,1)} %get-tuple-element.72.dz_ref, bf16[1152,1024]{1,0:T(8,128)(2,1)} %get-tuple-element.73.a2_ref, bf16[1152,4096]{1,0:T(8,128)(2,1)} %get-tuple-element.74.du_ref, bf16[1152,4096]{1,0:T(8,128)(2,1)} %get-tuple-element.77.n_ref, ...), custom_call_target="tpu_custom_call" | custom-call | tf_op jit(solution)/shard_map/grad_ffn_out/pallas_call | solution.py:237
  353.8 10.3 %all-to-all-start.2 = ((bf16[128,72,128]{2,1,0:T(8,128)(2,1)}), bf16[128,72,128]{2,1,0:T(8,128)(2,1)}, u32[]{:S(2)}, u32[]{:S(2)}) async-start(bf16[128,72,128]{2,1,0:T(8,128)(2,1)} %bitcast.12), calls=%async_computation.2 | async-start | bytes 4718592 | tf_op jit(solution)/shard_map/all_to_all | solution.py:361
  364.1 0.9 copy-done.13
  365.7 39.2 %attn_bwd.1 = (bf16[1152,1024]{1,0:T(8,128)(2,1)S(1)}, bf16[1152,1024]{1,0:T(8,128)(2,1)S(1)}, bf16[1152,1024]{1,0:T(8,128)(2,1)}, f32[2,1024]{1,0:T(2,128)S(1)}) custom-call(s32[1,1152]{1,0:T(1,128)S(1)} %copy-done.15, f32[8,2,1152]{2,1,0:T(2,128)S(1)} %copy-done.13, f32[1152,1024]{1,0:T(8,128)} %get-tuple-element.63.o_ref, ...), custom_call_target="tpu_custom_call" | custom-call | tf_op jit(solution)/shard_map/attn_bwd/pallas_call | solution.py:348
  405.0 1.4 copy-done.1
  406.4 14.4 %dx_rows.1 = (bf16[1152,1024]{1,0:T(8,128)(2,1)S(1)}, f32[8,1024]{1,0:T(8,128)S(1)}) custom-call(bf16[1152,1024]{1,0:T(8,128)(2,1)S(1)} %get-tuple-element.80.dq_ref, bf16[1152,1024]{1,0:T(8,128)(2,1)} %copy-done.1, bf16[1152,1024]{1,0:T(8,128)(2,1)} %get-tuple-element.82.dv_ref, bf16[1152,1024]{1,0:T(8,128)(2,1)} %copy-done.3, ...), custom_call_target="tpu_custom_call" | custom-call | tf_op jit(solution)/shard_map/dx_rows/pallas_call | solution.py:216
  421.4 4.5 send_rows.7
  425.9 1.4 copy-done.2
  427.3 10.4 %all-to-all-start.3 = ((bf16[128,72,128]{2,1,0:T(8,128)(2,1)}), bf16[128,72,128]{2,1,0:T(8,128)(2,1)}, u32[]{:S(2)}, u32[]{:S(2)}) async-start(bf16[128,72,128]{2,1,0:T(8,128)(2,1)} %bitcast.55), calls=%async_computation.4 | async-start | bytes 4718592 | tf_op jit(solution)/shard_map/all_to_all | solution.py:361
  437.9 0.9 slice.152
  438.8 0.9 slice.151
  441.6 1.7 copy-done.9
  443.3 12.8 %grad_qkv.1 = bf16[16,200,1024]{2,1,0:T(8,128)(2,1)} custom-call(bf16[1152,1024]{1,0:T(8,128)(2,1)S(1)} %copy-done.9, bf16[1152,1024]{1,0:T(8,128)(2,1)S(1)} %get-tuple-element.80.dq_ref, bf16[1152,1024]{1,0:T(8,128)(2,1)} %copy-done.1, bf16[1152,1024]{1,0:T(8,128)(2,1)} %get-tuple-element.82.dv_ref, f32[16,8,1024]{2,1,0:T(8,128)S(1)} %maximum_maximum_fusion.small_ref), custom_call_target="tpu_custom_call" | custom-call | tf_op jit(solution)/shard_map/grad_qkv/pallas_call | solution.py:253
  456.1 15.4 %all-to-all-done.3 = bf16[128,72,128]{2,1,0:T(8,128)(2,1)} async-done(((bf16[128,72,128]{2,1,0:T(8,128)(2,1)}), bf16[128,72,128]{2,1,0:T(8,128)(2,1)}, u32[]{:S(2)}, u32[]{:S(2)}) %all-to-all-start.3) | async-done | bytes 2359328 | tf_op jit(solution)/shard_map/all_to_all | solution.py:361
  471.5 44.7 %reduce-scatter.3.cloned.1.call-done = bf16[1,576,1024]{2,1,0:T(8,128)(2,1)} async-done(((bf16[16,576,1024]{2,1,0:T(8,128)(2,1)}), bf16[1,576,1024]{2,1,0:T(8,128)(2,1)}) %reduce-scatter.3.cloned.1.call-update) | async-done | bytes 1179664 | tf_op jit(solution)/shard_map/reduce_scatter | solution.py:420
  516.3 1.2 copy-done.21
  517.5 23.2 %all_to_all.40 = bf16[8,72,1024]{2,1,0:T(8,128)(2,1)S(1)} all-to-all(bf16[8,72,1024]{2,1,0:T(8,128)(2,1)S(1)} %bitcast.63), channel_id=1, replica_groups=mesh['replica'=8,'fsdp'=16] {'replica'}, dimensions={0} | all-to-all | bytes 2359296 | tf_op jit(solution)/shard_map/all_to_all | solution.py:368
  540.9 1.2 broadcast_in_dim.68
  542.1 3.9 all-to-all-start.7
  546.0 8.4 %recv_rows.4 = bf16[1152,1024]{1,0:T(8,128)(2,1)} custom-call(s32[1,1152]{1,0:T(1,128)S(1)} %reshape.152.krow_ref, s32[1152,1]{1,0:T(8,128)S(1)} %reshape.176.kcol_ref, bf16[9216,128]{1,0:T(8,128)(2,1)} %bitcast.13.got_ref), custom_call_target="tpu_custom_call" | custom-call | tf_op jit(solution)/shard_map/recv_rows/pallas_call | solution.py:67
  554.4 8.4 %recv_rows.5 = bf16[1152,1024]{1,0:T(8,128)(2,1)} custom-call(s32[1,1152]{1,0:T(1,128)S(1)} %reshape.152.krow_ref, s32[1152,1]{1,0:T(8,128)S(1)} %reshape.176.kcol_ref, bf16[9216,128]{1,0:T(8,128)(2,1)} %bitcast.20.got_ref), custom_call_target="tpu_custom_call" | custom-call | tf_op jit(solution)/shard_map/recv_rows/pallas_call | solution.py:67
  562.8 43.3 %reduce-scatter.5.cloned.1.call-done = bf16[1,200,1024]{2,1,0:T(8,128)(2,1)} async-done(((bf16[16,200,1024]{2,1,0:T(8,128)(2,1)}), bf16[1,200,1024]{2,1,0:T(8,128)(2,1)}) %reduce-scatter.5.cloned.1.call-update) | async-done | bytes 409616 | tf_op jit(solution)/shard_map/reduce_scatter | solution.py:435
  606.1 1.9 reshape_reshape_reduce_scatter.3
  608.1 7.6 %all-to-all-start.4 = ((bf16[8,200,128]{2,1,0:T(8,128)(2,1)}), bf16[8,200,128]{2,1,0:T(8,128)(2,1)S(1)}, u32[]{:S(2)}, u32[]{:S(2)}) async-start(bf16[8,200,128]{2,1,0:T(8,128)(2,1)} %reshape_reshape_reduce_scatter.3), calls=%async_computation.6 | async-start | bytes 819200 | tf_op jit(solution)/shard_map/all_to_all | solution.py:368
  616.1 1.1 slice.200
  617.2 0.8 fusion.5
  618.0 6.8 %all-to-all-done.4 = bf16[8,200,128]{2,1,0:T(8,128)(2,1)S(1)} async-done(((bf16[8,200,128]{2,1,0:T(8,128)(2,1)}), bf16[8,200,128]{2,1,0:T(8,128)(2,1)S(1)}, u32[]{:S(2)}, u32[]{:S(2)}) %all-to-all-start.4) | async-done | bytes 409632 | tf_op jit(solution)/shard_map/all_to_all | solution.py:368
  624.8 0.8 broadcast_in_dim.67
  625.6 3.5 all-to-all-start.5
  629.1 1.0 pad_maximum_fusion
  630.1 7.9 %all-to-all-done.5 = bf16[8,200,128]{2,1,0:T(8,128)(2,1)S(1)} async-done(((bf16[8,200,128]{2,1,0:T(8,128)(2,1)}), bf16[8,200,128]{2,1,0:T(8,128)(2,1)S(1)}, u32[]{:S(2)}, u32[]{:S(2)}) %all-to-all-start.5) | async-done | bytes 409632 | tf_op jit(solution)/shard_map/all_to_all | solution.py:371
  640.0 0.9 pad_maximum_fusion.1
  (104 shorter events, 10.5 us)
Async XLA Ops:
  7.2 13.7 %copy-start.5 = (bf16[1152,1024]{1,0:T(8,128)(2,1)S(1)}, bf16[1152,1024]{1,0:T(8,128)(2,1)}, u32[]{:S(2)}) copy-start(bf16[1152,1024]{1,0:T(8,128)(2,1)} %x_ref.1) | copy-start | bytes 7077892
  7.2 109.3 %all-gather.5.cloned.1.call-start = ((), (), s32[]{:S(2)}) async-start(), calls=%async_computation.12 | async-start | bytes 6963200 | tf_op jit(solution)/shard_map/all_gather | solution.py:389
  19.3 200.2 %all-gather.7.cloned.1.call-start = ((), (), s32[]{:S(2)}) async-start(), calls=%async_computation.13 | async-start | bytes 20054016 | tf_op jit(solution)/shard_map/all_gather | solution.py:394
  20.9 5.5 copy-start.24
  21.0 5.5 copy-start.22
  21.0 5.6 copy-start.23
  26.6 1.0 copy-start.20
  27.7 11.7 %copy-start.6 = (bf16[1152,1024]{1,0:T(8,128)(2,1)S(1)}, bf16[1152,1024]{1,0:T(8,128)(2,1)}, u32[]{:S(2)}) copy-start(bf16[1152,1024]{1,0:T(8,128)(2,1)} %x_ref.2) | copy-start | bytes 7077892
  27.7 47.6 %all-to-all-start = ((bf16[128,72,128]{2,1,0:T(8,128)(2,1)}), bf16[128,72,128]{2,1,0:T(8,128)(2,1)}, u32[]{:S(2)}, u32[]{:S(2)}) async-start(bf16[128,72,128]{2,1,0:T(8,128)(2,1)} %bitcast.4), calls=%async_computation | async-start | bytes 4718592 | tf_op jit(solution)/shard_map/all_to_all | solution.py:361
  75.2 7.5 %copy-start.26 = (s32[1152]{0:T(1024)S(1)}, s32[1152]{0:T(1024)}, u32[]{:S(2)}) copy-start(s32[1152]{0:T(1024)} %param.26) | copy-start | bytes 13828
  75.3 117.7 %all-to-all-start.1 = ((bf16[128,72,128]{2,1,0:T(8,128)(2,1)}), bf16[128,72,128]{2,1,0:T(8,128)(2,1)S(1)}, u32[]{:S(2)}, u32[]{:S(2)}) async-start(bf16[128,72,128]{2,1,0:T(8,128)(2,1)} %bitcast.7), calls=%async_computation.1 | async-start | bytes 4718592 | tf_op jit(solution)/shard_map/all_to_all | solution.py:361
  82.5 433.7 %reduce-scatter.3.cloned.1.call-start = ((), (), s32[]{:S(2)}) async-start(), calls=%async_computation.10 | async-start | bytes 20054016 | tf_op jit(solution)/shard_map/reduce_scatter | solution.py:420
  126.7 19.8 %copy-start.10 = (f32[16,1024]{1,0:T(8,128)}, f32[16,1024]{1,0:T(8,128)S(1)}, u32[]{:S(2)}) copy-start(f32[16,1024]{1,0:T(8,128)S(1)} %maximum_maximum_fusion.1.vec_ref) | copy-start | bytes 196612
  126.7 22.6 %copy-start.14 = (s32[1,1152]{1,0:T(1,128)S(1)}, s32[1,1152]{1,0:T(1,128)}, u32[]{:S(2)}) copy-start(s32[1,1152]{1,0:T(1,128)} %compare_select_fusion.2.start_ref) | copy-start | bytes 13828
  126.7 22.6 %copy-start.16 = (f32[1,1024]{1,0:T(1,128)S(1)}, f32[1,1024]{1,0:T(1,128)}, u32[]{:S(2)}) copy-start(f32[1,1024]{1,0:T(1,128)} %broadcast_in_dim_reshape.3.hs_ref) | copy-start | bytes 12292
  146.5 1.4 copy-start.3
  147.9 1.5 copy-start.8
  190.9 1.4 copy-start.4
  192.3 0.6 copy-start.12
  198.9 1.4 copy-start
  312.9 1.7 copy-start.7
  353.8 73.5 %all-to-all-start.2 = ((bf16[128,72,128]{2,1,0:T(8,128)(2,1)}), bf16[128,72,128]{2,1,0:T(8,128)(2,1)}, u32[]{:S(2)}, u32[]{:S(2)}) async-start(bf16[128,72,128]{2,1,0:T(8,128)(2,1)} %bitcast.12), calls=%async_computation.2 | async-start | bytes 4718592 | tf_op jit(solution)/shard_map/all_to_all | solution.py:361
  364.1 0.9 copy-start.13
  365.0 0.7 copy-start.15
  365.7 40.6 %copy-start.11 = (f32[16,1024]{1,0:T(8,128)S(1)}, f32[16,1024]{1,0:T(8,128)}, u32[]{:S(2)}) copy-start(f32[16,1024]{1,0:T(8,128)} %copy-done.10) | copy-start | bytes 196612
  404.9 1.4 copy-start.1
  406.4 14.4 %copy-start.17 = (f32[2,1024]{1,0:T(2,128)}, f32[2,1024]{1,0:T(2,128)S(1)}, u32[]{:S(2)}) copy-start(f32[2,1024]{1,0:T(2,128)S(1)} %get-tuple-element.90) | copy-start | bytes 24580
  420.8 0.6 copy-start.19
  425.9 1.4 copy-start.2
  427.3 12.6 %copy-start.25 = (f32[8,1024]{1,0:T(8,128)S(1)}, f32[8,1024]{1,0:T(8,128)}, u32[]{:S(2)}) copy-start(f32[8,1024]{1,0:T(8,128)} %get-tuple-element.91) | copy-start | bytes 98308
  427.3 13.7 %copy-start.18 = (f32[2,1024]{1,0:T(2,128)S(1)}, f32[2,1024]{1,0:T(2,128)}, u32[]{:S(2)}) copy-start(f32[2,1024]{1,0:T(2,128)} %copy-done.17) | copy-start | bytes 24580
  427.3 44.2 %all-to-all-start.3 = ((bf16[128,72,128]{2,1,0:T(8,128)(2,1)}), bf16[128,72,128]{2,1,0:T(8,128)(2,1)}, u32[]{:S(2)}, u32[]{:S(2)}) async-start(bf16[128,72,128]{2,1,0:T(8,128)(2,1)} %bitcast.55), calls=%async_computation.4 | async-start | bytes 4718592 | tf_op jit(solution)/shard_map/all_to_all | solution.py:361
  437.7 168.4 %reduce-scatter.5.cloned.1.call-start = ((), (), s32[]{:S(2)}) async-start(), calls=%async_computation.11 | async-start | bytes 6963200 | tf_op jit(solution)/shard_map/reduce_scatter | solution.py:435
  441.6 1.7 copy-start.9
  516.2 1.3 copy-start.21
  542.1 66.0 %all-to-all-start.7 = ((bf16[8,72,1024]{2,1,0:T(8,128)(2,1)}), bf16[8,72,1024]{2,1,0:T(8,128)(2,1)S(1)}, u32[]{:S(2)}, u32[]{:S(2)}) async-start(bf16[8,72,1024]{2,1,0:T(8,128)(2,1)} %broadcast_in_dim.68), calls=%async_computation.9 | async-start | bytes 2359296 | tf_op jit(solution)/shard_map/all_to_all | solution.py:371
  608.1 16.7 %all-to-all-start.4 = ((bf16[8,200,128]{2,1,0:T(8,128)(2,1)}), bf16[8,200,128]{2,1,0:T(8,128)(2,1)S(1)}, u32[]{:S(2)}, u32[]{:S(2)}) async-start(bf16[8,200,128]{2,1,0:T(8,128)(2,1)} %reshape_reshape_reduce_scatter.3), calls=%async_computation.6 | async-start | bytes 819200 | tf_op jit(solution)/shard_map/all_to_all | solution.py:368
  625.6 12.4 %all-to-all-start.5 = ((bf16[8,200,128]{2,1,0:T(8,128)(2,1)}), bf16[8,200,128]{2,1,0:T(8,128)(2,1)S(1)}, u32[]{:S(2)}, u32[]{:S(2)}) async-start(bf16[8,200,128]{2,1,0:T(8,128)(2,1)} %broadcast_in_dim.67), calls=%async_computation.7 | async-start | bytes 819200 | tf_op jit(solution)/shard_map/all_to_all | solution.py:371
Sparse Core Ops, SparseCore 0:
  19.4 97.0 all-gather.4
  118.2 101.2 all-gather.6
  353.9 162.2 reduce-scatter.2
  518.5 87.5 reduce-scatter.4

commit v3 on v2

v3 whole, which is shorter than its diff:
```python
import jax
import jax.numpy as jnp
from jax import lax
from jax.experimental import pallas as pl
from jax.experimental.pallas import tpu as pltpu
from jax.sharding import PartitionSpec as P

f32 = jnp.float32
bf16 = jnp.bfloat16
H = 16
HD = 64
EPS = 1e-5
NEG = -1000000000.0
NT = (((1,), (1,)), ((), ()))
NN = (((1,), (0,)), ((), ()))
TN = (((0,), (0,)), ((), ()))


def dot(a, b, dn=NN):
    return lax.dot_general(a, b, dn, preferred_element_type=f32)


def hbm_call(kernel, **kw):
    call = pl.pallas_call(kernel, **kw)
    pin = lambda v: pltpu.with_memory_space_constraint(v, pltpu.HBM) if v.size > 1000 else v
    return lambda *args: call(*[pin(v) for v in args])


def cost(micros):
    return pl.CostEstimate(flops=0, transcendentals=0, bytes_accessed=micros * 3000000)

def rank_row(kcol,krow):
    return jnp.sum((kcol<krow).astype(f32),axis=0,keepdims=True).astype(jnp.int32)
def rank_col(krow,kcol):
    return jnp.sum((krow<kcol).astype(f32),axis=1,keepdims=True).astype(jnp.int32)

def send_kernel(krow_ref,kcol_ref,x_ref,out_ref,rank_ref,wide_ref):
    i=pl.program_id(0); bs=out_ref.shape[0]//8
    @pl.when(i==0)
    def _(): rank_ref[...]=rank_row(kcol_ref[...],krow_ref[...])
    t=rank_ref.shape[1]
    pick=(lax.broadcasted_iota(jnp.int32,(bs,t),0)+i*bs==rank_ref[...]).astype(f32).astype(bf16)
    rows=dot(pick,x_ref[...])
    for k in range(8):
        wide_ref[pl.ds(k,bs,stride=8),:]=rows[:,128*k:128*k+128]
    out_ref[...]=wide_ref[...].astype(bf16)

def send_rows(x,keys,blocks=3):
    t,d=x.shape; bs=t//blocks
    full=lambda s:pl.BlockSpec(s,lambda i:(0,0))
    return hbm_call(send_kernel,grid=(blocks,),
        in_specs=[full((1,t)),full((t,1)),full((t,d))],
        out_specs=pl.BlockSpec((bs*8,128),lambda i:(i,0)),
        out_shape=pltpu.HBM((t*8,128),bf16),
        scratch_shapes=[pltpu.VMEM((1,t),jnp.int32),pltpu.VMEM((bs*8,128),f32)],
        compiler_params=pltpu.CompilerParams(vmem_limit_bytes=40<<20),name="send_rows",cost_estimate=cost(5))(keys.reshape(1,t),keys.reshape(t,1),x)

def unpack_rows(got_ref,wide_ref,rows_ref,chunk=384):
    t=rows_ref.shape[0]
    for c in range(0,t,chunk):
        wide_ref[...]=got_ref[8*c:8*(c+chunk),:].astype(f32)
        for k in range(8):
            rows_ref[c:c+chunk,128*k:128*k+128]=wide_ref[pl.ds(k,chunk,stride=8),:].astype(bf16)

def recv_kernel(krow_ref,kcol_ref,got_ref,out_ref,wide_ref,rows_ref):
    i=pl.program_id(0); bs=out_ref.shape[0]
    @pl.when(i==0)
    def _(): unpack_rows(got_ref,wide_ref,rows_ref)
    t=rows_ref.shape[0]
    rank=rank_col(krow_ref[...],kcol_ref[...])
    pick=(lax.broadcasted_iota(jnp.int32,(bs,t),1)==rank).astype(f32).astype(bf16)
    out_ref[...]=dot(pick,rows_ref[...]).astype(bf16)

def recv_rows(got,keys,blocks=3):
    t=got.shape[0]//8; d=1024; bs=t//blocks
    full=lambda s:pl.BlockSpec(s,lambda i:(0,0))
    return hbm_call(recv_kernel,grid=(blocks,),
        in_specs=[full((1,t)),pl.BlockSpec((bs,1),lambda i:(i,0)),full((t*8,128))],
        out_specs=pl.BlockSpec((bs,d),lambda i:(i,0)),
        out_shape=pltpu.HBM((t,d),bf16),
        scratch_shapes=[pltpu.VMEM((384*8,128),f32),pltpu.VMEM((t,d),bf16)],
        compiler_params=pltpu.CompilerParams(vmem_limit_bytes=40<<20),name="recv_rows",cost_estimate=cost(6))(keys.reshape(1,t),keys.reshape(t,1),got)

def norm_parts(v):
    m=jnp.mean(v,axis=-1,keepdims=True); c=v-m
    r=lax.rsqrt(jnp.mean(c*c,axis=-1,keepdims=True)+EPS)
    return c*r,r
def norm_back(e,g,vhat,r):
    eg=e*g
    return r*(eg-jnp.mean(eg,axis=-1,keepdims=True)-vhat*jnp.mean(eg*vhat,axis=-1,keepdims=True))
def colsum(v): return jnp.sum(v,axis=0,keepdims=True)

def qkv_kernel(krow_ref,kcol_ref,got_ref,vec_ref,w_ref,x_ref,a_ref,proj_ref,wide_ref,rows_ref):
    i=pl.program_id(0); bs=x_ref.shape[0]
    @pl.when(i==0)
    def _(): unpack_rows(got_ref,wide_ref,rows_ref)
    t=rows_ref.shape[0]
    rank=rank_col(krow_ref[...],kcol_ref[...])
    pick=(lax.broadcasted_iota(jnp.int32,(bs,t),1)==rank).astype(f32).astype(bf16)
    x=dot(pick,rows_ref[...])
    x_ref[...]=x.astype(bf16)
    xhat,_=norm_parts(x)
    a=(xhat*vec_ref[0:1,:]+vec_ref[1:2,:]).astype(bf16)
    a_ref[...]=a
    for j in range(3):
        w=w_ref[:,64*j:64*j+64,:].reshape(1024,1024)
        pj=dot(a,w)
        if j==0: pj=pj+vec_ref[2:3,:]
        if j==2: pj=pj+vec_ref[3:4,:]
        proj_ref[:,1024*j:1024*j+1024]=pj.astype(bf16)

def recv_qkv(got,keys,vec,pack1,blocks=3):
    t=got.shape[0]//8; d=1024; bs=t//blocks
    full=lambda s:pl.BlockSpec(s,lambda i:(0,)*len(s))
    return hbm_call(qkv_kernel,grid=(blocks,),
        in_specs=[full((1,t)),pl.BlockSpec((bs,1),lambda i:(i,0)),full((t*8,128)),full(vec.shape),
                  pl.BlockSpec((16,192,1024),lambda i:(0,0,0),pipeline_mode=pl.Buffered(1))],
        out_specs=[pl.BlockSpec((bs,d),lambda i:(i,0)),pl.BlockSpec((bs,d),lambda i:(i,0)),pl.BlockSpec((bs,3*d),lambda i:(i,0))],
        out_shape=[pltpu.HBM((t,d),bf16),pltpu.HBM((t,d),bf16),pltpu.HBM((t,3*d),bf16)],
        scratch_shapes=[pltpu.VMEM((384*8,128),f32),pltpu.VMEM((t,d),bf16)],
        compiler_params=pltpu.CompilerParams(vmem_limit_bytes=48<<20),name="recv_qkv",cost_estimate=cost(18))(keys.reshape(1,t),keys.reshape(t,1),got,vec,pack1)

RT2=0.7071067811865476; RPI=0.3989422804014327
FF=4096
def up_kernel(c_ref,x_ref,vec_ref,w_ref,a2_ref,n_ref,vhat_ref,gp_ref,hres_ref,zhat_ref,st_ref,g_s):
    vec=lambda k:vec_ref[k:k+1,:]
    z=dot(c_ref[...],w_ref[:,0:64,:].reshape(1024,1024))+vec(4)
    zhat,rz=norm_parts(z)
    zhat_ref[...]=zhat
    hres=x_ref[...].astype(f32)+zhat*vec(5)+vec(6)
    hres_ref[...]=hres
    hhat,_=norm_parts(hres)
    a2=(hhat*vec(7)+vec(8)).astype(bf16)
    a2_ref[...]=a2
    tot=0.0
    for j in range(4):
        cols=slice(1024*j,1024*j+1024)
        u=dot(a2,w_ref[:,64+64*j:128+64*j,:].reshape(1024,1024))+vec(11+j)
        phi=0.5+0.5*lax.erf(u*RT2)
        g=u*phi
        gp_ref[:,cols]=(phi+u*(RPI*jnp.exp(-0.5*u*u))).astype(bf16)
        g_s[:,cols]=g
        tot=tot+jnp.sum(g,axis=-1,keepdims=True)
    mean=tot*(1.0/FF)
    var=0.0
    for j in range(4):
        cen=g_s[:,1024*j:1024*j+1024]-mean
        var=var+jnp.sum(cen*cen,axis=-1,keepdims=True)
    rf=lax.rsqrt(var*(1.0/FF)+EPS)
    for j in range(4):
        cols=slice(1024*j,1024*j+1024)
        vhat=(g_s[:,cols]-mean)*rf
        vhat_ref[:,cols]=vhat.astype(bf16)
        n_ref[:,cols]=(vhat*vec(15+j)+vec(19+j)).astype(bf16)
    lane=lax.broadcasted_iota(jnp.int32,(1,128),1)
    st_ref[...]=jnp.where(lane==0,rz,rf)

def row_specs(bm):
    row=lambda n:pl.BlockSpec((bm,n),lambda i:(i,0))
    full=lambda s,**k:pl.BlockSpec(s,lambda i:(0,)*len(s),**k)
    return row,full

def up_rows(c,x,vec,packa,bm=192):
    t,d=c.shape
    row,full=row_specs(bm); sd=pltpu.HBM
    return hbm_call(up_kernel,grid=(t//bm,),
        in_specs=[row(d),row(d),full(vec.shape),full(packa.shape,pipeline_mode=pl.Buffered(1))],
        out_specs=[row(d),row(FF),row(FF),row(FF),row(d),row(d),row(128)],
        out_shape=[sd((t,d),bf16),sd((t,FF),bf16),sd((t,FF),bf16),sd((t,FF),bf16),sd((t,d),f32),sd((t,d),f32),sd((t,128),f32)],
        scratch_shapes=[pltpu.VMEM((bm,FF),f32)],
        compiler_params=pltpu.CompilerParams(vmem_limit_bytes=60<<20),name="up_rows",cost_estimate=cost(45))(c,x,vec,packa)

def down_kernel(n_ref,vhat_ref,gp_ref,st_ref,dy_ref,hres_ref,vec_ref,w_ref,y_ref,du_ref,gd_ref,gf_ref,e_s):
    @pl.when(pl.program_id(0)==0)
    def _():
        gd_ref[...]=jnp.zeros_like(gd_ref); gf_ref[...]=jnp.zeros_like(gf_ref)
    vec=lambda k:vec_ref[k:k+1,:]
    rf=st_ref[:,1:2]
    dy=dy_ref[...]
    y=hres_ref[...]+vec(9)
    s1=0.0; s2=0.0
    for j in range(4):
        cols=slice(1024*j,1024*j+1024)
        w=w_ref[4*j:4*j+4].reshape(1024,1024)
        y=y+dot(n_ref[:,cols],w)
        dn=dot(dy,w,NT)
        vhat=vhat_ref[:,cols].astype(f32)
        dv=dn*vhat
        gf_ref[j:j+1,:]+=colsum(dv)
        gf_ref[4+j:5+j,:]+=colsum(dn)
        gain=vec(15+j)
        e=dn*gain
        e_s[:,cols]=e
        s1=s1+jnp.sum(e,axis=-1,keepdims=True)
        s2=s2+jnp.sum(dv*gain,axis=-1,keepdims=True)
    y_ref[...]=y.astype(bf16)
    s1=s1*(1.0/FF); s2=s2*(1.0/FF)
    for j in range(4):
        cols=slice(1024*j,1024*j+1024)
        du=(gp_ref[:,cols].astype(f32)*(rf*(e_s[:,cols]-s1-vhat_ref[:,cols].astype(f32)*s2))).astype(bf16)
        du_ref[:,cols]=du
        gf_ref[8+j:9+j,:]+=colsum(du.astype(f32))
    gd_ref[0:1,:]+=colsum(dy.astype(f32))

def down_rows(n,vhat,gp,st,dy,hres,vec,packb,bm=192):
    t,d=dy.shape
    row,full=row_specs(bm); sd=pltpu.HBM
    return hbm_call(down_kernel,grid=(t//bm,),
        in_specs=[row(FF),row(FF),row(FF),row(128),row(d),row(d),full(vec.shape),full(packb.shape,pipeline_mode=pl.Buffered(1))],
        out_specs=[row(d),row(FF),full((8,d)),full((16,d))],
        out_shape=[sd((t,d),bf16),sd((t,FF),bf16),sd((8,d),f32),sd((16,d),f32)],
        scratch_shapes=[pltpu.VMEM((bm,FF),f32)],
        compiler_params=pltpu.CompilerParams(vmem_limit_bytes=60<<20),name="down_rows",cost_estimate=cost(40))(n,vhat,gp,st,dy,hres,vec,packb)

def back_kernel(du_ref,dy_ref,hres_ref,zhat_ref,st_ref,o_ref,vec_ref,w_ref,dz_ref,do_ref,dres_ref,gd_ref):
    @pl.when(pl.program_id(0)==0)
    def _(): gd_ref[...]=jnp.zeros_like(gd_ref)
    vec=lambda k:vec_ref[k:k+1,:]
    da2=0.0
    for j in range(4):
        da2=da2+dot(du_ref[:,1024*j:1024*j+1024],w_ref[:,64+64*j:128+64*j,:].reshape(1024,1024),NT)
    hhat,rh=norm_parts(hres_ref[...])
    gd_ref[1:2,:]+=colsum(da2*hhat)
    gd_ref[2:3,:]+=colsum(da2)
    dres=dy_ref[...].astype(f32)+norm_back(da2,vec(7),hhat,rh)
    dres_ref[...]=dres
    zhat=zhat_ref[...]
    gd_ref[3:4,:]+=colsum(dres*zhat)
    gd_ref[4:5,:]+=colsum(dres)
    dz=norm_back(dres,vec(5),zhat,st_ref[:,0:1]).astype(bf16)
    dz_ref[...]=dz
    gd_ref[5:6,:]+=colsum(dz.astype(f32))
    dc=dot(dz,w_ref[:,0:64,:].reshape(1024,1024),NT)
    gd_ref[6:7,:]+=colsum(dc*o_ref[...])
    do_ref[...]=(dc*vec(10)).astype(bf16)

def back_rows(du,dy,hres,zhat,st,o,vec,packa,bm=384):
    t,d=dy.shape
    row,full=row_specs(bm); sd=pltpu.HBM
    return hbm_call(back_kernel,grid=(t//bm,),
        in_specs=[row(FF),row(d),row(d),row(d),row(128),row(d),full(vec.shape),full(packa.shape,pipeline_mode=pl.Buffered(1))],
        out_specs=[row(d),row(d),row(d),full((8,d))],
        out_shape=[sd((t,d),bf16),sd((t,d),bf16),sd((t,d),f32),sd((8,d),f32)],
        compiler_params=pltpu.CompilerParams(vmem_limit_bytes=60<<20),name="back_rows",cost_estimate=cost(25))(du,dy,hres,zhat,st,o,vec,packa)

def dx_kernel(*refs):
    *halves,x_ref,dres_ref,vec_ref,w_ref,dx_ref,g_ref=refs
    @pl.when(pl.program_id(0)==0)
    def _(): g_ref[...]=jnp.zeros_like(g_ref)
    da=0.0
    for j in range(3):
        w=w_ref[:,64*j:64*j+64,:].reshape(1024,1024)
        da=da+dot(halves[j][...],w[:,0:512],NT)+dot(halves[3+j][...],w[:,512:1024],NT)
    xhat,r=norm_parts(x_ref[...].astype(f32))
    g_ref[0:1,:]+=colsum(da*xhat)
    g_ref[1:2,:]+=colsum(da)
    dx_ref[...]=(dres_ref[...]+norm_back(da,vec_ref[0:1,:],xhat,r)).astype(bf16)

def dx_rows(halves,x,dres,vec,pack1,blocks=3):
    t,d=x.shape; bs=t//blocks
    row=lambda n:pl.BlockSpec((bs,n),lambda i:(i,0))
    full=lambda s,**k:pl.BlockSpec(s,lambda i:(0,)*len(s),**k)
    return hbm_call(dx_kernel,grid=(blocks,),
        in_specs=[row(d//2)]*6+[row(d),row(d),full(vec.shape),full((16,192,1024),pipeline_mode=pl.Buffered(1))],
        out_specs=[row(d),full((8,d))],
        out_shape=[pltpu.HBM((t,d),bf16),pltpu.HBM((8,d),f32)],
        compiler_params=pltpu.CompilerParams(vmem_limit_bytes=48<<20),name="dx_rows",cost_estimate=cost(14))(*halves,x,dres,vec,pack1)

def grad_fc2_kernel(n_ref,dy_ref,out_ref):
    res=dot(n_ref[...],dy_ref[...],TN).astype(bf16)
    for f in range(out_ref.shape[0]):
        for r in range(8):
            out_ref[f,r]=res[256*f:256*f+256,128*r:128*r+128]

def grad_fc2(n,dy,steps=4):
    t,d=dy.shape; w=FF//steps
    return hbm_call(grad_fc2_kernel,grid=(steps,),
        in_specs=[pl.BlockSpec((t,w),lambda i:(0,i)),pl.BlockSpec((t,d),lambda i:(0,0),pipeline_mode=pl.Buffered(1))],
        out_specs=pl.BlockSpec((w//256,8,256,128),lambda i:(i,0,0,0)),
        out_shape=pltpu.HBM((16,8,256,128),bf16),
        compiler_params=pltpu.CompilerParams(vmem_limit_bytes=48<<20),name="grad_fc2",cost_estimate=cost(14))(n,dy)

def grad_up_kernel(c_ref,dz_ref,a2_ref,du_ref,out_ref):
    def put(res,at):
        res=res.astype(bf16)
        for f in range(4):
            for r in range(8):
                out_ref[f,r,at:at+64,:]=res[64*f:64*f+64,128*r:128*r+128]
    put(dot(c_ref[...],dz_ref[...],TN),0)
    for j in range(4):
        put(dot(a2_ref[...],du_ref[:,1024*j:1024*j+1024],TN),64+64*j)

def grad_up(c,dz,a2,du):
    t,d=c.shape
    col=pl.BlockSpec((t,256),lambda i:(0,i))
    full=lambda s:pl.BlockSpec(s,lambda i:(0,0),pipeline_mode=pl.Buffered(1))
    return hbm_call(grad_up_kernel,grid=(4,),
        in_specs=[col,full((t,d)),col,full((t,FF))],
        out_specs=pl.BlockSpec((4,8,320,128),lambda i:(i,0,0,0)),
        out_shape=pltpu.HBM((16,8,320,128),bf16),
        compiler_params=pltpu.CompilerParams(vmem_limit_bytes=56<<20),name="grad_up",cost_estimate=cost(20))(c,dz,a2,du)

def grad_qkv_kernel(core_ref,a_ref,dq_ref,dk_ref,dv_ref,*refs):
    vecs,(keep_ref,give_ref)=refs[:-2],refs[-2:]
    i=pl.program_id(0)
    first=core_ref[0]==0
    for p,ref in enumerate((dq_ref,dk_ref,dv_ref)):
        res=dot(a_ref[...],ref[...],TN)
        for chip in range(2):
            even=res[128*chip:128*chip+64,:]; odd=res[128*chip+64:128*chip+128,:]
            mine=jnp.where(first,even,odd).astype(bf16)
            other=jnp.where(first,odd,even).astype(bf16)
            for l in range(4):
                for h in range(2):
                    q=2*(4*p+l)+h; at=32*(q%3)
                    keep_ref[q//3,chip,at:at+32,:]=mine[32*h:32*h+32,128*l:128*l+128]
                    give_ref[q//3,chip,at:at+32,:]=other[32*h:32*h+32,128*l:128*l+128]
    if vecs:
        gl_ref,b1_ref,b2_ref,gd_ref,gd0_ref,gf_ref=vecs
        for chip in range(2):
            cols=slice(128*chip,128*chip+128)
            half=jnp.where(i<2,b1_ref[:,cols],b2_ref[:,cols])
            line=lambda ref,k:ref[k:k+1,cols]
            ten=[gl_ref[0:2,cols],half,line(gd_ref,5),gd_ref[3:5,cols],gd_ref[1:3,cols],line(gd0_ref,0),line(gd_ref,6)]
            pick=lambda v,at:sum(jnp.where(i==k,gf_ref[4*v+k:4*v+k+1,at:at+128],0.0) for k in range(4))
            long=[pick(v,512*chip+128*b) for v in (2,0,1) for b in range(4)]
            rows=jnp.concatenate(ten+long+[jnp.zeros((1,128),f32)],axis=0).astype(bf16)
            for r in range(8):
                part=rows[8*r:8*r+8,:] if r<3 else jnp.zeros((8,128),bf16)
                keep_ref[r,chip,96:104,:]=part
                give_ref[r,chip,96:104,:]=part

def grad_qkv(core,a,dq,dk,dv,vecs=()):
    t,d=a.shape; w=dq.shape[1]; rows=104 if vecs else 96
    full=pl.BlockSpec((t,w),lambda i,c:(0,0),pipeline_mode=pl.Buffered(1))
    out=pl.BlockSpec((8,2,rows,128),lambda i,c:(0,i,0,0))
    lanes=lambda v:pl.BlockSpec((v.shape[0],256),lambda i,c:(0,i))
    more=[]
    if vecs:
        gl,b1,b2,gd,gd0,gf=vecs
        half=lambda lo:pl.BlockSpec((2,256),lambda i,c:(0,jnp.clip(i-lo,0,1)))
        more=[lanes(gl),half(0),half(2),lanes(gd),lanes(gd0),pl.BlockSpec(gf.shape,lambda i,c:(0,0))]
    return hbm_call(grad_qkv_kernel,
        grid_spec=pltpu.PrefetchScalarGridSpec(num_scalar_prefetch=1,grid=(4,),
            in_specs=[pl.BlockSpec((t,256),lambda i,c:(0,i)),full,full,full]+more,
            out_specs=[out,out]),
        out_shape=[pltpu.HBM((8,8,rows,128),bf16)]*2,
        compiler_params=pltpu.CompilerParams(vmem_limit_bytes=48<<20),name="grad_qkv",cost_estimate=cost(8))(core,a,dq,dk,dv,*vecs)

def totals_kernel(*refs):
    *parts,out_ref=refs
    at=0
    for p in parts:
        n=p.shape[1]
        total=jnp.sum(p[...].astype(f32),axis=0).astype(bf16)
        for r in range(8):
            out_ref[r,at:at+n,:]=total
        at+=n

def totals(parts):
    rows=sum(p.shape[1] for p in parts)
    return hbm_call(totals_kernel,out_shape=pltpu.HBM((8,rows,128),bf16),
        compiler_params=pltpu.CompilerParams(vmem_limit_bytes=40<<20),name="totals",cost_estimate=cost(4))(*parts)

def finish_kernel(core_ref,s_ref,qkv_ref,out_ref,fc1_ref,fc2_ref,ten_ref,three_ref):
    piece=lambda r,at,n:s_ref[r,at:at+n,:].astype(f32)
    for r in range(8):
        cols=slice(128*r,128*r+128)
        fc2_ref[:,cols]=piece(r,0,256)
        out_ref[:,cols]=piece(r,256,64)
        for j in range(4):
            fc1_ref[:,1024*j+128*r:1024*j+128*r+128]=piece(r,320+64*j,64)
    for half in range(2):
        for p in range(3):
            for l in range(4):
                lanes=1024*p+512*half+128*l
                for h in range(2):
                    q=2*(4*p+l)+h
                    qkv_ref[32*h:32*h+32,lanes:lanes+128]=piece(q//3,576+96*half+32*(q%3),32)
    first=core_ref[0]==0
    rows=jnp.concatenate([piece(r,768,8) for r in range(3)],axis=0)
    ten_ref[0:11,:]=jnp.where(first,rows[0:11,0:64],rows[0:11,64:128])
    ten_ref[11:16,:]=jnp.zeros((5,64),f32)
    for v in range(3):
        b=[rows[11+4*v+k:12+4*v+k,:] for k in range(4)]
        three_ref[v:v+1,0:128]=jnp.where(first,b[0],b[2])
        three_ref[v:v+1,128:256]=jnp.where(first,b[1],b[3])
    three_ref[3:8,:]=jnp.zeros((5,256),f32)

def finish(core,sums):
    sd=pltpu.HBM
    shapes=[(64,3072),(64,1024),(64,4096),(256,1024),(16,64),(8,256)]
    return hbm_call(finish_kernel,
        grid_spec=pltpu.PrefetchScalarGridSpec(num_scalar_prefetch=1,grid=(1,),
            in_specs=[pl.BlockSpec(sums.shape,lambda i,c:(0,0,0))],
            out_specs=[pl.BlockSpec(s,lambda i,c:(0,0)) for s in shapes]),
        out_shape=[sd(s,f32) for s in shapes],
        compiler_params=pltpu.CompilerParams(vmem_limit_bytes=40<<20),name="finish",cost_estimate=cost(5))(core,sums)

def pack_kernel(at_ref,*refs):
    *vecs,w_ref,out_ref=refs
    shard=at_ref[0]
    for j in range(3):
        out_ref[64*j:64*j+64,:]=w_ref[:,1024*j:1024*j+1024]
    lane=lax.broadcasted_iota(jnp.int32,(1,1024),1)
    rows=[]
    for r in vecs[:10]:
        v=r[...].astype(f32).reshape(1,-1)
        v=jnp.concatenate([v,v],axis=1)
        rows.append(jnp.where(lane//64==shard,jnp.concatenate([v]*8,axis=1),0.0))
    rows.append(jnp.where(lane//64==shard,jnp.broadcast_to(vecs[10][...].astype(f32).reshape(1,1),(1,1024)),0.0))
    for r in vecs[11:14]:
        v=jnp.concatenate([r[...].astype(f32).reshape(1,-1)]*4,axis=1)
        for j in range(4):
            rows.append(jnp.where(lane//256+4*j==shard,v,0.0))
    rows.append(jnp.zeros((1,1024),f32))
    out_ref[192:216,:]=jnp.concatenate(rows,axis=0).astype(bf16)

def pack_first(shard,vectors,w_qkv):
    full=lambda s:pl.BlockSpec(s,lambda i,c:(0,)*len(s))
    return hbm_call(pack_kernel,
        grid_spec=pltpu.PrefetchScalarGridSpec(num_scalar_prefetch=1,grid=(1,),
            in_specs=[full(v.shape) for v in vectors]+[full(w_qkv.shape)],out_specs=full((216,1024))),
        out_shape=pltpu.HBM((216,1024),bf16),name="pack_first",cost_estimate=cost(2))(shard,*vectors,w_qkv)

T=1152; D=1024
BLOCKS=[(0,256),(256,256),(512,256),(768,256),(1024,128)]


def masked_scores(sT, start_row, q0, bq):
    keys=q0+bq
    kio=lax.broadcasted_iota(jnp.int32,(128,bq),0)
    qio=lax.broadcasted_iota(jnp.int32,(1,bq),1)+q0
    parts=[]
    for k0 in range(0,keys,128):
        t=sT[k0:k0+128]
        ok=None
        if k0==0 or q0>=1024:
            ok=kio>=start_row-k0
        if k0+127>q0:
            low=kio<=qio-k0
            ok=low if ok is None else ok&low
        parts.append(t if ok is None else jnp.where(ok,t,NEG))
    return jnp.concatenate(parts,axis=0) if len(parts)>1 else parts[0]

def fwd_kernel(start_ref,hs_ref,q_ref,k_ref,v_ref,o_ref,c_ref,lse_ref):
    lane=lax.broadcasted_iota(jnp.int32,(1,128),1)
    vT=v_ref[...].T
    oT=[]
    for q0,bq in BLOCKS:
        keys=q0+bq
        k=k_ref[0:keys,:]
        qb=q_ref[q0:q0+bq,:]*jnp.asarray(HD**-0.5,bf16)
        start=start_ref[0:1,q0:q0+bq]
        halves=[]
        for h in range(2):
            qh=jnp.where((lane>=64*h)&(lane<64*h+64),qb,jnp.zeros_like(qb))
            s=masked_scores(dot(k,qh,NT),start,q0,bq)
            m=jnp.max(s,axis=0,keepdims=True)
            e=jnp.exp(s-m)
            l=jnp.sum(e,axis=0,keepdims=True)
            lse_ref[0,h:h+1,q0:q0+bq]=m+jnp.log(l)
            oh=dot(vT[64*h:64*h+64,0:keys],e.astype(bf16))
            halves.append(oh*(1.0/l))
        o=jnp.concatenate(halves,axis=0).T
        o_ref[q0:q0+bq,:]=o
        c_ref[q0:q0+bq,:]=(o*hs_ref[10:11,:]).astype(bf16)

def attn_fwd(proj,start,hs_cols):
    return hbm_call(fwd_kernel,
        grid=(H//2,),
        in_specs=[pl.BlockSpec((1,T),lambda p:(0,0)),pl.BlockSpec((24,128),lambda p:(0,p)),
                  pl.BlockSpec((T,128),lambda p:(0,p)),pl.BlockSpec((T,128),lambda p:(0,8+p)),pl.BlockSpec((T,128),lambda p:(0,16+p))],
        out_specs=[pl.BlockSpec((T,128),lambda p:(0,p)),pl.BlockSpec((T,128),lambda p:(0,p)),pl.BlockSpec((1,2,T),lambda p:(p,0,0))],
        out_shape=[pltpu.HBM((T,D),f32),pltpu.HBM((T,D),bf16),pltpu.HBM((H//2,2,T),f32)],
        compiler_params=pltpu.CompilerParams(vmem_limit_bytes=48<<20),
        name="attn_fwd",cost_estimate=cost(40))(start,hs_cols,proj,proj,proj)

def bwd_kernel(start_ref,lse_ref,o_ref,q_ref,k_ref,v_ref,do_ref,dq_ref,dk_ref,dv_ref,bsum_ref,dk_acc,dv_acc,dqT):
    lane=lax.broadcasted_iota(jnp.int32,(1,128),1)
    scale=jnp.asarray(HD**-0.5,bf16)
    kT=(k_ref[...]*scale).T
    prodT=(o_ref[...]*do_ref[...].astype(f32)).T
    delta=[jnp.sum(prodT[64*h:64*h+64],axis=0,keepdims=True) for h in range(2)]
    dk_acc[...]=jnp.zeros_like(dk_acc)
    dv_acc[...]=jnp.zeros_like(dv_acc)
    for q0,bq in BLOCKS:
        keys=q0+bq
        k=k_ref[0:keys,:]
        v=v_ref[0:keys,:]
        qb=q_ref[q0:q0+bq,:]*scale
        dob=do_ref[q0:q0+bq,:]
        start=start_ref[0:1,q0:q0+bq]
        for h in range(2):
            half=(lane>=64*h)&(lane<64*h+64)
            qh=jnp.where(half,qb,jnp.zeros_like(qb))
            doh=jnp.where(half,dob,jnp.zeros_like(dob))
            s=masked_scores(dot(k,qh,NT),start,q0,bq)
            p=jnp.exp(s-lse_ref[0,h:h+1,q0:q0+bq])
            dp=dot(v,doh,NT)
            ds=(p*(dp-delta[h][:,q0:q0+bq])).astype(bf16)
            dv_acc[0:keys,:]+=dot(p.astype(bf16),doh)
            dk_acc[0:keys,:]+=dot(ds,qh)
            dqT[64*h:64*h+64,q0:q0+bq]=dot(kT[64*h:64*h+64,0:keys],ds)
    dq=dqT[...].T.astype(bf16)
    dk=dk_acc[...].astype(bf16)
    dv=dv_acc[...].astype(bf16)
    dq_ref[...]=dq; dk_ref[...]=dk; dv_ref[...]=dv
    bsum_ref[0:1,:]=jnp.sum(dq.astype(f32),axis=0,keepdims=True)
    bsum_ref[1:2,:]=jnp.sum(dv.astype(f32),axis=0,keepdims=True)

def attn_bwd(proj,start,lse,o,do,half):
    pairs=H//4; at=half*pairs
    blk=lambda off:pl.BlockSpec((T,128),lambda p:(0,off+at+p))
    out=pl.BlockSpec((T,128),lambda p:(0,p))
    return hbm_call(bwd_kernel,
        grid=(pairs,),
        in_specs=[pl.BlockSpec((1,T),lambda p:(0,0)),pl.BlockSpec((1,2,T),lambda p:(at+p,0,0)),blk(0),blk(0),blk(8),blk(16),blk(0)],
        out_specs=[out,out,out,pl.BlockSpec((2,128),lambda p:(0,p))],
        out_shape=[pltpu.HBM((T,D//2),bf16)]*3+[pltpu.HBM((2,D//2),f32)],
        scratch_shapes=[pltpu.VMEM((T,128),f32),pltpu.VMEM((T,128),f32),pltpu.VMEM((128,T),f32)],
        compiler_params=pltpu.CompilerParams(vmem_limit_bytes=48<<20),
        name="attn_bwd",cost_estimate=cost(20))(start,lse,o,proj,proj,proj,do)

EVERY = ("replica", "chip", "core")
SHARD = ("chip", "core")
PEERS = ("replica", "chip")


def exchange(slab, devices):
    return lax.all_to_all(slab.reshape(devices, -1, 128), EVERY, split_axis=0, concat_axis=0, tiled=True).reshape(-1, 128)


def replica_parts(part):
    return lax.all_to_all(part, "replica", split_axis=0, concat_axis=0, tiled=True)


def core_sum(keep, give):
    taken = lax.ppermute(give, "core", [(0, 1), (1, 0)])
    both = keep.astype(f32) + taken.astype(f32)
    return both.astype(bf16).reshape(64, *keep.shape[2:])


def peer_parts(both):
    return lax.all_to_all(both, PEERS, split_axis=0, concat_axis=0, tiled=True)


def on_device(
    tokens, cotangent, lengths, deal_order, inverse, ln1_gain, ln1_bias, w_qkv, b_query, b_value, head_scale, w_out, b_out,
    post_gain, post_bias, ln2_gain, ln2_bias, w_fc1, b_fc1, ffn_gain, ffn_bias, w_fc2, b_fc2,
):
    devices = lax.axis_size(EVERY)
    replicas = lax.axis_size("replica")
    count, width = tokens.shape
    core = lax.axis_index("core").astype(jnp.int32).reshape(1)
    shard = lax.axis_index(SHARD).astype(jnp.int32).reshape(1)
    vectors = [ln1_gain, ln1_bias, b_query, b_value, b_out, post_gain, post_bias, ln2_gain, ln2_bias, b_fc2, head_scale,
               b_fc1, ffn_gain, ffn_bias]
    first = pack_first(shard, vectors, w_qkv)
    pack1 = lax.all_gather(first, SHARD, axis=0)
    recv_keys = deal_order // count * count + jnp.arange(count, dtype=jnp.int32)
    first, tokens = lax.optimization_barrier((first, tokens))
    sent_x = send_rows(tokens, inverse)
    got_x = exchange(sent_x, devices)
    sent_x, w_out, w_fc1, cotangent = lax.optimization_barrier((sent_x, w_out, w_fc1, cotangent))
    packa = lax.all_gather(jnp.concatenate([w_out] + [w_fc1[:, width * j : width * j + width] for j in range(4)], axis=0), SHARD, axis=0)
    packb = lax.all_gather(w_fc2, SHARD, axis=0)
    sent_dy = send_rows(cotangent, inverse)
    sent_dy, got_x, pack1 = lax.optimization_barrier((sent_dy, got_x, pack1))
    got_dy = exchange(sent_dy, devices)
    vec = jnp.sum(pack1[:, 192:216].astype(f32), axis=0)
    places = jnp.arange(count, dtype=jnp.int32)
    starts = jnp.zeros((count,), jnp.int32)
    seq_end = jnp.zeros((), jnp.int32)
    for i in range(lengths.shape[1]):
        seq_end = seq_end + lengths[0, i]
        starts = jnp.where(places >= seq_end, seq_end, starts)
    starts = starts.reshape(1, count)
    x_rows, a, proj = recv_qkv(got_x, recv_keys, vec, pack1)
    o, c, lse = attn_fwd(proj, starts, vec)
    got_dy, c = lax.optimization_barrier((got_dy, c))
    dy_rows = recv_rows(got_dy, recv_keys)
    a2, n, vhat, gp, hres, zhat, stats = up_rows(c, x_rows, vec, packa)
    grads_fc2 = grad_fc2(n, dy_rows)
    grads_fc2, gp = lax.optimization_barrier((grads_fc2, gp))
    part_fc2 = lax.psum_scatter(grads_fc2, SHARD, scatter_dimension=0)
    y, du, gd0, gf = down_rows(n, vhat, gp, stats, dy_rows, hres, vec, packb)
    sent_y = send_rows(y, recv_keys)
    sent_y, du = lax.optimization_barrier((sent_y, du))
    got_y = exchange(sent_y, devices)
    dz, do, dres, gd = back_rows(du, dy_rows, hres, zhat, stats, o, vec, packa)
    grads_up = grad_up(c, dz, a2, du)
    grads_up, do, got_y = lax.optimization_barrier((grads_up, do, got_y))
    grads_up, part_fc2 = lax.optimization_barrier((grads_up, part_fc2))
    part_up = lax.psum_scatter(grads_up, SHARD, scatter_dimension=0)
    parts_fc2 = replica_parts(part_fc2)
    halves1 = attn_bwd(proj, starts, lse, o, do, 0)
    dq1, parts_fc2 = lax.optimization_barrier((halves1[0], parts_fc2))
    both1 = core_sum(*grad_qkv(core, a, dq1, *halves1[1:3]))
    parts1 = peer_parts(both1)
    both1, do = lax.optimization_barrier((both1, do))
    halves2 = attn_bwd(proj, starts, lse, o, do, 1)
    dq2, parts1 = lax.optimization_barrier((halves2[0], parts1))
    dx, gl = dx_rows([dq1, *halves1[1:3], dq2, *halves2[1:3]], x_rows, dres, vec, pack1)
    sent_dx = send_rows(dx, recv_keys)
    sent_dx, gl = lax.optimization_barrier((sent_dx, gl))
    got_dx = exchange(sent_dx, devices)
    both2 = core_sum(*grad_qkv(core, a, dq2, *halves2[1:3], (gl, halves1[3], halves2[3], gd, gd0, gf)))
    both2, got_y = lax.optimization_barrier((both2, got_y))
    output = recv_rows(got_y, inverse)
    both2, got_dx, output = lax.optimization_barrier((both2, got_dx, output))
    parts_up = replica_parts(part_up)
    both2, parts_up = lax.optimization_barrier((both2, parts_up))
    parts2 = peer_parts(both2)
    spread = totals([parts_fc2, parts_up, parts1, parts2])
    sums = lax.all_to_all(spread, "replica", split_axis=0, concat_axis=0, tiled=True)
    grad_tokens = recv_rows(got_dx, inverse)
    g_qkv, g_out, g_fc1, g_fc2, ten, three = finish(core, sums)
    v = [ten[k] for k in range(10)]
    return (
        output, grad_tokens, v[0], v[1], g_qkv, v[2], v[3], jnp.sum(ten[10]).reshape(1), g_out, v[4], v[5], v[6], v[7], v[8], g_fc1,
        three[0], three[1], three[2], g_fc2, v[9],
    )


def solution(mesh):
    replicas, shards = mesh.devices.shape
    mesh = jax.sharding.Mesh(mesh.devices.reshape(replicas, shards // 2, 2), EVERY)
    rows, vector, matrix = P(EVERY, None), P(SHARD), P(SHARD, None)
    in_specs = (
        rows, rows, rows, P(EVERY), P(EVERY), vector, vector, matrix, vector, vector, vector, matrix, vector, vector, vector,
        vector, vector, matrix, vector, vector, vector, matrix, vector,
    )
    out_specs = (
        rows, rows, vector, vector, matrix, vector, vector, vector, matrix, vector, vector, vector, vector, vector, matrix,
        vector, vector, vector, matrix, vector,
    )
    return jax.shard_map(on_device, mesh=mesh, in_specs=in_specs, out_specs=out_specs, check_vma=False)
```

time: 653 us -> 579 us (0.89)
  waiting for transfers between devices: 194 us -> 92.6 us
  Pallas kernels: 299 us -> 346 us
  local copies, waits for them, and re-layouts: 50.4 us -> 11.5 us
  blocking collectives: 23.2 us -> 32.9 us
  starting transfers between devices: 54.9 us -> 61.9 us
    reduce_scatter x2, waiting for transfers between devices: 88.1 us -> 0.02 us  [the longest x1 0.02 us: on_device(): part_fc2 = lax.psum_scatter(grads_fc2, SHARD, scatter_dimension=0)]
    pallas_call x14 -> x22, Pallas kernels: 299 us -> 346 us  [hbm_call(): return lambda *args: call(*[pin(v) for v in args])]
    all_gather x2 -> x3, waiting for transfers between devices: 45.7 us -> 17 us  [the longest x1 14.7 us: on_device(): pack1 = lax.all_gather(first, SHARD, axis=0)]
    unnamed x60 -> x32, local copies, waits for them, and re-layouts: 17 us -> 4.89 us
    all_to_all x7 -> x8, waiting for transfers between devices: 60.5 us -> 71 us  [the longest x4 53.8 us: exchange(): lax.all_to_all(slab.reshape(devices, -1, 128), EVERY, split_axis=0, conca...]
    concatenate x8 -> x1, local copies, waits for them, and re-layouts: 10.3 us -> 0.01 us  [on_device(): jnp.concatenate([w_out] + [w_fc1[:, width * j:width * j + width] for j in...]
    all_to_all x1, blocking collectives: 23.2 us -> 32.9 us  [peer_parts(): return lax.all_to_all(both, PEERS, split_axis=0, concat_axis=0, tiled=True)]
    all_to_all x7 -> x8, starting transfers between devices: 54.6 us -> 61.4 us  [the longest x4 36.1 us: exchange(): lax.all_to_all(slab.reshape(devices, -1, 128), EVERY, split_axis=0, conca...]
  transfers between devices with their start and end apart: 11 -> 15, of which waited for: 8 -> 7; matrix products, arithmetic and copies ran while one was open for 4% -> 3% of each run, Pallas kernels for 26% -> 59%
where the time goes in v3:
time: 579 us; the launch traced here: 574 us
  Pallas kernels  346 us (60%)
  waiting for transfers between devices  92.6 us (16%)
  starting transfers between devices  61.9 us (11%)
  blocking collectives  32.9 us (6%)
  between operations  17.2 us (3%)
  other arithmetic  11.9 us (2%)
  local copies, waits for them, and re-layouts  11.5 us (2%)
    pallas_call x22, Pallas kernels, hbm_call(): return lambda *args: call(*[pin(v) for v in args])  346 us
    all_to_all x4, waiting for transfers between devices, exchange(): lax.all_to_all(slab.reshape(devices, -1, 128), EVERY, split_axis=0, conca...  53.8 us
    all_to_all x4, starting transfers between devices, exchange(): lax.all_to_all(slab.reshape(devices, -1, 128), EVERY, split_axis=0, conca...  36.1 us
    all_to_all x1, blocking collectives, peer_parts(): return lax.all_to_all(both, PEERS, split_axis=0, concat_axis=0, tiled=True)  32.9 us
    all_gather x1, waiting for transfers between devices, on_device(): pack1 = lax.all_gather(first, SHARD, axis=0)  14.7 us
    all_to_all x1, waiting for transfers between devices, on_device(): lax.all_to_all(spread, 'replica', split_axis=0, concat_axis=0, tiled=True)  12.9 us
  transfers between devices with their start and end apart: 15, of which 7 were waited for; matrix products, arithmetic and copies ran while one was open for 3% of the time, Pallas kernels for 59%

profile of v3, /device:TPU:0, one launch (start us, length us, event | category | flops | bytes accessed | tf_op | source)
XLA Modules:
  0.0 573.8 jit_solution(17106552881829014956)
XLA Ops:
  7.2 0.0 all-gather.7.cloned.1.call-start
  7.9 2.1 pack_first.1
  10.0 0.0 all-gather.9.cloned.1.call-start
  10.0 1.3 reshape.135.krow_ref
  11.3 1.7 reshape.153.kcol_ref
  13.1 7.4 %send_rows.4 = bf16[9216,128]{1,0:T(8,128)(2,1)} custom-call(s32[1,1152]{1,0:T(1,128)} %reshape.135.krow_ref, s32[1152,1]{1,0:T(8,128)} %reshape.153.kcol_ref, bf16[1152,1024]{1,0:T(8,128)(2,1)} %x_ref), custom_call_target="tpu_custom_call" | custom-call | bytes 15000000 | tf_op jit(solution)/shard_map/send_rows/pallas_call | solution.py:26
  20.6 0.8 copy-done.9
  21.4 0.0 all-gather.9.cloned.1.call-update
  21.4 0.0 all-gather.11.cloned.1.call-start
  21.5 0.7 all-gather.11.cloned.1.call-update
  22.1 11.2 %all-to-all-start = ((bf16[128,72,128]{2,1,0:T(8,128)(2,1)}), bf16[128,72,128]{2,1,0:T(8,128)(2,1)S(1)}, u32[]{:S(2)}, u32[]{:S(2)}) async-start(bf16[128,72,128]{2,1,0:T(8,128)(2,1)} %bitcast.2), calls=%async_computation | async-start | bytes 4718592 | tf_op jit(solution)/shard_map/all_to_all | solution.py:531
  33.3 7.4 %send_rows.5 = bf16[9216,128]{1,0:T(8,128)(2,1)} custom-call(s32[1,1152]{1,0:T(1,128)} %reshape.135.krow_ref, s32[1152,1]{1,0:T(8,128)} %reshape.153.kcol_ref, bf16[1152,1024]{1,0:T(8,128)(2,1)} %x_ref.1), custom_call_target="tpu_custom_call" | custom-call | bytes 15000000 | tf_op jit(solution)/shard_map/send_rows/pallas_call | solution.py:26
  40.8 28.9 %all-to-all-done = bf16[128,72,128]{2,1,0:T(8,128)(2,1)S(1)} async-done(((bf16[128,72,128]{2,1,0:T(8,128)(2,1)}), bf16[128,72,128]{2,1,0:T(8,128)(2,1)S(1)}, u32[]{:S(2)}, u32[]{:S(2)}) %all-to-all-start) | async-done | bytes 2359328 | tf_op jit(solution)/shard_map/all_to_all | solution.py:531
  69.6 14.7 %all-gather.7.cloned.1.call-done = bf16[3456,1024]{1,0:T(8,128)(2,1)} async-done(((bf16[216,1024]{1,0:T(8,128)(2,1)}), bf16[3456,1024]{1,0:T(8,128)(2,1)}) %all-gather.7.cloned.1.call-update) | async-done | bytes 7077904 | tf_op jit(solution)/shard_map/all_gather | solution.py:560
  84.4 9.4 %all-to-all-start.1 = ((bf16[128,72,128]{2,1,0:T(8,128)(2,1)}), bf16[128,72,128]{2,1,0:T(8,128)(2,1)S(1)}, u32[]{:S(2)}, u32[]{:S(2)}) async-start(bf16[128,72,128]{2,1,0:T(8,128)(2,1)} %bitcast.51), calls=%async_computation.1 | async-start | bytes 4718592 | tf_op jit(solution)/shard_map/all_to_all | solution.py:531
  93.7 0.3 reduce-scatter.3.cloned.1.call-start
  94.0 0.6 reshape.133.krow_ref
  94.6 1.0 reshape.152.kcol_ref
  95.7 0.6 fusion.4
  98.2 1.3 compare_select_fusion.2.start_ref
  99.5 1.9 convert_reduce_fusion.vec_ref.hs_ref.refs_8_
  101.4 19.5 %recv_qkv.1 = (bf16[1152,1024]{1,0:T(8,128)(2,1)}, bf16[1152,1024]{1,0:T(8,128)(2,1)}, bf16[1152,3072]{1,0:T(8,128)(2,1)}) custom-call(s32[1,1152]{1,0:T(1,128)} %reshape.133.krow_ref, s32[1152,1]{1,0:T(8,128)} %reshape.152.kcol_ref, bf16[9216,128]{1,0:T(8,128)(2,1)} %bitcast.55, f32[24,1024]{1,0:T(8,128)} %convert_reduce_fusion.vec_ref.hs_ref.refs_8_, ...), custom_call_target="tpu_custom_call" | custom-call | bytes 54000000 | tf_op jit(solution)/shard_map/recv_qkv/pallas_call | solution.py:26
  120.9 41.5 %attn_fwd.1 = (f32[1152,1024]{1,0:T(8,128)}, bf16[1152,1024]{1,0:T(8,128)(2,1)}, f32[8,2,1152]{2,1,0:T(2,128)}) custom-call(s32[1,1152]{1,0:T(1,128)} %compare_select_fusion.2.start_ref, f32[24,1024]{1,0:T(8,128)} %convert_reduce_fusion.vec_ref.hs_ref.refs_8_, bf16[1152,3072]{1,0:T(8,128)(2,1)} %get-tuple-element.98.q_ref.k_ref.v_ref, ...), custom_call_target="tpu_custom_call" | custom-call | bytes 120000000 | tf_op jit(solution)/shard_map/attn_fwd/pallas_call | solution.py:26
  162.4 1.4 copy-done.2
  163.9 8.6 %recv_rows.3.dy_ref = bf16[1152,1024]{1,0:T(8,128)(2,1)} custom-call(s32[1,1152]{1,0:T(1,128)} %reshape.133.krow_ref, s32[1152,1]{1,0:T(8,128)} %reshape.152.kcol_ref, bf16[9216,128]{1,0:T(8,128)(2,1)} %bitcast.52), custom_call_target="tpu_custom_call" | custom-call | bytes 18000000 | tf_op jit(solution)/shard_map/recv_rows/pallas_call | solution.py:26
  172.5 36.3 %up_rows.1 = (bf16[1152,1024]{1,0:T(8,128)(2,1)}, bf16[1152,4096]{1,0:T(8,128)(2,1)}, bf16[1152,4096]{1,0:T(8,128)(2,1)}, bf16[1152,4096]{1,0:T(8,128)(2,1)}, f3...) custom-call(bf16[1152,1024]{1,0:T(8,128)(2,1)} %get-tuple-element.103.c_ref, ...), custom_call_target="tpu_custom_call" | custom-call | bytes 135000000 | tf_op jit(solution)/shard_map/up_rows/pallas_call | solution.py:26
  208.8 15.5 %grad_fc2.1 = bf16[16,8,256,128]{3,2,1,0:T(8,128)(2,1)} custom-call(bf16[1152,4096]{1,0:T(8,128)(2,1)} %get-tuple-element.107.n_ref, bf16[1152,1024]{1,0:T(8,128)(2,1)} %recv_rows.3.dy_ref), custom_call_target="tpu_custom_call" | custom-call | bytes 42000000 | tf_op jit(solution)/shard_map/grad_fc2/pallas_call | solution.py:26
  224.3 0.0 reduce-scatter.3.cloned.1.call-update
  224.4 2.3 all-gather.11.cloned.1.call-done
  226.6 47.2 %down_rows.1 = (bf16[1152,1024]{1,0:T(8,128)(2,1)}, bf16[1152,4096]{1,0:T(8,128)(2,1)}, f32[8,1024]{1,0:T(8,128)}, f32[16,1024]{1,0:T(8,128)}) custom-call(bf16[1152,4096]{1,0:T(8,128)(2,1)} %get-tuple-element.107.n_ref, bf16[1152,4096]{1,0:T(8,128)(2,1)} %get-tuple-element.108.vhat_ref, bf16[1152,4096]{1,0:T(8,128)(2,1)} %get-tuple-element.111.gp_ref, ...), custom_call_target="tpu_custom_call" | custom-call | bytes 120000000 | tf_op jit(solution)/shard_map/down_rows/pallas_call | solution.py:26
  273.8 7.6 %send_rows.6 = bf16[9216,128]{1,0:T(8,128)(2,1)} custom-call(s32[1,1152]{1,0:T(1,128)} %reshape.133.krow_ref, s32[1152,1]{1,0:T(8,128)} %reshape.152.kcol_ref, bf16[1152,1024]{1,0:T(8,128)(2,1)} %get-tuple-element.114.x_ref), custom_call_target="tpu_custom_call" | custom-call | bytes 15000000 | tf_op jit(solution)/shard_map/send_rows/pallas_call | solution.py:26
  281.4 9.7 %all-to-all-start.2 = ((bf16[128,72,128]{2,1,0:T(8,128)(2,1)}), bf16[128,72,128]{2,1,0:T(8,128)(2,1)S(1)}, u32[]{:S(2)}, u32[]{:S(2)}) async-start(bf16[128,72,128]{2,1,0:T(8,128)(2,1)} %bitcast.54), calls=%async_computation.2 | async-start | bytes 4718592 | tf_op jit(solution)/shard_map/all_to_all | solution.py:531
  291.1 0.0 reduce-scatter.5.cloned.1.call-start
  291.1 26.2 %back_rows.1 = (bf16[1152,1024]{1,0:T(8,128)(2,1)}, bf16[1152,1024]{1,0:T(8,128)(2,1)}, f32[1152,1024]{1,0:T(8,128)}, f32[8,1024]{1,0:T(8,128)}) custom-call(bf16[1152,4096]{1,0:T(8,128)(2,1)} %get-tuple-element.116.du_ref, bf16[1152,1024]{1,0:T(8,128)(2,1)} %recv_rows.3.dy_ref, f32[1152,1024]{1,0:T(8,128)} %get-tuple-element.113.hres_ref, ...), custom_call_target="tpu_custom_call" | custom-call | bytes 75000000 | tf_op jit(solution)/shard_map/back_rows/pallas_call | solution.py:26
  317.3 20.9 %grad_up.1 = bf16[16,8,320,128]{3,2,1,0:T(8,128)(2,1)} custom-call(bf16[1152,1024]{1,0:T(8,128)(2,1)} %get-tuple-element.103.c_ref, bf16[1152,1024]{1,0:T(8,128)(2,1)} %get-tuple-element.118.dz_ref, bf16[1152,1024]{1,0:T(8,128)(2,1)} %get-tuple-element.119.a2_ref, bf16[1152,4096]{1,0:T(8,128)(2,1)} %get-tuple-element.116.du_ref), custom_call_target="tpu_custom_call" | custom-call | bytes 60000000 | tf_op jit(solution)/shard_map/grad_up/pallas_call | solution.py:26
  338.2 0.0 reduce-scatter.3.cloned.1.call-done
  338.2 0.0 reduce-scatter.5.cloned.1.call-update
  338.2 1.3 copy-done
  339.6 6.4 %all-to-all-start.3 = ((bf16[8,256,128]{2,1,0:T(8,128)(2,1)}), bf16[8,256,128]{2,1,0:T(8,128)(2,1)S(1)}, u32[]{:S(2)}, u32[]{:S(2)}) async-start(bf16[8,256,128]{2,1,0:T(8,128)(2,1)} %bitcast.59), calls=%async_computation.4 | async-start | bytes 1048576 | tf_op jit(solution)/shard_map/all_to_all | solution.py:535
  346.0 20.6 %attn_bwd.2 = (bf16[1152,512]{1,0:T(8,128)(2,1)}, bf16[1152,512]{1,0:T(8,128)(2,1)}, bf16[1152,512]{1,0:T(8,128)(2,1)}, f32[2,512]{1,0:T(2,128)}) custom-call(s32[1,1152]{1,0:T(1,128)} %compare_select_fusion.2.start_ref, f32[8,2,1152]{2,1,0:T(2,128)} %get-tuple-element.99.lse_ref, f32[1152,1024]{1,0:T(8,128)} %get-tuple-element.100.o_ref, ...), custom_call_target="tpu_custom_call" | custom-call | bytes 60000000 | tf_op jit(solution)/shard_map/attn_bwd/pallas_call | solution.py:26
  366.6 8.4 %grad_qkv.2 = (bf16[8,8,96,128]{3,2,1,0:T(8,128)(2,1)}, bf16[8,8,96,128]{3,2,1,0:T(8,128)(2,1)}) custom-call(s32[1]{0:T(128)} %bitcast.core_ref, bf16[1152,1024]{1,0:T(8,128)(2,1)} %get-tuple-element.97.a_ref, bf16[1152,512]{1,0:T(8,128)(2,1)} %get-tuple-element.127.dq_ref.refs_0_, bf16[1152,512]{1,0:T(8,128)(2,1)} %get-tuple-element.128.dk_ref.refs_1_, ...), custom_call_target="tpu_custom_call" | custom-call | bytes 24000000 | tf_op jit(solution)/shard_map/grad_qkv/pallas_call | solution.py:26
  375.1 3.7 collective-permute-done
  378.8 3.1 add_convert_fusion.1
  381.9 11.5 %all-to-all-start.4 = ((bf16[64,96,128]{2,1,0:T(8,128)(2,1)}), bf16[64,96,128]{2,1,0:T(8,128)(2,1)S(1)}, u32[]{:S(2)}, u32[]{:S(2)}) async-start(bf16[64,96,128]{2,1,0:T(8,128)(2,1)} %bitcast.15), calls=%async_computation.5 | async-start | bytes 3145728 | tf_op jit(solution)/shard_map/all_to_all | solution.py:545
  393.4 20.5 %attn_bwd.3 = (bf16[1152,512]{1,0:T(8,128)(2,1)}, bf16[1152,512]{1,0:T(8,128)(2,1)}, bf16[1152,512]{1,0:T(8,128)(2,1)}, f32[2,512]{1,0:T(2,128)}) custom-call(s32[1,1152]{1,0:T(1,128)} %compare_select_fusion.2.start_ref, f32[8,2,1152]{2,1,0:T(2,128)} %get-tuple-element.99.lse_ref, f32[1152,1024]{1,0:T(8,128)} %get-tuple-element.100.o_ref, ...), custom_call_target="tpu_custom_call" | custom-call | bytes 60000000 | tf_op jit(solution)/shard_map/attn_bwd/pallas_call | solution.py:26
  413.9 4.4 all-to-all-done.4.refs_2_
  418.2 15.9 %dx_rows.1 = (bf16[1152,1024]{1,0:T(8,128)(2,1)}, f32[8,1024]{1,0:T(8,128)}) custom-call(bf16[1152,512]{1,0:T(8,128)(2,1)} %get-tuple-element.127.dq_ref.refs_0_, bf16[1152,512]{1,0:T(8,128)(2,1)} %get-tuple-element.128.dk_ref.refs_1_, bf16[1152,512]{1,0:T(8,128)(2,1)} %get-tuple-element.129.dv_ref.refs_2_, ...), custom_call_target="tpu_custom_call" | custom-call | bytes 42000000 | tf_op jit(solution)/shard_map/dx_rows/pallas_call | solution.py:26
  434.1 7.4 %send_rows.7 = bf16[9216,128]{1,0:T(8,128)(2,1)} custom-call(s32[1,1152]{1,0:T(1,128)} %reshape.133.krow_ref, s32[1152,1]{1,0:T(8,128)} %reshape.152.kcol_ref, bf16[1152,1024]{1,0:T(8,128)(2,1)} %get-tuple-element.138.x_ref), custom_call_target="tpu_custom_call" | custom-call | bytes 15000000 | tf_op jit(solution)/shard_map/send_rows/pallas_call | solution.py:26
  441.5 5.9 %all-to-all-start.5 = ((bf16[128,72,128]{2,1,0:T(8,128)(2,1)}), bf16[128,72,128]{2,1,0:T(8,128)(2,1)S(1)}, u32[]{:S(2)}, u32[]{:S(2)}) async-start(bf16[128,72,128]{2,1,0:T(8,128)(2,1)} %bitcast.53), calls=%async_computation.6 | async-start | bytes 4718592 | tf_op jit(solution)/shard_map/all_to_all | solution.py:531
  447.4 8.4 %grad_qkv.3 = (bf16[8,8,104,128]{3,2,1,0:T(8,128)(2,1)}, bf16[8,8,104,128]{3,2,1,0:T(8,128)(2,1)}) custom-call(s32[1]{0:T(128)} %bitcast.core_ref, bf16[1152,1024]{1,0:T(8,128)(2,1)} %get-tuple-element.97.a_ref, bf16[1152,512]{1,0:T(8,128)(2,1)} %get-tuple-element.134.refs_3_.dq_ref, bf16[1152,512]{1,0:T(8,128)(2,1)} %get-tuple-element.135.refs_4_.dk_ref, ...), custom_call_target="tpu_custom_call" | custom-call | bytes 24000000 | tf_op jit(solution)/shard_map/grad_qkv/pallas_call | solution.py:26
  455.8 0.1 collective-permute-start.1
  455.9 24.9 %all-to-all-done.5 = bf16[128,72,128]{2,1,0:T(8,128)(2,1)S(1)} async-done(((bf16[128,72,128]{2,1,0:T(8,128)(2,1)}), bf16[128,72,128]{2,1,0:T(8,128)(2,1)S(1)}, u32[]{:S(2)}, u32[]{:S(2)}) %all-to-all-start.5) | async-done | bytes 2359328 | tf_op jit(solution)/shard_map/all_to_all | solution.py:531
  480.8 3.8 all-to-all-start.6
  484.7 3.6 add_convert_fusion
  488.3 8.7 %recv_rows.4 = bf16[1152,1024]{1,0:T(8,128)(2,1)} custom-call(s32[1,1152]{1,0:T(1,128)} %reshape.135.krow_ref, s32[1152,1]{1,0:T(8,128)} %reshape.153.kcol_ref, bf16[9216,128]{1,0:T(8,128)(2,1)} %bitcast.49), custom_call_target="tpu_custom_call" | custom-call | bytes 18000000 | tf_op jit(solution)/shard_map/recv_rows/pallas_call | solution.py:26
  497.0 32.9 %all_to_all.45.refs_3_ = bf16[64,104,128]{2,1,0:T(8,128)(2,1)} all-to-all(bf16[64,104,128]{2,1,0:T(8,128)(2,1)S(1)} %bitcast.57), channel_id=1, replica_groups=mesh['replica'=8,'chip'=8,'core'=2] {'replica','chip'}, dimensions={0} | all-to-all | bytes 3407872 | tf_op jit(solution)/shard_map/all_to_all | solution.py:545
  529.9 4.1 totals.1
  533.9 3.6 all-to-all-start.8
  537.5 8.6 %recv_rows.5 = bf16[1152,1024]{1,0:T(8,128)(2,1)} custom-call(s32[1,1152]{1,0:T(1,128)} %reshape.135.krow_ref, s32[1152,1]{1,0:T(8,128)} %reshape.153.kcol_ref, bf16[9216,128]{1,0:T(8,128)(2,1)} %bitcast.50), custom_call_target="tpu_custom_call" | custom-call | bytes 18000000 | tf_op jit(solution)/shard_map/recv_rows/pallas_call | solution.py:26
  546.1 12.9 %all-to-all-done.8.s_ref = bf16[8,776,128]{2,1,0:T(8,128)(2,1)S(1)} async-done(((bf16[8,776,128]{2,1,0:T(8,128)(2,1)}), bf16[8,776,128]{2,1,0:T(8,128)(2,1)S(1)}, u32[]{:S(2)}, u32[]{:S(2)}) %all-to-all-start.8) | async-done | bytes 1589280 | tf_op jit(solution)/shard_map/all_to_all | solution.py:616
  559.0 1.2 copy-done.5
  560.2 3.1 finish.1
  563.3 2.1 slice_bitcast_fusion
  565.4 1.4 fusion.3
  (39 shorter events, 0.2 us)
Async XLA Ops:
  7.2 77.2 %all-gather.7.cloned.1.call-start = ((), (), s32[]{:S(2)}) async-start(), calls=%async_computation.13 | async-start | bytes 7520256 | tf_op jit(solution)/shard_map/all_gather | solution.py:560
  10.0 162.5 %all-gather.9.cloned.1.call-start = ((), (), s32[]{:S(2)}) async-start(), calls=%async_computation.14 | async-start | bytes 11141120 | tf_op jit(solution)/shard_map/all_gather | solution.py:566
  13.1 7.4 %copy-start.11 = (bf16[64,1024]{1,0:T(8,128)(2,1)S(1)}, bf16[64,1024]{1,0:T(8,128)(2,1)}, u32[]{:S(2)}) copy-start(bf16[64,1024]{1,0:T(8,128)(2,1)} %param.34) | copy-start | bytes 393220
  13.1 7.4 %copy-start.10 = (bf16[64,4096]{1,0:T(8,128)(2,1)S(1)}, bf16[64,4096]{1,0:T(8,128)(2,1)}, u32[]{:S(2)}) copy-start(bf16[64,4096]{1,0:T(8,128)(2,1)} %param.40) | copy-start | bytes 1572868
  20.5 0.8 copy-start.9
  21.4 205.2 %all-gather.11.cloned.1.call-start = ((), (), s32[]{:S(2)}) async-start(), calls=%async_computation.15 | async-start | bytes 8912896 | tf_op jit(solution)/shard_map/all_gather | solution.py:567
  22.1 47.5 %all-to-all-start = ((bf16[128,72,128]{2,1,0:T(8,128)(2,1)}), bf16[128,72,128]{2,1,0:T(8,128)(2,1)S(1)}, u32[]{:S(2)}, u32[]{:S(2)}) async-start(bf16[128,72,128]{2,1,0:T(8,128)(2,1)} %bitcast.2), calls=%async_computation | async-start | bytes 4718592 | tf_op jit(solution)/shard_map/all_to_all | solution.py:531
  69.6 14.7 %copy-start.3 = (bf16[128,72,128]{2,1,0:T(8,128)(2,1)}, bf16[128,72,128]{2,1,0:T(8,128)(2,1)S(1)}, u32[]{:S(2)}) copy-start(bf16[128,72,128]{2,1,0:T(8,128)(2,1)S(1)} %all-to-all-done) | copy-start | bytes 7077892
  84.3 9.7 %copy-start.12 = (s32[1152]{0:T(1024)S(1)}, s32[1152]{0:T(1024)}, u32[]{:S(2)}) copy-start(s32[1152]{0:T(1024)} %param.26) | copy-start | bytes 13828
  84.3 11.3 %copy-start.13 = (s32[1,3]{1,0:T(1,128)S(1)}, s32[1,3]{1,0:T(1,128)}, u32[]{:S(2)}) copy-start(s32[1,3]{1,0:T(1,128)} %param.25) | copy-start | bytes 40
  84.4 78.1 %all-to-all-start.1 = ((bf16[128,72,128]{2,1,0:T(8,128)(2,1)}), bf16[128,72,128]{2,1,0:T(8,128)(2,1)S(1)}, u32[]{:S(2)}, u32[]{:S(2)}) async-start(bf16[128,72,128]{2,1,0:T(8,128)(2,1)} %bitcast.51), calls=%async_computation.1 | async-start | bytes 4718592 | tf_op jit(solution)/shard_map/all_to_all | solution.py:531
  93.7 244.5 %reduce-scatter.3.cloned.1.call-start = ((), (), s32[]{:S(2)}) async-start(), calls=%async_computation.11 | async-start | bytes 8912896 | tf_op jit(solution)/shard_map/reduce_scatter | solution.py:586
  162.4 1.4 copy-start.2
  281.4 56.8 %all-to-all-start.2 = ((bf16[128,72,128]{2,1,0:T(8,128)(2,1)}), bf16[128,72,128]{2,1,0:T(8,128)(2,1)S(1)}, u32[]{:S(2)}, u32[]{:S(2)}) async-start(bf16[128,72,128]{2,1,0:T(8,128)(2,1)} %bitcast.54), calls=%async_computation.2 | async-start | bytes 4718592 | tf_op jit(solution)/shard_map/all_to_all | solution.py:531
  291.1 189.7 %reduce-scatter.5.cloned.1.call-start = ((), (), s32[]{:S(2)}) async-start(), calls=%async_computation.12 | async-start | bytes 11141120 | tf_op jit(solution)/shard_map/reduce_scatter | solution.py:595
  338.2 1.4 copy-start
  339.6 27.0 %all-to-all-start.3 = ((bf16[8,256,128]{2,1,0:T(8,128)(2,1)}), bf16[8,256,128]{2,1,0:T(8,128)(2,1)S(1)}, u32[]{:S(2)}, u32[]{:S(2)}) async-start(bf16[8,256,128]{2,1,0:T(8,128)(2,1)} %bitcast.59), calls=%async_computation.4 | async-start | bytes 1048576 | tf_op jit(solution)/shard_map/all_to_all | solution.py:535
  366.6 8.4 %copy-start.8 = (bf16[8,256,128]{2,1,0:T(8,128)(2,1)}, bf16[8,256,128]{2,1,0:T(8,128)(2,1)S(1)}, u32[]{:S(2)}) copy-start(bf16[8,256,128]{2,1,0:T(8,128)(2,1)S(1)} %all-to-all-done.3.refs_0_) | copy-start | bytes 1572868
  375.1 3.7 collective-permute-start
  381.9 36.4 %all-to-all-start.4 = ((bf16[64,96,128]{2,1,0:T(8,128)(2,1)}), bf16[64,96,128]{2,1,0:T(8,128)(2,1)S(1)}, u32[]{:S(2)}, u32[]{:S(2)}) async-start(bf16[64,96,128]{2,1,0:T(8,128)(2,1)} %bitcast.15), calls=%async_computation.5 | async-start | bytes 3145728 | tf_op jit(solution)/shard_map/all_to_all | solution.py:545
  418.2 15.9 %copy-start.6 = (bf16[64,96,128]{2,1,0:T(8,128)(2,1)}, bf16[64,96,128]{2,1,0:T(8,128)(2,1)S(1)}, u32[]{:S(2)}) copy-start(bf16[64,96,128]{2,1,0:T(8,128)(2,1)S(1)} %all-to-all-done.4.refs_2_) | copy-start | bytes 4718596
  441.5 39.3 %all-to-all-start.5 = ((bf16[128,72,128]{2,1,0:T(8,128)(2,1)}), bf16[128,72,128]{2,1,0:T(8,128)(2,1)S(1)}, u32[]{:S(2)}, u32[]{:S(2)}) async-start(bf16[128,72,128]{2,1,0:T(8,128)(2,1)} %bitcast.53), calls=%async_computation.6 | async-start | bytes 4718592 | tf_op jit(solution)/shard_map/all_to_all | solution.py:531
  455.8 28.9 %collective-permute-start.1 = (bf16[8,8,104,128]{3,2,1,0:T(8,128)(2,1)}, bf16[8,8,104,128]{3,2,1,0:T(8,128)(2,1)}, u32[]{:S(2)}, u32[]{:S(2)}) collective-permute-start(bf16[8,8,104,128]{3,2,1,0:T(8,128)(2,1)} %get-tuple-element.147), channel_id=1, source_target_pairs={{0,1},{1,0},{2,3},{3,2},{4,5},{5,4},{6,7},{7,6},{8,9},{9,8},{10,11... | collective-permute-start | bytes 5111816 | tf_op jit(solution)/shard_map/ppermute | solution.py:539
  480.8 7.5 %copy-start.1 = (bf16[128,72,128]{2,1,0:T(8,128)(2,1)}, bf16[128,72,128]{2,1,0:T(8,128)(2,1)S(1)}, u32[]{:S(2)}) copy-start(bf16[128,72,128]{2,1,0:T(8,128)(2,1)S(1)} %all-to-all-done.5) | copy-start | bytes 7077892
  480.8 16.1 %all-to-all-start.6 = ((bf16[8,320,128]{2,1,0:T(8,128)(2,1)}), bf16[8,320,128]{2,1,0:T(8,128)(2,1)S(1)}, u32[]{:S(2)}, u32[]{:S(2)}) async-start(bf16[8,320,128]{2,1,0:T(8,128)(2,1)} %bitcast.58), calls=%async_computation.8 | async-start | bytes 1310720 | tf_op jit(solution)/shard_map/all_to_all | solution.py:535
  488.3 8.7 %copy-start.4 = (bf16[8,8,104,128]{3,2,1,0:T(8,128)(2,1)S(1)}, bf16[8,8,104,128]{3,2,1,0:T(8,128)(2,1)}, u32[]{:S(2)}) copy-start(bf16[8,8,104,128]{3,2,1,0:T(8,128)(2,1)} %add_convert_fusion) | copy-start | bytes 5111812
  496.9 32.9 %copy-start.7 = (bf16[8,320,128]{2,1,0:T(8,128)(2,1)}, bf16[8,320,128]{2,1,0:T(8,128)(2,1)S(1)}, u32[]{:S(2)}) copy-start(bf16[8,320,128]{2,1,0:T(8,128)(2,1)S(1)} %all-to-all-done.6.refs_1_) | copy-start | bytes 1966084
  533.9 25.0 %all-to-all-start.8 = ((bf16[8,776,128]{2,1,0:T(8,128)(2,1)}), bf16[8,776,128]{2,1,0:T(8,128)(2,1)S(1)}, u32[]{:S(2)}, u32[]{:S(2)}) async-start(bf16[8,776,128]{2,1,0:T(8,128)(2,1)} %totals.1), calls=%async_computation.10 | async-start | bytes 3178496 | tf_op jit(solution)/shard_map/all_to_all | solution.py:616
  559.0 1.2 copy-start.5
Sparse Core Ops, SparseCore 0:
  10.3 73.9 all-gather.6
  86.6 85.1 all-gather.8
  173.5 53.0 all-gather.10
  228.9 100.2 reduce-scatter.2
  338.4 100.5 reduce-scatter.4

commit v4 on v3

--- a/solution.py
+++ b/solution.py
@@ -80,6 +80,54 @@
         out_shape=pltpu.HBM((t,d),bf16),
         scratch_shapes=[pltpu.VMEM((384*8,128),f32),pltpu.VMEM((t,d),bf16)],
         compiler_params=pltpu.CompilerParams(vmem_limit_bytes=40<<20),name="recv_rows",cost_estimate=cost(6))(keys.reshape(1,t),keys.reshape(t,1),got)
+
+def send_more_kernel(krow_ref,kcol_ref,x_ref,more_ref,out_ref,rank_ref,wide_ref):
+    i=pl.program_id(0); slabs=out_ref.shape[0]; bs=slabs*9
+    @pl.when(i==0)
+    def _(): rank_ref[...]=rank_row(kcol_ref[...],krow_ref[...])
+    t=rank_ref.shape[1]
+    pick=(lax.broadcasted_iota(jnp.int32,(bs,t),0)+i*bs==rank_ref[...]).astype(f32).astype(bf16)
+    rows=dot(pick,x_ref[...])
+    for k in range(8):
+        wide_ref[pl.ds(k,bs,stride=8),:]=rows[:,128*k:128*k+128]
+    out_ref[:,0:72,:]=wide_ref[...].astype(bf16).reshape(slabs,72,128)
+    more=more_ref[...].astype(bf16)
+    for d in range(slabs):
+        chip=d%16//2
+        out_ref[d,72:80,:]=more[:,128*chip:128*chip+128]
+
+def send_more(x,keys,more,blocks=4):
+    t,d=x.shape; bs=t//blocks
+    full=lambda s:pl.BlockSpec(s,lambda i:(0,0))
+    return hbm_call(send_more_kernel,grid=(blocks,),
+        in_specs=[full((1,t)),full((t,1)),full((t,d)),full((8,d))],
+        out_specs=pl.BlockSpec((bs//9,80,128),lambda i:(i,0,0)),
+        out_shape=pltpu.HBM((t//9,80,128),bf16),
+        scratch_shapes=[pltpu.VMEM((1,t),jnp.int32),pltpu.VMEM((bs*8,128),f32)],
+        compiler_params=pltpu.CompilerParams(vmem_limit_bytes=40<<20),name="send_more",cost_estimate=cost(5))(keys.reshape(1,t),keys.reshape(t,1),x,more)
+
+def recv_more_kernel(krow_ref,kcol_ref,got_ref,out_ref,more_ref,wide_ref,rows_ref):
+    i=pl.program_id(0); bs=out_ref.shape[0]; t=rows_ref.shape[0]
+    @pl.when(i==0)
+    def _():
+        for c in range(0,t,288):
+            wide_ref[...]=got_ref[c//9:c//9+32,0:72,:].reshape(288*8,128).astype(f32)
+            for k in range(8):
+                rows_ref[c:c+288,128*k:128*k+128]=wide_ref[pl.ds(k,288,stride=8),:].astype(bf16)
+        more_ref[...]=jnp.sum(got_ref[:,72:80,:].astype(f32),axis=0)
+    rank=rank_col(krow_ref[...],kcol_ref[...])
+    pick=(lax.broadcasted_iota(jnp.int32,(bs,t),1)==rank).astype(f32).astype(bf16)
+    out_ref[...]=dot(pick,rows_ref[...]).astype(bf16)
+
+def recv_more(got,keys,blocks=3):
+    t=got.shape[0]*9; d=1024; bs=t//blocks
+    full=lambda s:pl.BlockSpec(s,lambda i:(0,)*len(s))
+    return hbm_call(recv_more_kernel,grid=(blocks,),
+        in_specs=[full((1,t)),pl.BlockSpec((bs,1),lambda i:(i,0)),full(got.shape)],
+        out_specs=[pl.BlockSpec((bs,d),lambda i:(i,0)),full((8,128))],
+        out_shape=[pltpu.HBM((t,d),bf16),pltpu.HBM((8,128),f32)],
+        scratch_shapes=[pltpu.VMEM((288*8,128),f32),pltpu.VMEM((t,d),bf16)],
+        compiler_params=pltpu.CompilerParams(vmem_limit_bytes=40<<20),name="recv_more",cost_estimate=cost(6))(keys.reshape(1,t),keys.reshape(t,1),got)
 
 def norm_parts(v):
     m=jnp.mean(v,axis=-1,keepdims=True); c=v-m
@@ -160,7 +208,7 @@
     full=lambda s,**k:pl.BlockSpec(s,lambda i:(0,)*len(s),**k)
     return row,full
 
-def up_rows(c,x,vec,packa,bm=192):
+def up_rows(c,x,vec,packa,bm=384):
     t,d=c.shape
     row,full=row_specs(bm); sd=pltpu.HBM
     return hbm_call(up_kernel,grid=(t//bm,),
@@ -177,15 +225,13 @@
     vec=lambda k:vec_ref[k:k+1,:]
     rf=st_ref[:,1:2]
     dy=dy_ref[...]
-    y=hres_ref[...]+vec(9)
+    w=lambda j:w_ref[4*j:4*j+4].reshape(1024,1024)
     s1=0.0; s2=0.0
+    dn=dot(dy,w(0),NT)
     for j in range(4):
         cols=slice(1024*j,1024*j+1024)
-        w=w_ref[4*j:4*j+4].reshape(1024,1024)
-        y=y+dot(n_ref[:,cols],w)
-        dn=dot(dy,w,NT)
-        vhat=vhat_ref[:,cols].astype(f32)
-        dv=dn*vhat
+        ahead=dot(dy,w(j+1),NT) if j<3 else None
+        dv=dn*vhat_ref[:,cols].astype(f32)
         gf_ref[j:j+1,:]+=colsum(dv)
         gf_ref[4+j:5+j,:]+=colsum(dn)
         gain=vec(15+j)
@@ -193,16 +239,19 @@
         e_s[:,cols]=e
         s1=s1+jnp.sum(e,axis=-1,keepdims=True)
         s2=s2+jnp.sum(dv*gain,axis=-1,keepdims=True)
-    y_ref[...]=y.astype(bf16)
-    s1=s1*(1.0/FF); s2=s2*(1.0/FF)
+        dn=ahead
+    s1=rf*s1*(1.0/FF); s2=rf*s2*(1.0/FF)
+    y=hres_ref[...]+vec(9)
     for j in range(4):
         cols=slice(1024*j,1024*j+1024)
-        du=(gp_ref[:,cols].astype(f32)*(rf*(e_s[:,cols]-s1-vhat_ref[:,cols].astype(f32)*s2))).astype(bf16)
-        du_ref[:,cols]=du
-        gf_ref[8+j:9+j,:]+=colsum(du.astype(f32))
+        y=y+dot(n_ref[:,cols],w(j))
+        du=gp_ref[:,cols].astype(f32)*(rf*e_s[:,cols]-s1-vhat_ref[:,cols].astype(f32)*s2)
+        du_ref[:,cols]=du.astype(bf16)
+        gf_ref[8+j:9+j,:]+=colsum(du)
+    y_ref[...]=y.astype(bf16)
     gd_ref[0:1,:]+=colsum(dy.astype(f32))
 
-def down_rows(n,vhat,gp,st,dy,hres,vec,packb,bm=192):
+def down_rows(n,vhat,gp,st,dy,hres,vec,packb,bm=288):
     t,d=dy.shape
     row,full=row_specs(bm); sd=pltpu.HBM
     return hbm_call(down_kernel,grid=(t//bm,),
@@ -234,7 +283,7 @@
     gd_ref[6:7,:]+=colsum(dc*o_ref[...])
     do_ref[...]=(dc*vec(10)).astype(bf16)
 
-def back_rows(du,dy,hres,zhat,st,o,vec,packa,bm=384):
+def back_rows(du,dy,hres,zhat,st,o,vec,packa,bm=288):
     t,d=dy.shape
     row,full=row_specs(bm); sd=pltpu.HBM
     return hbm_call(back_kernel,grid=(t//bm,),
@@ -280,24 +329,29 @@
         out_shape=pltpu.HBM((16,8,256,128),bf16),
         compiler_params=pltpu.CompilerParams(vmem_limit_bytes=48<<20),name="grad_fc2",cost_estimate=cost(14))(n,dy)
 
-def grad_up_kernel(c_ref,dz_ref,a2_ref,du_ref,out_ref):
-    def put(res,at):
+def grad_up_kernel(c_ref,dz_ref,a2_ref,du_ref,out_ref,left):
+    i=pl.program_id(0)
+    def put(res):
         res=res.astype(bf16)
-        for f in range(4):
+        for f in range(16):
             for r in range(8):
-                out_ref[f,r,at:at+64,:]=res[64*f:64*f+64,128*r:128*r+128]
-    put(dot(c_ref[...],dz_ref[...],TN),0)
-    for j in range(4):
-        put(dot(a2_ref[...],du_ref[:,1024*j:1024*j+1024],TN),64+64*j)
+                out_ref[f,r]=res[64*f:64*f+64,128*r:128*r+128]
+    @pl.when(i==0)
+    def _():
+        left[...]=c_ref[...].T
+        put(dot(left[...],dz_ref[...]))
+        left[...]=a2_ref[...].T
+    @pl.when(i>0)
+    def _(): put(dot(left[...],du_ref[...]))
 
 def grad_up(c,dz,a2,du):
     t,d=c.shape
-    col=pl.BlockSpec((t,256),lambda i:(0,i))
-    full=lambda s:pl.BlockSpec(s,lambda i:(0,0),pipeline_mode=pl.Buffered(1))
-    return hbm_call(grad_up_kernel,grid=(4,),
-        in_specs=[col,full((t,d)),col,full((t,FF))],
-        out_specs=pl.BlockSpec((4,8,320,128),lambda i:(i,0,0,0)),
+    full=pl.BlockSpec((t,d),lambda i:(0,0),pipeline_mode=pl.Buffered(1))
+    return hbm_call(grad_up_kernel,grid=(5,),
+        in_specs=[full,full,full,pl.BlockSpec((t,1024),lambda i:(0,jnp.maximum(i-1,0)))],
+        out_specs=pl.BlockSpec((16,8,64,128),lambda i:(0,0,i,0)),
         out_shape=pltpu.HBM((16,8,320,128),bf16),
+        scratch_shapes=[pltpu.VMEM((d,t),bf16)],
         compiler_params=pltpu.CompilerParams(vmem_limit_bytes=56<<20),name="grad_up",cost_estimate=cost(20))(c,dz,a2,du)
 
 def grad_qkv_kernel(core_ref,a_ref,dq_ref,dk_ref,dv_ref,*refs):
@@ -316,12 +370,12 @@
                     keep_ref[q//3,chip,at:at+32,:]=mine[32*h:32*h+32,128*l:128*l+128]
                     give_ref[q//3,chip,at:at+32,:]=other[32*h:32*h+32,128*l:128*l+128]
     if vecs:
-        gl_ref,b1_ref,b2_ref,gd_ref,gd0_ref,gf_ref=vecs
+        b1_ref,b2_ref,gd_ref,gd0_ref,gf_ref=vecs
         for chip in range(2):
             cols=slice(128*chip,128*chip+128)
             half=jnp.where(i<2,b1_ref[:,cols],b2_ref[:,cols])
             line=lambda ref,k:ref[k:k+1,cols]
-            ten=[gl_ref[0:2,cols],half,line(gd_ref,5),gd_ref[3:5,cols],gd_ref[1:3,cols],line(gd0_ref,0),line(gd_ref,6)]
+            ten=[jnp.zeros((2,128),f32),half,line(gd_ref,5),gd_ref[3:5,cols],gd_ref[1:3,cols],line(gd0_ref,0),line(gd_ref,6)]
             pick=lambda v,at:sum(jnp.where(i==k,gf_ref[4*v+k:4*v+k+1,at:at+128],0.0) for k in range(4))
             long=[pick(v,512*chip+128*b) for v in (2,0,1) for b in range(4)]
             rows=jnp.concatenate(ten+long+[jnp.zeros((1,128),f32)],axis=0).astype(bf16)
@@ -337,9 +391,9 @@
     lanes=lambda v:pl.BlockSpec((v.shape[0],256),lambda i,c:(0,i))
     more=[]
     if vecs:
-        gl,b1,b2,gd,gd0,gf=vecs
+        b1,b2,gd,gd0,gf=vecs
         half=lambda lo:pl.BlockSpec((2,256),lambda i,c:(0,jnp.clip(i-lo,0,1)))
-        more=[lanes(gl),half(0),half(2),lanes(gd),lanes(gd0),pl.BlockSpec(gf.shape,lambda i,c:(0,0))]
+        more=[half(0),half(2),lanes(gd),lanes(gd0),pl.BlockSpec(gf.shape,lambda i,c:(0,0))]
     return hbm_call(grad_qkv_kernel,
         grid_spec=pltpu.PrefetchScalarGridSpec(num_scalar_prefetch=1,grid=(4,),
             in_specs=[pl.BlockSpec((t,256),lambda i,c:(0,i)),full,full,full]+more,
@@ -424,6 +478,7 @@
         out_shape=pltpu.HBM((216,1024),bf16),name="pack_first",cost_estimate=cost(2))(shard,*vectors,w_qkv)
 
 T=1152; D=1024
+FWD_BLOCKS=[(0,384),(384,384),(768,384)]
 BLOCKS=[(0,256),(256,256),(512,256),(768,256),(1024,128)]
 
 
@@ -435,7 +490,7 @@
     for k0 in range(0,keys,128):
         t=sT[k0:k0+128]
         ok=None
-        if k0==0 or q0>=1024:
+        if k0==0 or q0+bq>1024:
             ok=kio>=start_row-k0
         if k0+127>q0:
             low=kio<=qio-k0
@@ -447,7 +502,7 @@
     lane=lax.broadcasted_iota(jnp.int32,(1,128),1)
     vT=v_ref[...].T
     oT=[]
-    for q0,bq in BLOCKS:
+    for q0,bq in FWD_BLOCKS:
         keys=q0+bq
         k=k_ref[0:keys,:]
         qb=q_ref[q0:q0+bq,:]*jnp.asarray(HD**-0.5,bf16)
@@ -601,24 +656,26 @@
     both1, do = lax.optimization_barrier((both1, do))
     halves2 = attn_bwd(proj, starts, lse, o, do, 1)
     dq2, parts1 = lax.optimization_barrier((halves2[0], parts1))
+    both2 = core_sum(*grad_qkv(core, a, dq2, *halves2[1:3], (halves1[3], halves2[3], gd, gd0, gf)))
+    parts2 = peer_parts(both2)
+    both2, dq2 = lax.optimization_barrier((both2, dq2))
     dx, gl = dx_rows([dq1, *halves1[1:3], dq2, *halves2[1:3]], x_rows, dres, vec, pack1)
-    sent_dx = send_rows(dx, recv_keys)
-    sent_dx, gl = lax.optimization_barrier((sent_dx, gl))
-    got_dx = exchange(sent_dx, devices)
-    both2 = core_sum(*grad_qkv(core, a, dq2, *halves2[1:3], (gl, halves1[3], halves2[3], gd, gd0, gf)))
-    both2, got_y = lax.optimization_barrier((both2, got_y))
+    sent_dx = send_more(dx, recv_keys, gl)
+    sent_dx, parts2, part_up = lax.optimization_barrier((sent_dx, parts2, part_up))
+    parts_up = replica_parts(part_up)
+    sent_dx, parts_up = lax.optimization_barrier((sent_dx, parts_up))
+    got_dx = lax.all_to_all(sent_dx, EVERY, split_axis=0, concat_axis=0, tiled=True)
+    parts_up, got_y, sent_dx = lax.optimization_barrier((parts_up, got_y, sent_dx))
     output = recv_rows(got_y, inverse)
-    both2, got_dx, output = lax.optimization_barrier((both2, got_dx, output))
-    parts_up = replica_parts(part_up)
-    both2, parts_up = lax.optimization_barrier((both2, parts_up))
-    parts2 = peer_parts(both2)
     spread = totals([parts_fc2, parts_up, parts1, parts2])
+    spread, got_dx, output = lax.optimization_barrier((spread, got_dx, output))
     sums = lax.all_to_all(spread, "replica", split_axis=0, concat_axis=0, tiled=True)
-    grad_tokens = recv_rows(got_dx, inverse)
+    grad_tokens, g_ln1 = recv_more(got_dx, inverse)
+    g_ln1 = jnp.where(core[0] == 0, g_ln1[0:2, 0:64], g_ln1[0:2, 64:128])
     g_qkv, g_out, g_fc1, g_fc2, ten, three = finish(core, sums)
     v = [ten[k] for k in range(10)]
     return (
-        output, grad_tokens, v[0], v[1], g_qkv, v[2], v[3], jnp.sum(ten[10]).reshape(1), g_out, v[4], v[5], v[6], v[7], v[8], g_fc1,
+        output, grad_tokens, g_ln1[0], g_ln1[1], g_qkv, v[2], v[3], jnp.sum(ten[10]).reshape(1), g_out, v[4], v[5], v[6], v[7], v[8], g_fc1,
         three[0], three[1], three[2], g_fc2, v[9],
     )
 

time: 579 us -> 561 us (0.969)
  Pallas kernels: 346 us -> 319 us
  waiting for transfers between devices: 92.6 us -> 117 us
  blocking collectives: 32.9 us -> 16.5 us
    pallas_call x22, Pallas kernels: 346 us -> 319 us  [hbm_call(): return lambda *args: call(*[pin(v) for v in args])]
    all_to_all x4 -> x3, waiting for transfers between devices: 53.8 us -> 28.9 us  [exchange(): lax.all_to_all(slab.reshape(devices, -1, 128), EVERY, split_axis=0, conca...]
    all_to_all x0 -> x1, waiting for transfers between devices: none -> 23.5 us  [on_device(): lax.all_to_all(sent_dx, EVERY, split_axis=0, concat_axis=0, tiled=True)]
    all_to_all x1, blocking collectives: 32.9 us -> 16.5 us  [replica_parts(): lax.all_to_all(part, 'replica', split_axis=0, concat_axis=0, tiled=True)]
    all_gather x1, waiting for transfers between devices: 0.01 us -> 11.8 us  [on_device(): lax.all_gather(jnp.concatenate([w_out] + [w_fc1[:, width * j:width * j +...]
    all_to_all x0 -> x1, starting transfers between devices: none -> 6.27 us  [on_device(): lax.all_to_all(sent_dx, EVERY, split_axis=0, concat_axis=0, tiled=True)]
    all_to_all x4 -> x3, starting transfers between devices: 36.1 us -> 30.2 us  [exchange(): lax.all_to_all(slab.reshape(devices, -1, 128), EVERY, split_axis=0, conca...]
    all_to_all x1 -> x2, starting transfers between devices: 11.5 us -> 15.9 us  [peer_parts(): return lax.all_to_all(both, PEERS, split_axis=0, concat_axis=0, tiled=True)]
  transfers between devices with their start and end apart: 15 -> 15, of which waited for: 7 -> 11; matrix products, arithmetic and copies ran while one was open for 3% -> 3% of each run, Pallas kernels for 59% -> 57%
where the time goes in v4:
time: 561 us; the launch traced here: 555 us
  Pallas kernels  319 us (57%)
  waiting for transfers between devices  117 us (21%)
  starting transfers between devices  63.7 us (11%)
  between operations  17.2 us (3%)
  blocking collectives  16.5 us (3%)
  other arithmetic  12.2 us (2%)
  local copies, waits for them, and re-layouts  9.5 us (2%)
    pallas_call x22, Pallas kernels, hbm_call(): return lambda *args: call(*[pin(v) for v in args])  319 us
    all_to_all x3, starting transfers between devices, exchange(): lax.all_to_all(slab.reshape(devices, -1, 128), EVERY, split_axis=0, conca...  30.2 us
    all_to_all x3, waiting for transfers between devices, exchange(): lax.all_to_all(slab.reshape(devices, -1, 128), EVERY, split_axis=0, conca...  28.9 us
    all_to_all x1, waiting for transfers between devices, on_device(): lax.all_to_all(sent_dx, EVERY, split_axis=0, concat_axis=0, tiled=True)  23.5 us
    all_to_all x1, blocking collectives, replica_parts(): lax.all_to_all(part, 'replica', split_axis=0, concat_axis=0, tiled=True)  16.5 us
    all_to_all x2, starting transfers between devices, peer_parts(): return lax.all_to_all(both, PEERS, split_axis=0, concat_axis=0, tiled=True)  15.9 us
    all_gather x1, waiting for transfers between devices, on_device(): pack1 = lax.all_gather(first, SHARD, axis=0)  14.7 us
    all_to_all x1, waiting for transfers between devices, on_device(): lax.all_to_all(spread, 'replica', split_axis=0, concat_axis=0, tiled=True)  13.5 us
  transfers between devices with their start and end apart: 15, of which 11 were waited for; matrix products, arithmetic and copies ran while one was open for 3% of the time, Pallas kernels for 57%

profile of v4, /device:TPU:0, one launch (start us, length us, event | category | flops | bytes accessed | tf_op | source)
XLA Modules:
  0.0 555.0 jit_solution(12673322968940657392)
XLA Ops:
  7.2 0.0 all-gather.7.cloned.1.call-start
  7.9 2.1 pack_first.1
  10.0 0.0 all-gather.9.cloned.1.call-start
  10.0 1.3 reshape.126.krow_ref
  11.3 1.7 reshape.144.kcol_ref
  13.1 7.4 %send_rows.3 = bf16[9216,128]{1,0:T(8,128)(2,1)} custom-call(s32[1,1152]{1,0:T(1,128)} %reshape.126.krow_ref, s32[1152,1]{1,0:T(8,128)} %reshape.144.kcol_ref, bf16[1152,1024]{1,0:T(8,128)(2,1)} %x_ref), custom_call_target="tpu_custom_call" | custom-call | bytes 15000000 | tf_op jit(solution)/shard_map/send_rows/pallas_call | solution.py:26
  20.6 0.8 copy-done.7
  21.4 0.0 all-gather.11.cloned.1.call-start
  21.5 0.7 all-gather.11.cloned.1.call-update
  22.2 11.1 %all-to-all-start = ((bf16[128,72,128]{2,1,0:T(8,128)(2,1)}), bf16[128,72,128]{2,1,0:T(8,128)(2,1)S(1)}, u32[]{:S(2)}, u32[]{:S(2)}) async-start(bf16[128,72,128]{2,1,0:T(8,128)(2,1)} %bitcast.4), calls=%async_computation | async-start | bytes 4718592 | tf_op jit(solution)/shard_map/all_to_all | solution.py:586
  33.3 7.4 %send_rows.4 = bf16[9216,128]{1,0:T(8,128)(2,1)} custom-call(s32[1,1152]{1,0:T(1,128)} %reshape.126.krow_ref, s32[1152,1]{1,0:T(8,128)} %reshape.144.kcol_ref, bf16[1152,1024]{1,0:T(8,128)(2,1)} %x_ref.1), custom_call_target="tpu_custom_call" | custom-call | bytes 15000000 | tf_op jit(solution)/shard_map/send_rows/pallas_call | solution.py:26
  40.8 28.9 %all-to-all-done = bf16[128,72,128]{2,1,0:T(8,128)(2,1)S(1)} async-done(((bf16[128,72,128]{2,1,0:T(8,128)(2,1)}), bf16[128,72,128]{2,1,0:T(8,128)(2,1)S(1)}, u32[]{:S(2)}, u32[]{:S(2)}) %all-to-all-start) | async-done | bytes 2359328 | tf_op jit(solution)/shard_map/all_to_all | solution.py:586
  69.6 14.7 %all-gather.7.cloned.1.call-done = bf16[3456,1024]{1,0:T(8,128)(2,1)} async-done(((bf16[216,1024]{1,0:T(8,128)(2,1)}), bf16[3456,1024]{1,0:T(8,128)(2,1)}) %all-gather.7.cloned.1.call-update) | async-done | bytes 7077904 | tf_op jit(solution)/shard_map/all_gather | solution.py:615
  84.4 9.4 %all-to-all-start.1 = ((bf16[128,72,128]{2,1,0:T(8,128)(2,1)}), bf16[128,72,128]{2,1,0:T(8,128)(2,1)S(1)}, u32[]{:S(2)}, u32[]{:S(2)}) async-start(bf16[128,72,128]{2,1,0:T(8,128)(2,1)} %bitcast.48), calls=%async_computation.1 | async-start | bytes 4718592 | tf_op jit(solution)/shard_map/all_to_all | solution.py:586
  93.7 0.3 reduce-scatter.3.cloned.1.call-start
  94.0 0.6 reshape.131.krow_ref
  94.6 1.0 reshape.145.kcol_ref
  95.7 0.6 fusion.4
  98.2 1.3 compare_select_fusion.2.start_ref
  99.5 1.9 convert_reduce_fusion.vec_ref.hs_ref.refs_8_
  101.4 19.6 %recv_qkv.1 = (bf16[1152,1024]{1,0:T(8,128)(2,1)}, bf16[1152,1024]{1,0:T(8,128)(2,1)}, bf16[1152,3072]{1,0:T(8,128)(2,1)}) custom-call(s32[1,1152]{1,0:T(1,128)} %reshape.131.krow_ref, s32[1152,1]{1,0:T(8,128)} %reshape.145.kcol_ref, bf16[9216,128]{1,0:T(8,128)(2,1)} %bitcast.51, f32[24,1024]{1,0:T(8,128)} %convert_reduce_fusion.vec_ref.hs_ref.refs_8_, ...), custom_call_target="tpu_custom_call" | custom-call | bytes 54000000 | tf_op jit(solution)/shard_map/recv_qkv/pallas_call | solution.py:26
  120.9 28.9 %attn_fwd.1 = (f32[1152,1024]{1,0:T(8,128)}, bf16[1152,1024]{1,0:T(8,128)(2,1)}, f32[8,2,1152]{2,1,0:T(2,128)}) custom-call(s32[1,1152]{1,0:T(1,128)} %compare_select_fusion.2.start_ref, f32[24,1024]{1,0:T(8,128)} %convert_reduce_fusion.vec_ref.hs_ref.refs_8_, bf16[1152,3072]{1,0:T(8,128)(2,1)} %get-tuple-element.101.q_ref.k_ref.v_ref, ...), custom_call_target="tpu_custom_call" | custom-call | bytes 120000000 | tf_op jit(solution)/shard_map/attn_fwd/pallas_call | solution.py:26
  149.9 1.4 copy-done.2
  151.3 8.6 %recv_rows.2.dy_ref = bf16[1152,1024]{1,0:T(8,128)(2,1)} custom-call(s32[1,1152]{1,0:T(1,128)} %reshape.131.krow_ref, s32[1152,1]{1,0:T(8,128)} %reshape.145.kcol_ref, bf16[9216,128]{1,0:T(8,128)(2,1)} %bitcast.49), custom_call_target="tpu_custom_call" | custom-call | bytes 18000000 | tf_op jit(solution)/shard_map/recv_rows/pallas_call | solution.py:26
  159.9 11.8 %all-gather.9.cloned.1.call-done = bf16[5120,1024]{1,0:T(8,128)(2,1)} async-done(((bf16[320,1024]{1,0:T(8,128)(2,1)}), bf16[5120,1024]{1,0:T(8,128)(2,1)}) %all-gather.9.cloned.1.call-update) | async-done | bytes 10485776 | tf_op jit(solution)/shard_map/all_gather | solution.py:621
  171.7 34.2 %up_rows.1 = (bf16[1152,1024]{1,0:T(8,128)(2,1)}, bf16[1152,4096]{1,0:T(8,128)(2,1)}, bf16[1152,4096]{1,0:T(8,128)(2,1)}, bf16[1152,4096]{1,0:T(8,128)(2,1)}, f3...) custom-call(bf16[1152,1024]{1,0:T(8,128)(2,1)} %get-tuple-element.106.c_ref, ...), custom_call_target="tpu_custom_call" | custom-call | bytes 135000000 | tf_op jit(solution)/shard_map/up_rows/pallas_call | solution.py:26
  205.9 15.6 %grad_fc2.1 = bf16[16,8,256,128]{3,2,1,0:T(8,128)(2,1)} custom-call(bf16[1152,4096]{1,0:T(8,128)(2,1)} %get-tuple-element.110.n_ref, bf16[1152,1024]{1,0:T(8,128)(2,1)} %recv_rows.2.dy_ref), custom_call_target="tpu_custom_call" | custom-call | bytes 42000000 | tf_op jit(solution)/shard_map/grad_fc2/pallas_call | solution.py:26
  221.5 5.1 all-gather.11.cloned.1.call-done
  226.6 36.3 %down_rows.1 = (bf16[1152,1024]{1,0:T(8,128)(2,1)}, bf16[1152,4096]{1,0:T(8,128)(2,1)}, f32[8,1024]{1,0:T(8,128)}, f32[16,1024]{1,0:T(8,128)}) custom-call(bf16[1152,4096]{1,0:T(8,128)(2,1)} %get-tuple-element.110.n_ref, bf16[1152,4096]{1,0:T(8,128)(2,1)} %get-tuple-element.111.vhat_ref, bf16[1152,4096]{1,0:T(8,128)(2,1)} %get-tuple-element.114.gp_ref, ...), custom_call_target="tpu_custom_call" | custom-call | bytes 120000000 | tf_op jit(solution)/shard_map/down_rows/pallas_call | solution.py:26
  262.9 7.5 %send_rows.5 = bf16[9216,128]{1,0:T(8,128)(2,1)} custom-call(s32[1,1152]{1,0:T(1,128)} %reshape.131.krow_ref, s32[1152,1]{1,0:T(8,128)} %reshape.145.kcol_ref, bf16[1152,1024]{1,0:T(8,128)(2,1)} %get-tuple-element.117.x_ref), custom_call_target="tpu_custom_call" | custom-call | bytes 15000000 | tf_op jit(solution)/shard_map/send_rows/pallas_call | solution.py:26
  270.4 9.7 %all-to-all-start.2 = ((bf16[128,72,128]{2,1,0:T(8,128)(2,1)}), bf16[128,72,128]{2,1,0:T(8,128)(2,1)S(1)}, u32[]{:S(2)}, u32[]{:S(2)}) async-start(bf16[128,72,128]{2,1,0:T(8,128)(2,1)} %bitcast.50), calls=%async_computation.2 | async-start | bytes 4718592 | tf_op jit(solution)/shard_map/all_to_all | solution.py:586
  280.1 0.0 reduce-scatter.5.cloned.1.call-start
  280.1 25.8 %back_rows.1 = (bf16[1152,1024]{1,0:T(8,128)(2,1)}, bf16[1152,1024]{1,0:T(8,128)(2,1)}, f32[1152,1024]{1,0:T(8,128)}, f32[8,1024]{1,0:T(8,128)}) custom-call(bf16[1152,4096]{1,0:T(8,128)(2,1)} %get-tuple-element.119.du_ref, bf16[1152,1024]{1,0:T(8,128)(2,1)} %recv_rows.2.dy_ref, f32[1152,1024]{1,0:T(8,128)} %get-tuple-element.116.hres_ref, ...), custom_call_target="tpu_custom_call" | custom-call | bytes 75000000 | tf_op jit(solution)/shard_map/back_rows/pallas_call | solution.py:26
  306.0 19.9 %grad_up.1 = bf16[16,8,320,128]{3,2,1,0:T(8,128)(2,1)} custom-call(bf16[1152,1024]{1,0:T(8,128)(2,1)} %get-tuple-element.106.c_ref, bf16[1152,1024]{1,0:T(8,128)(2,1)} %get-tuple-element.121.dz_ref, bf16[1152,1024]{1,0:T(8,128)(2,1)} %get-tuple-element.122.a2_ref, bf16[1152,4096]{1,0:T(8,128)(2,1)} %get-tuple-element.119.du_ref), custom_call_target="tpu_custom_call" | custom-call | bytes 60000000 | tf_op jit(solution)/shard_map/grad_up/pallas_call | solution.py:26
  325.9 3.2 reduce-scatter.3.cloned.1.call-done
  329.1 6.5 %all-to-all-start.3 = ((bf16[8,256,128]{2,1,0:T(8,128)(2,1)}), bf16[8,256,128]{2,1,0:T(8,128)(2,1)S(1)}, u32[]{:S(2)}, u32[]{:S(2)}) async-start(bf16[8,256,128]{2,1,0:T(8,128)(2,1)} %bitcast.54), calls=%async_computation.4 | async-start | bytes 1048576 | tf_op jit(solution)/shard_map/all_to_all | solution.py:590
  335.6 20.6 %attn_bwd.2 = (bf16[1152,512]{1,0:T(8,128)(2,1)}, bf16[1152,512]{1,0:T(8,128)(2,1)}, bf16[1152,512]{1,0:T(8,128)(2,1)}, f32[2,512]{1,0:T(2,128)}) custom-call(s32[1,1152]{1,0:T(1,128)} %compare_select_fusion.2.start_ref, f32[8,2,1152]{2,1,0:T(2,128)} %get-tuple-element.102.lse_ref, f32[1152,1024]{1,0:T(8,128)} %get-tuple-element.103.o_ref, ...), custom_call_target="tpu_custom_call" | custom-call | bytes 60000000 | tf_op jit(solution)/shard_map/attn_bwd/pallas_call | solution.py:26
  356.2 8.4 %grad_qkv.2 = (bf16[8,8,96,128]{3,2,1,0:T(8,128)(2,1)}, bf16[8,8,96,128]{3,2,1,0:T(8,128)(2,1)}) custom-call(s32[1]{0:T(128)} %bitcast.14.core_ref, bf16[1152,1024]{1,0:T(8,128)(2,1)} %get-tuple-element.134.a_ref, bf16[1152,512]{1,0:T(8,128)(2,1)} %get-tuple-element.131.dq_ref.refs_0_, bf16[1152,512]{1,0:T(8,128)(2,1)} %get-tuple-element.132.dk_ref.refs_1_, ...), custom_call_target="tpu_custom_call" | custom-call | bytes 24000000 | tf_op jit(solution)/shard_map/grad_qkv/pallas_call | solution.py:26
  364.7 3.6 collective-permute-done
  368.3 3.1 add_convert_fusion.1
  371.4 9.6 %all-to-all-start.4 = ((bf16[64,96,128]{2,1,0:T(8,128)(2,1)}), bf16[64,96,128]{2,1,0:T(8,128)(2,1)S(1)}, u32[]{:S(2)}, u32[]{:S(2)}) async-start(bf16[64,96,128]{2,1,0:T(8,128)(2,1)} %bitcast.15), calls=%async_computation.5 | async-start | bytes 3145728 | tf_op jit(solution)/shard_map/all_to_all | solution.py:600
  381.0 20.5 %attn_bwd.3 = (bf16[1152,512]{1,0:T(8,128)(2,1)}, bf16[1152,512]{1,0:T(8,128)(2,1)}, bf16[1152,512]{1,0:T(8,128)(2,1)}, f32[2,512]{1,0:T(2,128)}) custom-call(s32[1,1152]{1,0:T(1,128)} %compare_select_fusion.2.start_ref, f32[8,2,1152]{2,1,0:T(2,128)} %get-tuple-element.102.lse_ref, f32[1152,1024]{1,0:T(8,128)} %get-tuple-element.103.o_ref, ...), custom_call_target="tpu_custom_call" | custom-call | bytes 60000000 | tf_op jit(solution)/shard_map/attn_bwd/pallas_call | solution.py:26
  401.5 4.8 all-to-all-done.4.refs_2_
  406.2 9.0 %grad_qkv.3 = (bf16[8,8,104,128]{3,2,1,0:T(8,128)(2,1)}, bf16[8,8,104,128]{3,2,1,0:T(8,128)(2,1)}) custom-call(s32[1]{0:T(128)} %bitcast.14.core_ref, bf16[1152,1024]{1,0:T(8,128)(2,1)} %get-tuple-element.134.a_ref, bf16[1152,512]{1,0:T(8,128)(2,1)} %get-tuple-element.149.dq_ref.refs_3_, bf16[1152,512]{1,0:T(8,128)(2,1)} %get-tuple-element.140.dk_ref.refs_4_, ...), custom_call_target="tpu_custom_call" | custom-call | bytes 24000000 | tf_op jit(solution)/shard_map/grad_qkv/pallas_call | solution.py:26
  415.2 0.1 collective-permute-start.1
  415.3 3.8 collective-permute-done.1
  419.1 3.1 add_convert_fusion
  422.2 6.2 %all-to-all-start.5 = ((bf16[64,104,128]{2,1,0:T(8,128)(2,1)}), bf16[64,104,128]{2,1,0:T(8,128)(2,1)S(1)}, u32[]{:S(2)}, u32[]{:S(2)}) async-start(bf16[64,104,128]{2,1,0:T(8,128)(2,1)} %bitcast.16), calls=%async_computation.6 | async-start | bytes 3407872 | tf_op jit(solution)/shard_map/all_to_all | solution.py:600
  428.5 15.3 %dx_rows.1 = (bf16[1152,1024]{1,0:T(8,128)(2,1)}, f32[8,1024]{1,0:T(8,128)}) custom-call(bf16[1152,512]{1,0:T(8,128)(2,1)} %get-tuple-element.131.dq_ref.refs_0_, bf16[1152,512]{1,0:T(8,128)(2,1)} %get-tuple-element.132.dk_ref.refs_1_, bf16[1152,512]{1,0:T(8,128)(2,1)} %get-tuple-element.133.dv_ref.refs_2_, ...), custom_call_target="tpu_custom_call" | custom-call | bytes 42000000 | tf_op jit(solution)/shard_map/dx_rows/pallas_call | solution.py:26
  443.8 7.6 %send_more.1 = bf16[128,80,128]{2,1,0:T(8,128)(2,1)} custom-call(s32[1,1152]{1,0:T(1,128)} %reshape.131.krow_ref, s32[1152,1]{1,0:T(8,128)} %reshape.145.kcol_ref, bf16[1152,1024]{1,0:T(8,128)(2,1)} %get-tuple-element.151.x_ref, f32[8,1024]{1,0:T(8,128)} %get-tuple-element.152.more_ref), custom_call_target="tpu_custom_call" | custom-call | bytes 15000000 | tf_op jit(solution)/shard_map/send_more/pallas_call | solution.py:26
  451.3 3.1 all-to-all-done.5.refs_3_
  454.4 16.5 %all_to_all.45.refs_1_ = bf16[8,320,128]{2,1,0:T(8,128)(2,1)} all-to-all(bf16[8,320,128]{2,1,0:T(8,128)(2,1)} %bitcast.53), channel_id=1, replica_groups=mesh['replica'=8,'chip'=8,'core'=2] {'replica'}, dimensions={0} | all-to-all | bytes 1310720 | tf_op jit(solution)/shard_map/all_to_all | solution.py:590
  470.9 6.3 %all-to-all-start.7 = ((bf16[128,80,128]{2,1,0:T(8,128)(2,1)}), bf16[128,80,128]{2,1,0:T(8,128)(2,1)S(1)}, u32[]{:S(2)}, u32[]{:S(2)}) async-start(bf16[128,80,128]{2,1,0:T(8,128)(2,1)} %send_more.1), calls=%async_computation.9 | async-start | bytes 5242880 | tf_op jit(solution)/shard_map/all_to_all | solution.py:667
  477.2 8.6 %recv_rows.3 = bf16[1152,1024]{1,0:T(8,128)(2,1)} custom-call(s32[1,1152]{1,0:T(1,128)} %reshape.126.krow_ref, s32[1152,1]{1,0:T(8,128)} %reshape.144.kcol_ref, bf16[9216,128]{1,0:T(8,128)(2,1)} %bitcast.47), custom_call_target="tpu_custom_call" | custom-call | bytes 18000000 | tf_op jit(solution)/shard_map/recv_rows/pallas_call | solution.py:26
  485.8 4.1 totals.1
  489.9 23.5 %all-to-all-done.7.got_ref = bf16[128,80,128]{2,1,0:T(8,128)(2,1)S(1)} async-done(((bf16[128,80,128]{2,1,0:T(8,128)(2,1)}), bf16[128,80,128]{2,1,0:T(8,128)(2,1)S(1)}, u32[]{:S(2)}, u32[]{:S(2)}) %all-to-all-start.7) | async-done | bytes 2621472 | tf_op jit(solution)/shard_map/all_to_all | solution.py:667
  513.4 4.3 all-to-all-start.8
  517.8 8.7 %recv_more.1 = (bf16[1152,1024]{1,0:T(8,128)(2,1)}, f32[8,128]{1,0:T(8,128)}) custom-call(s32[1,1152]{1,0:T(1,128)} %reshape.126.krow_ref, s32[1152,1]{1,0:T(8,128)} %reshape.144.kcol_ref, bf16[128,80,128]{2,1,0:T(8,128)(2,1)} %copy-done), custom_call_target="tpu_custom_call" | custom-call | bytes 18000000 | tf_op jit(solution)/shard_map/recv_more/pallas_call | solution.py:26
  526.5 0.8 slice_select_fusion
  527.3 0.5 slice_bitcast_fusion.8
  527.8 13.5 %all-to-all-done.8.s_ref = bf16[8,776,128]{2,1,0:T(8,128)(2,1)} async-done(((bf16[8,776,128]{2,1,0:T(8,128)(2,1)}), bf16[8,776,128]{2,1,0:T(8,128)(2,1)}, u32[]{:S(2)}, u32[]{:S(2)}) %all-to-all-start.8) | async-done | bytes 1589280 | tf_op jit(solution)/shard_map/all_to_all | solution.py:672
  541.4 3.1 finish.1
  544.5 2.0 slice_bitcast_fusion
  546.5 1.4 fusion.3
  (37 shorter events, 0.2 us)
Async XLA Ops:
  7.2 77.2 %all-gather.7.cloned.1.call-start = ((), (), s32[]{:S(2)}) async-start(), calls=%async_computation.13 | async-start | bytes 7520256 | tf_op jit(solution)/shard_map/all_gather | solution.py:615
  10.0 161.8 %all-gather.9.cloned.1.call-start = ((), (), s32[]{:S(2)}) async-start(), calls=%async_computation.14 | async-start | bytes 11141120 | tf_op jit(solution)/shard_map/all_gather | solution.py:621
  13.1 7.4 %copy-start.9 = (bf16[64,1024]{1,0:T(8,128)(2,1)S(1)}, bf16[64,1024]{1,0:T(8,128)(2,1)}, u32[]{:S(2)}) copy-start(bf16[64,1024]{1,0:T(8,128)(2,1)} %param.34) | copy-start | bytes 393220
  13.1 7.4 %copy-start.8 = (bf16[64,4096]{1,0:T(8,128)(2,1)S(1)}, bf16[64,4096]{1,0:T(8,128)(2,1)}, u32[]{:S(2)}) copy-start(bf16[64,4096]{1,0:T(8,128)(2,1)} %param.40) | copy-start | bytes 1572868
  20.6 0.8 copy-start.7
  21.4 205.2 %all-gather.11.cloned.1.call-start = ((), (), s32[]{:S(2)}) async-start(), calls=%async_computation.15 | async-start | bytes 8912896 | tf_op jit(solution)/shard_map/all_gather | solution.py:622
  22.2 47.5 %all-to-all-start = ((bf16[128,72,128]{2,1,0:T(8,128)(2,1)}), bf16[128,72,128]{2,1,0:T(8,128)(2,1)S(1)}, u32[]{:S(2)}, u32[]{:S(2)}) async-start(bf16[128,72,128]{2,1,0:T(8,128)(2,1)} %bitcast.4), calls=%async_computation | async-start | bytes 4718592 | tf_op jit(solution)/shard_map/all_to_all | solution.py:586
  69.6 14.7 %copy-start.3 = (bf16[128,72,128]{2,1,0:T(8,128)(2,1)}, bf16[128,72,128]{2,1,0:T(8,128)(2,1)S(1)}, u32[]{:S(2)}) copy-start(bf16[128,72,128]{2,1,0:T(8,128)(2,1)S(1)} %all-to-all-done) | copy-start | bytes 7077892
  84.4 9.7 %copy-start.10 = (s32[1152]{0:T(1024)S(1)}, s32[1152]{0:T(1024)}, u32[]{:S(2)}) copy-start(s32[1152]{0:T(1024)} %param.26) | copy-start | bytes 13828
  84.4 11.3 %copy-start.11 = (s32[1,3]{1,0:T(1,128)S(1)}, s32[1,3]{1,0:T(1,128)}, u32[]{:S(2)}) copy-start(s32[1,3]{1,0:T(1,128)} %param.25) | copy-start | bytes 40
  84.4 65.5 %all-to-all-start.1 = ((bf16[128,72,128]{2,1,0:T(8,128)(2,1)}), bf16[128,72,128]{2,1,0:T(8,128)(2,1)S(1)}, u32[]{:S(2)}, u32[]{:S(2)}) async-start(bf16[128,72,128]{2,1,0:T(8,128)(2,1)} %bitcast.48), calls=%async_computation.1 | async-start | bytes 4718592 | tf_op jit(solution)/shard_map/all_to_all | solution.py:586
  93.7 235.3 %reduce-scatter.3.cloned.1.call-start = ((), (), s32[]{:S(2)}) async-start(), calls=%async_computation.11 | async-start | bytes 8912896 | tf_op jit(solution)/shard_map/reduce_scatter | solution.py:641
  149.9 1.4 copy-start.2
  270.4 55.5 %all-to-all-start.2 = ((bf16[128,72,128]{2,1,0:T(8,128)(2,1)}), bf16[128,72,128]{2,1,0:T(8,128)(2,1)S(1)}, u32[]{:S(2)}, u32[]{:S(2)}) async-start(bf16[128,72,128]{2,1,0:T(8,128)(2,1)} %bitcast.50), calls=%async_computation.2 | async-start | bytes 4718592 | tf_op jit(solution)/shard_map/all_to_all | solution.py:586
  280.1 174.3 %reduce-scatter.5.cloned.1.call-start = ((), (), s32[]{:S(2)}) async-start(), calls=%async_computation.12 | async-start | bytes 11141120 | tf_op jit(solution)/shard_map/reduce_scatter | solution.py:650
  325.9 3.2 copy-start.1
  329.1 27.1 %all-to-all-start.3 = ((bf16[8,256,128]{2,1,0:T(8,128)(2,1)}), bf16[8,256,128]{2,1,0:T(8,128)(2,1)S(1)}, u32[]{:S(2)}, u32[]{:S(2)}) async-start(bf16[8,256,128]{2,1,0:T(8,128)(2,1)} %bitcast.54), calls=%async_computation.4 | async-start | bytes 1048576 | tf_op jit(solution)/shard_map/all_to_all | solution.py:590
  356.2 8.5 %copy-start.6 = (bf16[8,256,128]{2,1,0:T(8,128)(2,1)}, bf16[8,256,128]{2,1,0:T(8,128)(2,1)S(1)}, u32[]{:S(2)}) copy-start(bf16[8,256,128]{2,1,0:T(8,128)(2,1)S(1)} %all-to-all-done.3.refs_0_) | copy-start | bytes 1572868
  364.7 3.6 collective-permute-start
  371.4 34.9 %all-to-all-start.4 = ((bf16[64,96,128]{2,1,0:T(8,128)(2,1)}), bf16[64,96,128]{2,1,0:T(8,128)(2,1)S(1)}, u32[]{:S(2)}, u32[]{:S(2)}) async-start(bf16[64,96,128]{2,1,0:T(8,128)(2,1)} %bitcast.15), calls=%async_computation.5 | async-start | bytes 3145728 | tf_op jit(solution)/shard_map/all_to_all | solution.py:600
  406.2 9.0 %copy-start.5 = (bf16[64,96,128]{2,1,0:T(8,128)(2,1)}, bf16[64,96,128]{2,1,0:T(8,128)(2,1)S(1)}, u32[]{:S(2)}) copy-start(bf16[64,96,128]{2,1,0:T(8,128)(2,1)S(1)} %all-to-all-done.4.refs_2_) | copy-start | bytes 4718596
  415.2 3.9 collective-permute-start.1
  422.2 32.2 %all-to-all-start.5 = ((bf16[64,104,128]{2,1,0:T(8,128)(2,1)}), bf16[64,104,128]{2,1,0:T(8,128)(2,1)S(1)}, u32[]{:S(2)}, u32[]{:S(2)}) async-start(bf16[64,104,128]{2,1,0:T(8,128)(2,1)} %bitcast.16), calls=%async_computation.6 | async-start | bytes 3407872 | tf_op jit(solution)/shard_map/all_to_all | solution.py:600
  454.4 16.5 %copy-start.4 = (bf16[64,104,128]{2,1,0:T(8,128)(2,1)}, bf16[64,104,128]{2,1,0:T(8,128)(2,1)S(1)}, u32[]{:S(2)}) copy-start(bf16[64,104,128]{2,1,0:T(8,128)(2,1)S(1)} %all-to-all-done.5.refs_3_) | copy-start | bytes 5111812
  470.9 42.5 %all-to-all-start.7 = ((bf16[128,80,128]{2,1,0:T(8,128)(2,1)}), bf16[128,80,128]{2,1,0:T(8,128)(2,1)S(1)}, u32[]{:S(2)}, u32[]{:S(2)}) async-start(bf16[128,80,128]{2,1,0:T(8,128)(2,1)} %send_more.1), calls=%async_computation.9 | async-start | bytes 5242880 | tf_op jit(solution)/shard_map/all_to_all | solution.py:667
  513.4 4.3 copy-start
  513.4 27.9 %all-to-all-start.8 = ((bf16[8,776,128]{2,1,0:T(8,128)(2,1)}), bf16[8,776,128]{2,1,0:T(8,128)(2,1)}, u32[]{:S(2)}, u32[]{:S(2)}) async-start(bf16[8,776,128]{2,1,0:T(8,128)(2,1)} %totals.1), calls=%async_computation.10 | async-start | bytes 3178496 | tf_op jit(solution)/shard_map/all_to_all | solution.py:672
Sparse Core Ops, SparseCore 0:
  10.3 73.9 all-gather.6
  86.6 85.0 all-gather.8
  173.5 53.1 all-gather.10
  228.9 100.0 reduce-scatter.2
  331.3 96.7 reduce-scatter.4

commit v5 on v4

--- a/solution.py
+++ b/solution.py
@@ -80,31 +80,6 @@
         out_shape=pltpu.HBM((t,d),bf16),
         scratch_shapes=[pltpu.VMEM((384*8,128),f32),pltpu.VMEM((t,d),bf16)],
         compiler_params=pltpu.CompilerParams(vmem_limit_bytes=40<<20),name="recv_rows",cost_estimate=cost(6))(keys.reshape(1,t),keys.reshape(t,1),got)
-
-def send_more_kernel(krow_ref,kcol_ref,x_ref,more_ref,out_ref,rank_ref,wide_ref):
-    i=pl.program_id(0); slabs=out_ref.shape[0]; bs=slabs*9
-    @pl.when(i==0)
-    def _(): rank_ref[...]=rank_row(kcol_ref[...],krow_ref[...])
-    t=rank_ref.shape[1]
-    pick=(lax.broadcasted_iota(jnp.int32,(bs,t),0)+i*bs==rank_ref[...]).astype(f32).astype(bf16)
-    rows=dot(pick,x_ref[...])
-    for k in range(8):
-        wide_ref[pl.ds(k,bs,stride=8),:]=rows[:,128*k:128*k+128]
-    out_ref[:,0:72,:]=wide_ref[...].astype(bf16).reshape(slabs,72,128)
-    more=more_ref[...].astype(bf16)
-    for d in range(slabs):
-        chip=d%16//2
-        out_ref[d,72:80,:]=more[:,128*chip:128*chip+128]
-
-def send_more(x,keys,more,blocks=4):
-    t,d=x.shape; bs=t//blocks
-    full=lambda s:pl.BlockSpec(s,lambda i:(0,0))
-    return hbm_call(send_more_kernel,grid=(blocks,),
-        in_specs=[full((1,t)),full((t,1)),full((t,d)),full((8,d))],
-        out_specs=pl.BlockSpec((bs//9,80,128),lambda i:(i,0,0)),
-        out_shape=pltpu.HBM((t//9,80,128),bf16),
-        scratch_shapes=[pltpu.VMEM((1,t),jnp.int32),pltpu.VMEM((bs*8,128),f32)],
-        compiler_params=pltpu.CompilerParams(vmem_limit_bytes=40<<20),name="send_more",cost_estimate=cost(5))(keys.reshape(1,t),keys.reshape(t,1),x,more)
 
 def recv_more_kernel(krow_ref,kcol_ref,got_ref,out_ref,more_ref,wide_ref,rows_ref):
     i=pl.program_id(0); bs=out_ref.shape[0]; t=rows_ref.shape[0]
@@ -218,48 +193,62 @@
         scratch_shapes=[pltpu.VMEM((bm,FF),f32)],
         compiler_params=pltpu.CompilerParams(vmem_limit_bytes=60<<20),name="up_rows",cost_estimate=cost(45))(c,x,vec,packa)
 
-def down_kernel(n_ref,vhat_ref,gp_ref,st_ref,dy_ref,hres_ref,vec_ref,w_ref,y_ref,du_ref,gd_ref,gf_ref,e_s):
-    @pl.when(pl.program_id(0)==0)
+def down_kernel(n_ref,vhat_ref,gp_ref,st_ref,dy_ref,hres_ref,vec_ref,w_ref,krow_ref,kcol_ref,out_ref,du_ref,gd_ref,gf_ref,e_s,y_s,rank_ref,wide_ref):
+    i=pl.program_id(0); steps=4; bs=dy_ref.shape[0]
+    @pl.when(i==0)
     def _():
         gd_ref[...]=jnp.zeros_like(gd_ref); gf_ref[...]=jnp.zeros_like(gf_ref)
-    vec=lambda k:vec_ref[k:k+1,:]
-    rf=st_ref[:,1:2]
-    dy=dy_ref[...]
-    w=lambda j:w_ref[4*j:4*j+4].reshape(1024,1024)
-    s1=0.0; s2=0.0
-    dn=dot(dy,w(0),NT)
-    for j in range(4):
-        cols=slice(1024*j,1024*j+1024)
-        ahead=dot(dy,w(j+1),NT) if j<3 else None
-        dv=dn*vhat_ref[:,cols].astype(f32)
-        gf_ref[j:j+1,:]+=colsum(dv)
-        gf_ref[4+j:5+j,:]+=colsum(dn)
-        gain=vec(15+j)
-        e=dn*gain
-        e_s[:,cols]=e
-        s1=s1+jnp.sum(e,axis=-1,keepdims=True)
-        s2=s2+jnp.sum(dv*gain,axis=-1,keepdims=True)
-        dn=ahead
-    s1=rf*s1*(1.0/FF); s2=rf*s2*(1.0/FF)
-    y=hres_ref[...]+vec(9)
-    for j in range(4):
-        cols=slice(1024*j,1024*j+1024)
-        y=y+dot(n_ref[:,cols],w(j))
-        du=gp_ref[:,cols].astype(f32)*(rf*e_s[:,cols]-s1-vhat_ref[:,cols].astype(f32)*s2)
-        du_ref[:,cols]=du.astype(bf16)
-        gf_ref[8+j:9+j,:]+=colsum(du)
-    y_ref[...]=y.astype(bf16)
-    gd_ref[0:1,:]+=colsum(dy.astype(f32))
-
-def down_rows(n,vhat,gp,st,dy,hres,vec,packb,bm=288):
-    t,d=dy.shape
-    row,full=row_specs(bm); sd=pltpu.HBM
-    return hbm_call(down_kernel,grid=(t//bm,),
-        in_specs=[row(FF),row(FF),row(FF),row(128),row(d),row(d),full(vec.shape),full(packb.shape,pipeline_mode=pl.Buffered(1))],
-        out_specs=[row(d),row(FF),full((8,d)),full((16,d))],
-        out_shape=[sd((t,d),bf16),sd((t,FF),bf16),sd((8,d),f32),sd((16,d),f32)],
-        scratch_shapes=[pltpu.VMEM((bm,FF),f32)],
-        compiler_params=pltpu.CompilerParams(vmem_limit_bytes=60<<20),name="down_rows",cost_estimate=cost(40))(n,vhat,gp,st,dy,hres,vec,packb)
+        rank_ref[...]=rank_row(kcol_ref[...],krow_ref[...])
+    @pl.when(i<steps)
+    def _():
+        vec=lambda k:vec_ref[k:k+1,:]
+        rf=st_ref[:,1:2]
+        dy=dy_ref[...]
+        w=lambda j:w_ref[4*j:4*j+4].reshape(1024,1024)
+        s1=0.0; s2=0.0
+        dn=dot(dy,w(0),NT)
+        for j in range(4):
+            cols=slice(1024*j,1024*j+1024)
+            ahead=dot(dy,w(j+1),NT) if j<3 else None
+            dv=dn*vhat_ref[:,cols].astype(f32)
+            gf_ref[j:j+1,:]+=colsum(dv)
+            gf_ref[4+j:5+j,:]+=colsum(dn)
+            gain=vec(15+j)
+            e=dn*gain
+            e_s[:,cols]=e
+            s1=s1+jnp.sum(e,axis=-1,keepdims=True)
+            s2=s2+jnp.sum(dv*gain,axis=-1,keepdims=True)
+            dn=ahead
+        s1=rf*s1*(1.0/FF); s2=rf*s2*(1.0/FF)
+        y=hres_ref[...]+vec(9)
+        for j in range(4):
+            cols=slice(1024*j,1024*j+1024)
+            y=y+dot(n_ref[:,cols],w(j))
+            du=gp_ref[:,cols].astype(f32)*(rf*e_s[:,cols]-s1-vhat_ref[:,cols].astype(f32)*s2)
+            du_ref[:,cols]=du.astype(bf16)
+            gf_ref[8+j:9+j,:]+=colsum(du)
+        y_s[pl.ds(pl.multiple_of(i*bs,bs),bs),:]=y.astype(bf16)
+        gd_ref[0:1,:]+=colsum(dy.astype(f32))
+    @pl.when(i>=steps)
+    def _():
+        n=out_ref.shape[0]//8; t=rank_ref.shape[1]
+        pick=(lax.broadcasted_iota(jnp.int32,(n,t),0)+(i-steps)*n==rank_ref[...]).astype(f32).astype(bf16)
+        rows=dot(pick,y_s[...])
+        for k in range(8):
+            wide_ref[pl.ds(k,n,stride=8),:]=rows[:,128*k:128*k+128]
+        out_ref[...]=wide_ref[...].astype(bf16)
+
+def down_rows(n,vhat,gp,st,dy,hres,vec,packb,keys):
+    t,d=dy.shape; bm=t//4
+    row=lambda n:pl.BlockSpec((bm,n),lambda i:(jnp.minimum(i,3),0))
+    full=lambda s,**k:pl.BlockSpec(s,lambda i:(0,)*len(s),**k)
+    sd=pltpu.HBM
+    return hbm_call(down_kernel,grid=(7,),
+        in_specs=[row(FF),row(FF),row(FF),row(128),row(d),row(d),full(vec.shape),full(packb.shape,pipeline_mode=pl.Buffered(1)),full((1,t)),full((t,1))],
+        out_specs=[pl.BlockSpec((t//3*8,128),lambda i:(jnp.maximum(i-4,0),0)),row(FF),full((8,d)),full((16,d))],
+        out_shape=[sd((t*8,128),bf16),sd((t,FF),bf16),sd((8,d),f32),sd((16,d),f32)],
+        scratch_shapes=[pltpu.VMEM((bm,FF),f32),pltpu.VMEM((t,d),bf16),pltpu.VMEM((1,t),jnp.int32),pltpu.VMEM((t//3*8,128),f32)],
+        compiler_params=pltpu.CompilerParams(vmem_limit_bytes=60<<20),name="down_rows",cost_estimate=cost(40))(n,vhat,gp,st,dy,hres,vec,packb,keys.reshape(1,t),keys.reshape(t,1))
 
 def back_kernel(du_ref,dy_ref,hres_ref,zhat_ref,st_ref,o_ref,vec_ref,w_ref,dz_ref,do_ref,dres_ref,gd_ref):
     @pl.when(pl.program_id(0)==0)
@@ -292,28 +281,47 @@
         out_shape=[sd((t,d),bf16),sd((t,d),bf16),sd((t,d),f32),sd((8,d),f32)],
         compiler_params=pltpu.CompilerParams(vmem_limit_bytes=60<<20),name="back_rows",cost_estimate=cost(25))(du,dy,hres,zhat,st,o,vec,packa)
 
-def dx_kernel(*refs):
-    *halves,x_ref,dres_ref,vec_ref,w_ref,dx_ref,g_ref=refs
-    @pl.when(pl.program_id(0)==0)
-    def _(): g_ref[...]=jnp.zeros_like(g_ref)
-    da=0.0
-    for j in range(3):
-        w=w_ref[:,64*j:64*j+64,:].reshape(1024,1024)
-        da=da+dot(halves[j][...],w[:,0:512],NT)+dot(halves[3+j][...],w[:,512:1024],NT)
-    xhat,r=norm_parts(x_ref[...].astype(f32))
-    g_ref[0:1,:]+=colsum(da*xhat)
-    g_ref[1:2,:]+=colsum(da)
-    dx_ref[...]=(dres_ref[...]+norm_back(da,vec_ref[0:1,:],xhat,r)).astype(bf16)
-
-def dx_rows(halves,x,dres,vec,pack1,blocks=3):
-    t,d=x.shape; bs=t//blocks
-    row=lambda n:pl.BlockSpec((bs,n),lambda i:(i,0))
+def dx_send_kernel(*refs):
+    *halves,x_ref,dres_ref,vec_ref,w_ref,krow_ref,kcol_ref,out_ref,g_s,dx_s,rank_ref,wide_ref=refs
+    i=pl.program_id(0); steps=3
+    @pl.when(i==0)
+    def _():
+        g_s[...]=jnp.zeros_like(g_s)
+        rank_ref[...]=rank_row(kcol_ref[...],krow_ref[...])
+    @pl.when(i<steps)
+    def _():
+        bs=x_ref.shape[0]
+        da=0.0
+        for j in range(3):
+            w=w_ref[:,64*j:64*j+64,:].reshape(1024,1024)
+            da=da+dot(halves[j][...],w[:,0:512],NT)+dot(halves[3+j][...],w[:,512:1024],NT)
+        xhat,r=norm_parts(x_ref[...].astype(f32))
+        g_s[0:1,:]+=colsum(da*xhat)
+        g_s[1:2,:]+=colsum(da)
+        dx_s[pl.ds(pl.multiple_of(i*bs,bs),bs),:]=(dres_ref[...]+norm_back(da,vec_ref[0:1,:],xhat,r)).astype(bf16)
+    @pl.when(i>=steps)
+    def _():
+        slabs=out_ref.shape[0]; bs=slabs*9; t=rank_ref.shape[1]
+        pick=(lax.broadcasted_iota(jnp.int32,(bs,t),0)+(i-steps)*bs==rank_ref[...]).astype(f32).astype(bf16)
+        rows=dot(pick,dx_s[...])
+        for k in range(8):
+            wide_ref[pl.ds(k,bs,stride=8),:]=rows[:,128*k:128*k+128]
+        out_ref[:,0:72,:]=wide_ref[...].astype(bf16).reshape(slabs,72,128)
+        more=g_s[...].astype(bf16)
+        for d in range(slabs):
+            chip=d%16//2
+            out_ref[d,72:80,:]=more[:,128*chip:128*chip+128]
+
+def dx_send(halves,x,dres,vec,pack1,keys):
+    t,d=x.shape; bs=t//3
+    row=lambda n:pl.BlockSpec((bs,n),lambda i:(jnp.minimum(i,2),0))
     full=lambda s,**k:pl.BlockSpec(s,lambda i:(0,)*len(s),**k)
-    return hbm_call(dx_kernel,grid=(blocks,),
-        in_specs=[row(d//2)]*6+[row(d),row(d),full(vec.shape),full((16,192,1024),pipeline_mode=pl.Buffered(1))],
-        out_specs=[row(d),full((8,d))],
-        out_shape=[pltpu.HBM((t,d),bf16),pltpu.HBM((8,d),f32)],
-        compiler_params=pltpu.CompilerParams(vmem_limit_bytes=48<<20),name="dx_rows",cost_estimate=cost(14))(*halves,x,dres,vec,pack1)
+    return hbm_call(dx_send_kernel,grid=(7,),
+        in_specs=[row(d//2)]*6+[row(d),row(d),full(vec.shape),full((16,192,1024),pipeline_mode=pl.Buffered(1)),full((1,t)),full((t,1))],
+        out_specs=pl.BlockSpec((t//36,80,128),lambda i:(jnp.maximum(i-3,0),0,0)),
+        out_shape=pltpu.HBM((t//9,80,128),bf16),
+        scratch_shapes=[pltpu.VMEM((8,d),f32),pltpu.VMEM((t,d),bf16),pltpu.VMEM((1,t),jnp.int32),pltpu.VMEM((t//4*8,128),f32)],
+        compiler_params=pltpu.CompilerParams(vmem_limit_bytes=48<<20),name="dx_send",cost_estimate=cost(18))(*halves,x,dres,vec,pack1,keys.reshape(1,t),keys.reshape(t,1))
 
 def grad_fc2_kernel(n_ref,dy_ref,out_ref):
     res=dot(n_ref[...],dy_ref[...],TN).astype(bf16)
@@ -639,31 +647,30 @@
     grads_fc2 = grad_fc2(n, dy_rows)
     grads_fc2, gp = lax.optimization_barrier((grads_fc2, gp))
     part_fc2 = lax.psum_scatter(grads_fc2, SHARD, scatter_dimension=0)
-    y, du, gd0, gf = down_rows(n, vhat, gp, stats, dy_rows, hres, vec, packb)
-    sent_y = send_rows(y, recv_keys)
+    sent_y, du, gd0, gf = down_rows(n, vhat, gp, stats, dy_rows, hres, vec, packb, recv_keys)
     sent_y, du = lax.optimization_barrier((sent_y, du))
     got_y = exchange(sent_y, devices)
     dz, do, dres, gd = back_rows(du, dy_rows, hres, zhat, stats, o, vec, packa)
     grads_up = grad_up(c, dz, a2, du)
     grads_up, do, got_y = lax.optimization_barrier((grads_up, do, got_y))
-    grads_up, part_fc2 = lax.optimization_barrier((grads_up, part_fc2))
     part_up = lax.psum_scatter(grads_up, SHARD, scatter_dimension=0)
+    halves1 = attn_bwd(proj, starts, lse, o, do, 0)
+    dq1, part_fc2 = lax.optimization_barrier((halves1[0], part_fc2))
     parts_fc2 = replica_parts(part_fc2)
-    halves1 = attn_bwd(proj, starts, lse, o, do, 0)
-    dq1, parts_fc2 = lax.optimization_barrier((halves1[0], parts_fc2))
     both1 = core_sum(*grad_qkv(core, a, dq1, *halves1[1:3]))
+    both1, do, parts_fc2 = lax.optimization_barrier((both1, do, parts_fc2))
     parts1 = peer_parts(both1)
-    both1, do = lax.optimization_barrier((both1, do))
     halves2 = attn_bwd(proj, starts, lse, o, do, 1)
     dq2, parts1 = lax.optimization_barrier((halves2[0], parts1))
-    both2 = core_sum(*grad_qkv(core, a, dq2, *halves2[1:3], (halves1[3], halves2[3], gd, gd0, gf)))
+    keep2, give2 = grad_qkv(core, a, dq2, *halves2[1:3], (halves1[3], halves2[3], gd, gd0, gf))
+    keep2, give2, part_up = lax.optimization_barrier((keep2, give2, part_up))
+    parts_up = replica_parts(part_up)
+    both2 = core_sum(keep2, give2)
+    both2, parts_up = lax.optimization_barrier((both2, parts_up))
     parts2 = peer_parts(both2)
     both2, dq2 = lax.optimization_barrier((both2, dq2))
-    dx, gl = dx_rows([dq1, *halves1[1:3], dq2, *halves2[1:3]], x_rows, dres, vec, pack1)
-    sent_dx = send_more(dx, recv_keys, gl)
-    sent_dx, parts2, part_up = lax.optimization_barrier((sent_dx, parts2, part_up))
-    parts_up = replica_parts(part_up)
-    sent_dx, parts_up = lax.optimization_barrier((sent_dx, parts_up))
+    sent_dx = dx_send([dq1, *halves1[1:3], dq2, *halves2[1:3]], x_rows, dres, vec, pack1, recv_keys)
+    sent_dx, parts2 = lax.optimization_barrier((sent_dx, parts2))
     got_dx = lax.all_to_all(sent_dx, EVERY, split_axis=0, concat_axis=0, tiled=True)
     parts_up, got_y, sent_dx = lax.optimization_barrier((parts_up, got_y, sent_dx))
     output = recv_rows(got_y, inverse)

time: 561 us -> 572 us (1.020)
  waiting for transfers between devices: 117 us -> 141 us
  blocking collectives: 16.5 us -> 0 us
    all_to_all x1 -> x2, waiting for transfers between devices: 0.01 us -> 17.6 us  [replica_parts(): lax.all_to_all(part, 'replica', split_axis=0, concat_axis=0, tiled=True)]
    all_to_all x1 -> x0, blocking collectives: 16.5 us -> none  [replica_parts(): lax.all_to_all(part, 'replica', split_axis=0, concat_axis=0, tiled=True)]
    reduce_scatter x1, waiting for transfers between devices: 0.01 us -> 15.6 us  [on_device(): part_up = lax.psum_scatter(grads_up, SHARD, scatter_dimension=0)]
    ppermute x2, waiting for transfers between devices: 7.41 us -> 0.01 us  [core_sum(): taken = lax.ppermute(give, 'core', [(0, 1), (1, 0)])]
    all_to_all x1 -> x2, starting transfers between devices: 6.53 us -> 13.5 us  [replica_parts(): lax.all_to_all(part, 'replica', split_axis=0, concat_axis=0, tiled=True)]
    pallas_call x22 -> x20, Pallas kernels: 319 us -> 316 us  [hbm_call(): return lambda *args: call(*[pin(v) for v in args])]
  transfers between devices with their start and end apart: 15 -> 16, of which waited for: 11 -> 11; matrix products, arithmetic and copies ran while one was open for 3% -> 3% of each run, Pallas kernels for 57% -> 55%
where the time goes in v5:
time: 572 us; the launch traced here: 566 us
  Pallas kernels  316 us (55%)
  waiting for transfers between devices  141 us (25%)
  starting transfers between devices  67.3 us (12%)
  between operations  17.1 us (3%)
  local copies, waits for them, and re-layouts  12.9 us (2%)
  other arithmetic  12.2 us (2%)
    pallas_call x20, Pallas kernels, hbm_call(): return lambda *args: call(*[pin(v) for v in args])  316 us
    all_to_all x3, starting transfers between devices, exchange(): lax.all_to_all(slab.reshape(devices, -1, 128), EVERY, split_axis=0, conca...  30.2 us
    all_to_all x3, waiting for transfers between devices, exchange(): lax.all_to_all(slab.reshape(devices, -1, 128), EVERY, split_axis=0, conca...  28.9 us
    all_to_all x1, waiting for transfers between devices, on_device(): lax.all_to_all(sent_dx, EVERY, split_axis=0, concat_axis=0, tiled=True)  23.5 us
    all_to_all x2, waiting for transfers between devices, replica_parts(): lax.all_to_all(part, 'replica', split_axis=0, concat_axis=0, tiled=True)  17.6 us
    reduce_scatter x1, waiting for transfers between devices, on_device(): part_up = lax.psum_scatter(grads_up, SHARD, scatter_dimension=0)  15.6 us
    all_gather x1, waiting for transfers between devices, on_device(): pack1 = lax.all_gather(first, SHARD, axis=0)  14.7 us
    all_to_all x1, waiting for transfers between devices, on_device(): lax.all_to_all(spread, 'replica', split_axis=0, concat_axis=0, tiled=True)  13.5 us
  transfers between devices with their start and end apart: 16, of which 11 were waited for; matrix products, arithmetic and copies ran while one was open for 3% of the time, Pallas kernels for 55%

profile of v5, /device:TPU:0, one launch (start us, length us, event | category | flops | bytes accessed | tf_op | source)
XLA Modules:
  0.0 566.0 jit_solution(15023590457577591336)
XLA Ops:
  7.2 0.0 all-gather.7.cloned.1.call-start
  7.9 2.1 pack_first.1
  10.0 0.0 all-gather.9.cloned.1.call-start
  10.0 1.3 reshape.129.krow_ref
  11.3 1.7 reshape.145.kcol_ref
  13.1 7.4 %send_rows.2 = bf16[9216,128]{1,0:T(8,128)(2,1)} custom-call(s32[1,1152]{1,0:T(1,128)} %reshape.129.krow_ref, s32[1152,1]{1,0:T(8,128)} %reshape.145.kcol_ref, bf16[1152,1024]{1,0:T(8,128)(2,1)} %x_ref), custom_call_target="tpu_custom_call" | custom-call | bytes 15000000 | tf_op jit(solution)/shard_map/send_rows/pallas_call | solution.py:26
  20.6 0.8 copy-done.8
  21.4 0.0 all-gather.11.cloned.1.call-start
  21.5 0.7 all-gather.11.cloned.1.call-update
  22.1 11.2 %all-to-all-start = ((bf16[128,72,128]{2,1,0:T(8,128)(2,1)}), bf16[128,72,128]{2,1,0:T(8,128)(2,1)S(1)}, u32[]{:S(2)}, u32[]{:S(2)}) async-start(bf16[128,72,128]{2,1,0:T(8,128)(2,1)} %bitcast.2), calls=%async_computation | async-start | bytes 4718592 | tf_op jit(solution)/shard_map/all_to_all | solution.py:594
  33.3 7.4 %send_rows.3 = bf16[9216,128]{1,0:T(8,128)(2,1)} custom-call(s32[1,1152]{1,0:T(1,128)} %reshape.129.krow_ref, s32[1152,1]{1,0:T(8,128)} %reshape.145.kcol_ref, bf16[1152,1024]{1,0:T(8,128)(2,1)} %x_ref.1), custom_call_target="tpu_custom_call" | custom-call | bytes 15000000 | tf_op jit(solution)/shard_map/send_rows/pallas_call | solution.py:26
  40.8 28.9 %all-to-all-done = bf16[128,72,128]{2,1,0:T(8,128)(2,1)S(1)} async-done(((bf16[128,72,128]{2,1,0:T(8,128)(2,1)}), bf16[128,72,128]{2,1,0:T(8,128)(2,1)S(1)}, u32[]{:S(2)}, u32[]{:S(2)}) %all-to-all-start) | async-done | bytes 2359328 | tf_op jit(solution)/shard_map/all_to_all | solution.py:594
  69.6 14.7 %all-gather.7.cloned.1.call-done = bf16[3456,1024]{1,0:T(8,128)(2,1)} async-done(((bf16[216,1024]{1,0:T(8,128)(2,1)}), bf16[3456,1024]{1,0:T(8,128)(2,1)}) %all-gather.7.cloned.1.call-update) | async-done | bytes 7077904 | tf_op jit(solution)/shard_map/all_gather | solution.py:623
  84.4 9.4 %all-to-all-start.1 = ((bf16[128,72,128]{2,1,0:T(8,128)(2,1)}), bf16[128,72,128]{2,1,0:T(8,128)(2,1)S(1)}, u32[]{:S(2)}, u32[]{:S(2)}) async-start(bf16[128,72,128]{2,1,0:T(8,128)(2,1)} %bitcast.48), calls=%async_computation.1 | async-start | bytes 4718592 | tf_op jit(solution)/shard_map/all_to_all | solution.py:594
  93.7 0.3 reduce-scatter.3.cloned.1.call-start
  94.0 0.6 reshape.127.krow_ref.refs_10_
  94.6 1.0 reshape.144.kcol_ref.refs_11_
  95.7 0.6 fusion.4
  98.2 1.2 compare_select_fusion.2.start_ref
  99.5 1.9 convert_reduce_fusion.vec_ref.hs_ref.refs_8_
  101.4 19.5 %recv_qkv.1 = (bf16[1152,1024]{1,0:T(8,128)(2,1)}, bf16[1152,1024]{1,0:T(8,128)(2,1)}, bf16[1152,3072]{1,0:T(8,128)(2,1)}) custom-call(s32[1,1152]{1,0:T(1,128)} %reshape.127.krow_ref.refs_10_, s32[1152,1]{1,0:T(8,128)} %reshape.144.kcol_ref.refs_11_, bf16[9216,128]{1,0:T(8,128)(2,1)} %bitcast.50, f32[24,1024]{1,0:T(8,128)} %convert_reduce_fusion.vec_ref.hs_ref.refs_8_, ...), custom_call_target="tpu_custom_call" | custom-call | bytes 54000000 | tf_op jit(solution)/shard_map/recv_qkv/pallas_call | solution.py:26
  120.9 28.9 %attn_fwd.1 = (f32[1152,1024]{1,0:T(8,128)}, bf16[1152,1024]{1,0:T(8,128)(2,1)}, f32[8,2,1152]{2,1,0:T(2,128)}) custom-call(s32[1,1152]{1,0:T(1,128)} %compare_select_fusion.2.start_ref, f32[24,1024]{1,0:T(8,128)} %convert_reduce_fusion.vec_ref.hs_ref.refs_8_, bf16[1152,3072]{1,0:T(8,128)(2,1)} %get-tuple-element.102.q_ref.k_ref.v_ref, ...), custom_call_target="tpu_custom_call" | custom-call | bytes 120000000 | tf_op jit(solution)/shard_map/attn_fwd/pallas_call | solution.py:26
  149.7 1.4 copy-done.2
  151.2 8.7 %recv_rows.2.dy_ref = bf16[1152,1024]{1,0:T(8,128)(2,1)} custom-call(s32[1,1152]{1,0:T(1,128)} %reshape.127.krow_ref.refs_10_, s32[1152,1]{1,0:T(8,128)} %reshape.144.kcol_ref.refs_11_, bf16[9216,128]{1,0:T(8,128)(2,1)} %bitcast.49), custom_call_target="tpu_custom_call" | custom-call | bytes 18000000 | tf_op jit(solution)/shard_map/recv_rows/pallas_call | solution.py:26
  159.8 11.9 %all-gather.9.cloned.1.call-done = bf16[5120,1024]{1,0:T(8,128)(2,1)} async-done(((bf16[320,1024]{1,0:T(8,128)(2,1)}), bf16[5120,1024]{1,0:T(8,128)(2,1)}) %all-gather.9.cloned.1.call-update) | async-done | bytes 10485776 | tf_op jit(solution)/shard_map/all_gather | solution.py:629
  171.7 34.2 %up_rows.1 = (bf16[1152,1024]{1,0:T(8,128)(2,1)}, bf16[1152,4096]{1,0:T(8,128)(2,1)}, bf16[1152,4096]{1,0:T(8,128)(2,1)}, bf16[1152,4096]{1,0:T(8,128)(2,1)}, f3...) custom-call(bf16[1152,1024]{1,0:T(8,128)(2,1)} %get-tuple-element.107.c_ref, ...), custom_call_target="tpu_custom_call" | custom-call | bytes 135000000 | tf_op jit(solution)/shard_map/up_rows/pallas_call | solution.py:26
  205.9 15.6 %grad_fc2.1 = bf16[16,8,256,128]{3,2,1,0:T(8,128)(2,1)} custom-call(bf16[1152,4096]{1,0:T(8,128)(2,1)} %get-tuple-element.111.n_ref, bf16[1152,1024]{1,0:T(8,128)(2,1)} %recv_rows.2.dy_ref), custom_call_target="tpu_custom_call" | custom-call | bytes 42000000 | tf_op jit(solution)/shard_map/grad_fc2/pallas_call | solution.py:26
  221.5 5.1 all-gather.11.cloned.1.call-done
  226.6 43.0 %down_rows.1 = (bf16[9216,128]{1,0:T(8,128)(2,1)}, bf16[1152,4096]{1,0:T(8,128)(2,1)}, f32[8,1024]{1,0:T(8,128)}, f32[16,1024]{1,0:T(8,128)}) custom-call(bf16[1152,4096]{1,0:T(8,128)(2,1)} %get-tuple-element.111.n_ref, bf16[1152,4096]{1,0:T(8,128)(2,1)} %get-tuple-element.112.vhat_ref, bf16[1152,4096]{1,0:T(8,128)(2,1)} %get-tuple-element.115.gp_ref, ...), custom_call_target="tpu_custom_call" | custom-call | bytes 120000000 | tf_op jit(solution)/shard_map/down_rows/pallas_call | solution.py:26
  269.7 9.7 %all-to-all-start.2 = ((bf16[128,72,128]{2,1,0:T(8,128)(2,1)}), bf16[128,72,128]{2,1,0:T(8,128)(2,1)S(1)}, u32[]{:S(2)}, u32[]{:S(2)}) async-start(bf16[128,72,128]{2,1,0:T(8,128)(2,1)} %bitcast.52), calls=%async_computation.2 | async-start | bytes 4718592 | tf_op jit(solution)/shard_map/all_to_all | solution.py:594
  279.3 0.0 reduce-scatter.5.cloned.1.call-start
  279.4 25.8 %back_rows.1 = (bf16[1152,1024]{1,0:T(8,128)(2,1)}, bf16[1152,1024]{1,0:T(8,128)(2,1)}, f32[1152,1024]{1,0:T(8,128)}, f32[8,1024]{1,0:T(8,128)}) custom-call(bf16[1152,4096]{1,0:T(8,128)(2,1)} %get-tuple-element.120.du_ref, bf16[1152,1024]{1,0:T(8,128)(2,1)} %recv_rows.2.dy_ref, f32[1152,1024]{1,0:T(8,128)} %get-tuple-element.117.hres_ref, ...), custom_call_target="tpu_custom_call" | custom-call | bytes 75000000 | tf_op jit(solution)/shard_map/back_rows/pallas_call | solution.py:26
  305.2 19.9 %grad_up.1 = bf16[16,8,320,128]{3,2,1,0:T(8,128)(2,1)} custom-call(bf16[1152,1024]{1,0:T(8,128)(2,1)} %get-tuple-element.107.c_ref, bf16[1152,1024]{1,0:T(8,128)(2,1)} %get-tuple-element.122.dz_ref, bf16[1152,1024]{1,0:T(8,128)(2,1)} %get-tuple-element.123.a2_ref, bf16[1152,4096]{1,0:T(8,128)(2,1)} %get-tuple-element.120.du_ref), custom_call_target="tpu_custom_call" | custom-call | bytes 60000000 | tf_op jit(solution)/shard_map/grad_up/pallas_call | solution.py:26
  325.1 1.4 copy-done.1
  326.5 20.5 %attn_bwd.2 = (bf16[1152,512]{1,0:T(8,128)(2,1)}, bf16[1152,512]{1,0:T(8,128)(2,1)}, bf16[1152,512]{1,0:T(8,128)(2,1)}, f32[2,512]{1,0:T(2,128)}) custom-call(s32[1,1152]{1,0:T(1,128)} %compare_select_fusion.2.start_ref, f32[8,2,1152]{2,1,0:T(2,128)} %get-tuple-element.103.lse_ref, f32[1152,1024]{1,0:T(8,128)} %get-tuple-element.104.o_ref, ...), custom_call_target="tpu_custom_call" | custom-call | bytes 60000000 | tf_op jit(solution)/shard_map/attn_bwd/pallas_call | solution.py:26
  347.0 8.5 %grad_qkv.2 = (bf16[8,8,96,128]{3,2,1,0:T(8,128)(2,1)}, bf16[8,8,96,128]{3,2,1,0:T(8,128)(2,1)}) custom-call(s32[1]{0:T(128)} %bitcast.core_ref, bf16[1152,1024]{1,0:T(8,128)(2,1)} %get-tuple-element.101.a_ref, bf16[1152,512]{1,0:T(8,128)(2,1)} %get-tuple-element.129.dq_ref.refs_0_, bf16[1152,512]{1,0:T(8,128)(2,1)} %get-tuple-element.130.dk_ref.refs_1_, ...), custom_call_target="tpu_custom_call" | custom-call | bytes 24000000 | tf_op jit(solution)/shard_map/grad_qkv/pallas_call | solution.py:26
  355.5 6.5 %all-to-all-start.3 = ((bf16[8,256,128]{2,1,0:T(8,128)(2,1)}), bf16[8,256,128]{2,1,0:T(8,128)(2,1)S(1)}, u32[]{:S(2)}, u32[]{:S(2)}) async-start(bf16[8,256,128]{2,1,0:T(8,128)(2,1)} %bitcast.14), calls=%async_computation.4 | async-start | bytes 1048576 | tf_op jit(solution)/shard_map/all_to_all | solution.py:598
  362.0 3.0 add_convert_fusion.1
  365.0 8.3 %all-to-all-done.3.refs_0_ = bf16[8,256,128]{2,1,0:T(8,128)(2,1)S(1)} async-done(((bf16[8,256,128]{2,1,0:T(8,128)(2,1)}), bf16[8,256,128]{2,1,0:T(8,128)(2,1)S(1)}, u32[]{:S(2)}, u32[]{:S(2)}) %all-to-all-start.3) | async-done | bytes 524320 | tf_op jit(solution)/shard_map/all_to_all | solution.py:598
  373.3 0.8 copy-done.7
  374.1 7.5 %all-to-all-start.4 = ((bf16[64,96,128]{2,1,0:T(8,128)(2,1)}), bf16[64,96,128]{2,1,0:T(8,128)(2,1)S(1)}, u32[]{:S(2)}, u32[]{:S(2)}) async-start(bf16[64,96,128]{2,1,0:T(8,128)(2,1)} %bitcast.15), calls=%async_computation.5 | async-start | bytes 3145728 | tf_op jit(solution)/shard_map/all_to_all | solution.py:608
  381.6 20.5 %attn_bwd.3 = (bf16[1152,512]{1,0:T(8,128)(2,1)}, bf16[1152,512]{1,0:T(8,128)(2,1)}, bf16[1152,512]{1,0:T(8,128)(2,1)}, f32[2,512]{1,0:T(2,128)}) custom-call(s32[1,1152]{1,0:T(1,128)} %compare_select_fusion.2.start_ref, f32[8,2,1152]{2,1,0:T(2,128)} %get-tuple-element.103.lse_ref, f32[1152,1024]{1,0:T(8,128)} %get-tuple-element.104.o_ref, ...), custom_call_target="tpu_custom_call" | custom-call | bytes 60000000 | tf_op jit(solution)/shard_map/attn_bwd/pallas_call | solution.py:26
  402.1 4.3 all-to-all-done.4.refs_2_
  406.4 9.0 %grad_qkv.3 = (bf16[8,8,104,128]{3,2,1,0:T(8,128)(2,1)}, bf16[8,8,104,128]{3,2,1,0:T(8,128)(2,1)}) custom-call(s32[1]{0:T(128)} %bitcast.core_ref, bf16[1152,1024]{1,0:T(8,128)(2,1)} %get-tuple-element.101.a_ref, bf16[1152,512]{1,0:T(8,128)(2,1)} %get-tuple-element.156.dq_ref.refs_3_, bf16[1152,512]{1,0:T(8,128)(2,1)} %get-tuple-element.140.dk_ref.refs_4_, ...), custom_call_target="tpu_custom_call" | custom-call | bytes 24000000 | tf_op jit(solution)/shard_map/grad_qkv/pallas_call | solution.py:26
  415.4 15.6 %reduce-scatter.5.cloned.1.call-done = bf16[1,8,320,128]{3,2,1,0:T(8,128)(2,1)} async-done(((bf16[16,8,320,128]{3,2,1,0:T(8,128)(2,1)}), bf16[1,8,320,128]{3,2,1,0:T(8,128)(2,1)}) %reduce-scatter.5.cloned.1.call-update) | async-done | bytes 655376 | tf_op jit(solution)/shard_map/reduce_scatter | solution.py:656
  431.0 7.0 %all-to-all-start.5 = ((bf16[8,320,128]{2,1,0:T(8,128)(2,1)}), bf16[8,320,128]{2,1,0:T(8,128)(2,1)S(1)}, u32[]{:S(2)}, u32[]{:S(2)}) async-start(bf16[8,320,128]{2,1,0:T(8,128)(2,1)} %bitcast.53), calls=%async_computation.7 | async-start | bytes 1310720 | tf_op jit(solution)/shard_map/all_to_all | solution.py:598
  438.1 3.1 add_convert_fusion
  441.2 9.4 %all-to-all-done.5.refs_1_ = bf16[8,320,128]{2,1,0:T(8,128)(2,1)S(1)} async-done(((bf16[8,320,128]{2,1,0:T(8,128)(2,1)}), bf16[8,320,128]{2,1,0:T(8,128)(2,1)S(1)}, u32[]{:S(2)}, u32[]{:S(2)}) %all-to-all-start.5) | async-done | bytes 655392 | tf_op jit(solution)/shard_map/all_to_all | solution.py:598
  450.6 5.9 %all-to-all-start.6 = ((bf16[64,104,128]{2,1,0:T(8,128)(2,1)}), bf16[64,104,128]{2,1,0:T(8,128)(2,1)S(1)}, u32[]{:S(2)}, u32[]{:S(2)}) async-start(bf16[64,104,128]{2,1,0:T(8,128)(2,1)} %bitcast.17), calls=%async_computation.8 | async-start | bytes 3407872 | tf_op jit(solution)/shard_map/all_to_all | solution.py:608
  456.5 20.5 %dx_send.1 = bf16[128,80,128]{2,1,0:T(8,128)(2,1)} custom-call(bf16[1152,512]{1,0:T(8,128)(2,1)} %get-tuple-element.129.dq_ref.refs_0_, bf16[1152,512]{1,0:T(8,128)(2,1)} %get-tuple-element.130.dk_ref.refs_1_, bf16[1152,512]{1,0:T(8,128)(2,1)} %get-tuple-element.131.dv_ref.refs_2_, bf16[1152,512]{1,0:T(8,128)(2,1)} %get-tuple-element.156.dq_ref.refs_3_, ...), custom_call_target="tpu_custom_call" | custom-call | bytes 54000000 | tf_op jit(solution)/shard_map/dx_send/pallas_call | solution.py:26
  477.0 4.6 all-to-all-done.6.refs_3_
  481.7 1.2 copy-done.4
  482.9 5.5 all-to-all-start.7
  488.4 8.6 %recv_rows.3 = bf16[1152,1024]{1,0:T(8,128)(2,1)} custom-call(s32[1,1152]{1,0:T(1,128)} %reshape.129.krow_ref, s32[1152,1]{1,0:T(8,128)} %reshape.145.kcol_ref, bf16[9216,128]{1,0:T(8,128)(2,1)} %bitcast.47), custom_call_target="tpu_custom_call" | custom-call | bytes 18000000 | tf_op jit(solution)/shard_map/recv_rows/pallas_call | solution.py:26
  497.0 4.1 totals.1
  501.0 23.5 %all-to-all-done.7.got_ref = bf16[128,80,128]{2,1,0:T(8,128)(2,1)S(1)} async-done(((bf16[128,80,128]{2,1,0:T(8,128)(2,1)}), bf16[128,80,128]{2,1,0:T(8,128)(2,1)S(1)}, u32[]{:S(2)}, u32[]{:S(2)}) %all-to-all-start.7) | async-done | bytes 2621472 | tf_op jit(solution)/shard_map/all_to_all | solution.py:674
  524.6 4.3 all-to-all-start.8
  528.9 8.7 %recv_more.1 = (bf16[1152,1024]{1,0:T(8,128)(2,1)}, f32[8,128]{1,0:T(8,128)}) custom-call(s32[1,1152]{1,0:T(1,128)} %reshape.129.krow_ref, s32[1152,1]{1,0:T(8,128)} %reshape.145.kcol_ref, bf16[128,80,128]{2,1,0:T(8,128)(2,1)} %copy-done), custom_call_target="tpu_custom_call" | custom-call | bytes 18000000 | tf_op jit(solution)/shard_map/recv_more/pallas_call | solution.py:26
  537.6 0.8 slice_select_fusion
  538.5 0.5 slice_bitcast_fusion.8
  539.0 13.5 %all-to-all-done.8.s_ref = bf16[8,776,128]{2,1,0:T(8,128)(2,1)} async-done(((bf16[8,776,128]{2,1,0:T(8,128)(2,1)}), bf16[8,776,128]{2,1,0:T(8,128)(2,1)}, u32[]{:S(2)}, u32[]{:S(2)}) %all-to-all-start.8) | async-done | bytes 1589280 | tf_op jit(solution)/shard_map/all_to_all | solution.py:679
  552.5 3.1 finish.1
  555.7 2.0 slice_bitcast_fusion
  557.7 1.4 fusion.3
  (38 shorter events, 0.2 us)
Async XLA Ops:
  7.2 77.2 %all-gather.7.cloned.1.call-start = ((), (), s32[]{:S(2)}) async-start(), calls=%async_computation.13 | async-start | bytes 7520256 | tf_op jit(solution)/shard_map/all_gather | solution.py:623
  10.0 161.8 %all-gather.9.cloned.1.call-start = ((), (), s32[]{:S(2)}) async-start(), calls=%async_computation.14 | async-start | bytes 11141120 | tf_op jit(solution)/shard_map/all_gather | solution.py:629
  13.1 7.4 %copy-start.10 = (bf16[64,1024]{1,0:T(8,128)(2,1)S(1)}, bf16[64,1024]{1,0:T(8,128)(2,1)}, u32[]{:S(2)}) copy-start(bf16[64,1024]{1,0:T(8,128)(2,1)} %param.34) | copy-start | bytes 393220
  13.1 7.4 %copy-start.9 = (bf16[64,4096]{1,0:T(8,128)(2,1)S(1)}, bf16[64,4096]{1,0:T(8,128)(2,1)}, u32[]{:S(2)}) copy-start(bf16[64,4096]{1,0:T(8,128)(2,1)} %param.40) | copy-start | bytes 1572868
  20.5 0.8 copy-start.8
  21.4 205.2 %all-gather.11.cloned.1.call-start = ((), (), s32[]{:S(2)}) async-start(), calls=%async_computation.15 | async-start | bytes 8912896 | tf_op jit(solution)/shard_map/all_gather | solution.py:630
  22.1 47.5 %all-to-all-start = ((bf16[128,72,128]{2,1,0:T(8,128)(2,1)}), bf16[128,72,128]{2,1,0:T(8,128)(2,1)S(1)}, u32[]{:S(2)}, u32[]{:S(2)}) async-start(bf16[128,72,128]{2,1,0:T(8,128)(2,1)} %bitcast.2), calls=%async_computation | async-start | bytes 4718592 | tf_op jit(solution)/shard_map/all_to_all | solution.py:594
  69.6 14.7 %copy-start.3 = (bf16[128,72,128]{2,1,0:T(8,128)(2,1)}, bf16[128,72,128]{2,1,0:T(8,128)(2,1)S(1)}, u32[]{:S(2)}) copy-start(bf16[128,72,128]{2,1,0:T(8,128)(2,1)S(1)} %all-to-all-done) | copy-start | bytes 7077892
  84.3 9.7 %copy-start.11 = (s32[1152]{0:T(1024)S(1)}, s32[1152]{0:T(1024)}, u32[]{:S(2)}) copy-start(s32[1152]{0:T(1024)} %param.26) | copy-start | bytes 13828
  84.3 11.3 %copy-start.12 = (s32[1,3]{1,0:T(1,128)S(1)}, s32[1,3]{1,0:T(1,128)}, u32[]{:S(2)}) copy-start(s32[1,3]{1,0:T(1,128)} %param.25) | copy-start | bytes 40
  84.4 65.4 %all-to-all-start.1 = ((bf16[128,72,128]{2,1,0:T(8,128)(2,1)}), bf16[128,72,128]{2,1,0:T(8,128)(2,1)S(1)}, u32[]{:S(2)}, u32[]{:S(2)}) async-start(bf16[128,72,128]{2,1,0:T(8,128)(2,1)} %bitcast.48), calls=%async_computation.1 | async-start | bytes 4718592 | tf_op jit(solution)/shard_map/all_to_all | solution.py:594
  93.7 253.2 %reduce-scatter.3.cloned.1.call-start = ((), (), s32[]{:S(2)}) async-start(), calls=%async_computation.11 | async-start | bytes 8912896 | tf_op jit(solution)/shard_map/reduce_scatter | solution.py:649
  149.7 1.4 copy-start.2
  269.7 55.4 %all-to-all-start.2 = ((bf16[128,72,128]{2,1,0:T(8,128)(2,1)}), bf16[128,72,128]{2,1,0:T(8,128)(2,1)S(1)}, u32[]{:S(2)}, u32[]{:S(2)}) async-start(bf16[128,72,128]{2,1,0:T(8,128)(2,1)} %bitcast.52), calls=%async_computation.2 | async-start | bytes 4718592 | tf_op jit(solution)/shard_map/all_to_all | solution.py:594
  279.3 151.7 %reduce-scatter.5.cloned.1.call-start = ((), (), s32[]{:S(2)}) async-start(), calls=%async_computation.12 | async-start | bytes 11141120 | tf_op jit(solution)/shard_map/reduce_scatter | solution.py:656
  325.1 1.4 copy-start.1
  355.5 6.5 %collective-permute-start = (bf16[8,8,96,128]{3,2,1,0:T(8,128)(2,1)}, bf16[8,8,96,128]{3,2,1,0:T(8,128)(2,1)S(1)}, u32[]{:S(2)}, u32[]{:S(2)}) collective-permute-start(bf16[8,8,96,128]{3,2,1,0:T(8,128)(2,1)} %get-tuple-element.133), channel_id=1, source_target_pairs={{0,1},{1,0},{2,3},{3,2},{4,5},{5,4},{6,7},{7,6},{8,9},{9,8},{10,11... | collective-permute-start | bytes 4718600 | tf_op jit(solution)/shard_map/ppermute | solution.py:602
  355.5 17.8 %all-to-all-start.3 = ((bf16[8,256,128]{2,1,0:T(8,128)(2,1)}), bf16[8,256,128]{2,1,0:T(8,128)(2,1)S(1)}, u32[]{:S(2)}, u32[]{:S(2)}) async-start(bf16[8,256,128]{2,1,0:T(8,128)(2,1)} %bitcast.14), calls=%async_computation.4 | async-start | bytes 1048576 | tf_op jit(solution)/shard_map/all_to_all | solution.py:598
  373.3 0.8 copy-start.7
  374.1 32.3 %all-to-all-start.4 = ((bf16[64,96,128]{2,1,0:T(8,128)(2,1)}), bf16[64,96,128]{2,1,0:T(8,128)(2,1)S(1)}, u32[]{:S(2)}, u32[]{:S(2)}) async-start(bf16[64,96,128]{2,1,0:T(8,128)(2,1)} %bitcast.15), calls=%async_computation.5 | async-start | bytes 3145728 | tf_op jit(solution)/shard_map/all_to_all | solution.py:608
  406.4 9.0 %copy-start.5 = (bf16[64,96,128]{2,1,0:T(8,128)(2,1)}, bf16[64,96,128]{2,1,0:T(8,128)(2,1)S(1)}, u32[]{:S(2)}) copy-start(bf16[64,96,128]{2,1,0:T(8,128)(2,1)S(1)} %all-to-all-done.4.refs_2_) | copy-start | bytes 4718596
  431.0 7.0 %collective-permute-start.1 = (bf16[8,8,104,128]{3,2,1,0:T(8,128)(2,1)}, bf16[8,8,104,128]{3,2,1,0:T(8,128)(2,1)S(1)}, u32[]{:S(2)}, u32[]{:S(2)}) collective-permute-start(bf16[8,8,104,128]{3,2,1,0:T(8,128)(2,1)} %get-tuple-element.151), channel_id=1, source_target_pairs={{0,1},{1,0},{2,3},{3,2},{4,5},{5,4},{6,7},{7,6},{8,9},{9,8},{10,11... | collective-permute-start | bytes 5111816 | tf_op jit(solution)/shard_map/ppermute | solution.py:602
  431.0 19.5 %all-to-all-start.5 = ((bf16[8,320,128]{2,1,0:T(8,128)(2,1)}), bf16[8,320,128]{2,1,0:T(8,128)(2,1)S(1)}, u32[]{:S(2)}, u32[]{:S(2)}) async-start(bf16[8,320,128]{2,1,0:T(8,128)(2,1)} %bitcast.53), calls=%async_computation.7 | async-start | bytes 1310720 | tf_op jit(solution)/shard_map/all_to_all | solution.py:598
  450.6 26.4 %copy-start.6 = (bf16[8,320,128]{2,1,0:T(8,128)(2,1)}, bf16[8,320,128]{2,1,0:T(8,128)(2,1)S(1)}, u32[]{:S(2)}) copy-start(bf16[8,320,128]{2,1,0:T(8,128)(2,1)S(1)} %all-to-all-done.5.refs_1_) | copy-start | bytes 1966084
  450.6 31.1 %all-to-all-start.6 = ((bf16[64,104,128]{2,1,0:T(8,128)(2,1)}), bf16[64,104,128]{2,1,0:T(8,128)(2,1)S(1)}, u32[]{:S(2)}, u32[]{:S(2)}) async-start(bf16[64,104,128]{2,1,0:T(8,128)(2,1)} %bitcast.17), calls=%async_computation.8 | async-start | bytes 3407872 | tf_op jit(solution)/shard_map/all_to_all | solution.py:608
  481.7 1.2 copy-start.4
  482.9 41.7 %all-to-all-start.7 = ((bf16[128,80,128]{2,1,0:T(8,128)(2,1)}), bf16[128,80,128]{2,1,0:T(8,128)(2,1)S(1)}, u32[]{:S(2)}, u32[]{:S(2)}) async-start(bf16[128,80,128]{2,1,0:T(8,128)(2,1)} %dx_send.1), calls=%async_computation.9 | async-start | bytes 5242880 | tf_op jit(solution)/shard_map/all_to_all | solution.py:674
  524.6 4.3 copy-start
  524.6 27.9 %all-to-all-start.8 = ((bf16[8,776,128]{2,1,0:T(8,128)(2,1)}), bf16[8,776,128]{2,1,0:T(8,128)(2,1)}, u32[]{:S(2)}, u32[]{:S(2)}) async-start(bf16[8,776,128]{2,1,0:T(8,128)(2,1)} %totals.1), calls=%async_computation.10 | async-start | bytes 3178496 | tf_op jit(solution)/shard_map/all_to_all | solution.py:679
Sparse Core Ops, SparseCore 0:
  10.3 73.9 all-gather.6
  86.6 85.0 all-gather.8
  173.5 53.1 all-gather.10
  228.9 100.5 reduce-scatter.2
  331.7 99.2 reduce-scatter.4
